TPU v7x, 32 devices: a whole 2x2x4 slice. The times are simulated.
32 devices in a mesh: dp: 4 (over y, x), graph: 8 (over z, core).
Axes of the slice: x: 2, y: 2, z: 4, core: 2. Of those that a mesh axis runs over, the one named last changes fastest.
Arguments:
- messages: bfloat16 [4, 8192, 512], P('dp', 'graph'), may hold values from -6 to 6
- cotangent: bfloat16 [4, 8192, 512], P('dp', 'graph'), may hold values from -6 to 6
- triplet_basis: bfloat16 [4, 8192, 3584], P('dp', 'graph'), may hold values from -6 to 6
- w_edge: bfloat16 [512, 512], replicated, may hold values from -0.25 to 0.25
- w_down: bfloat16 [512, 64], replicated, may hold values from -0.25 to 0.25
- w_bil: bfloat16 [112, 4096], replicated, may hold values from -0.01171875 to 0.01171875
- w_up: bfloat16 [2, 64, 512], replicated, may hold values from -0.75 to 0.75
- trip_src: int32 [4, 8192, 32], P('dp', 'graph'), may hold values from -1 to 2047, as said below
- send_rows: int32 [4, 32, 256], P('dp', 'graph'), may hold values from 0 to 1023, as said below
- send_count: int32 [4, 32], P('dp', 'graph'), may hold values from 1 to 256, as said below
- rev_src: int32 [4, 8192], P('dp', 'graph'), may hold values from -1 to 2047, as said below
- edge_count: int32 [4, 8], P('dp', 'graph'), may hold values from 614 to 1024, as said below
Outputs:
- grad_messages: bfloat16 [4, 8192, 512], P('dp', 'graph')
- grad_w_edge: float32 [512, 512], P('graph')
- grad_w_down: float32 [512, 64], P('graph')
- grad_w_bil: float32 [112, 4096], P(None, 'graph')
- grad_w_up: float32 [2, 64, 512], P(None, None, 'graph')
Inputs may be any that keep to these rules, and one draw needn't show every extreme that they name: `trip_src`: an entry below 1024 is a live edge of the same device; an entry 1024 + o * 256 + c names row c, below its count, of send list o of the device off(o) positions lower along graph (cyclically). Slots k at or beyond an edge's triplet count, and all slots of empty edges, are -1. `send_rows`: send list o of a device goes to the device off(o) positions higher along graph, cyclically. Its entries are distinct live rows; entries at or beyond the list's count are padding. `send_count`: in each slab some list holds exactly 256 rows. `rev_src`: every live edge has one reverse edge, on its own device or within 2 devices; if edge e reads row r as its reverse, the edge behind r reads e back. Empty slots hold -1. `edge_count`: in each slab some device is full.
All inputs are finite; a program needn't handle non-finite values.
Results may differ from a plain program's by a relative error of at most 0.023.
Values may be sent and summed in bfloat16 or wider, within the bound.
No kernel may reach another device: no remote copies, remote signals or barrier semaphores. Data moves between devices by JAX's collectives and lax.ppermute only.
A program may use at most 192 MiB of HBM per device.

v0:
```python
import math

import jax
import jax.numpy as jnp
from jax import lax
from jax.sharding import PartitionSpec as P

inv_root = 0.7071067811865476


def shifted(block, axis, distance):
    devices = range(lax.axis_size(axis))
    route = [((i - distance) % len(devices), i) for i in devices]
    return lax.ppermute(block, axis, route)


def silu_slope(values):
    sigma = jax.nn.sigmoid(values)
    return sigma * (1.0 + values * (1.0 - sigma))


def offsets(count):
    return [(which // 2 + 1) * (1 - 2 * (which % 2)) for which in range(count)]


def contract(left, right):
    return lax.dot_general(
        left, right, (((0,), (0,)), ((), ())), preferred_element_type=jnp.float32
    )


def packed(members, list_count):
    return jnp.concatenate([member.reshape(list_count, -1, 128) for member in members], axis=1)


def unpacked(bundle, widths, list_count, slot_count):
    pieces = []
    offset_row = 0
    for columns in widths:
        extent = slot_count * columns // 128
        pieces.append(
            bundle[:, offset_row : offset_row + extent].reshape(list_count, slot_count, columns)
        )
        offset_row = offset_row + extent
    return pieces


def deliver(payload, direction):
    list_count = payload.shape[0]
    shifts = offsets(list_count)
    arrived = []
    for which in range(list_count):
        arrived.append(shifted(payload[which], "graph", direction * shifts[which]))
    return jnp.stack(arrived)


def body(
    messages,
    cotangent,
    triplet_basis,
    w_edge,
    w_down,
    w_bil,
    w_up,
    trip_src,
    send_rows,
    send_count,
    rev_src,
    edge_count,
):
    edges = messages.shape[1]
    model = messages.shape[2]
    narrow = w_down.shape[1]
    slots = trip_src.shape[2]
    capacity = send_rows.shape[2]
    list_count = send_rows.shape[1]
    basis_count = w_bil.shape[0]
    pool_size = edges + list_count * capacity
    source = messages[0]
    own_cot = cotangent[0]
    alive = jnp.arange(edges) < edge_count[0, 0]
    pre_edge = jnp.dot(source, w_edge, preferred_element_type=jnp.float32)
    hidden = jax.nn.silu(pre_edge).astype(jnp.bfloat16)
    pre_down = jnp.dot(hidden, w_down, preferred_element_type=jnp.float32)
    reduced = jax.nn.silu(pre_down).astype(jnp.bfloat16)
    list_rows = send_rows[0]
    filled = jnp.arange(capacity)[None, :] < send_count[0][:, None]

    def outgoing(values):
        picked = values[list_rows]
        return jnp.where(filled[:, :, None], picked, jnp.zeros((), values.dtype))

    scaled = jnp.where(alive[:, None], own_cot.astype(jnp.float32) * inv_root, 0.0)
    arrived = deliver(packed([outgoing(reduced), outgoing(own_cot)], list_count), 1)
    recv_red, recv_cot = unpacked(arrived, [narrow, model], list_count, capacity)
    pool_cot = jnp.concatenate([own_cot, recv_cot.reshape(-1, model)], axis=0)
    pool_red = jnp.concatenate([reduced, recv_red.reshape(-1, narrow)], axis=0)
    trips = trip_src[0]
    valid = trips >= 0
    trip_index = jnp.maximum(trips, 0)
    gathered = jnp.where(valid[:, :, None], pool_red[trip_index], jnp.zeros((), jnp.bfloat16))
    basis = triplet_basis[0].reshape(edges, slots, basis_count)
    outer = jnp.einsum("ekb,ekc->ebc", basis, gathered, preferred_element_type=jnp.float32)
    outer = outer.astype(jnp.bfloat16).reshape(edges, basis_count * narrow)
    w_flat = w_bil.reshape(basis_count * narrow, narrow)
    state = jnp.dot(outer, w_flat, preferred_element_type=jnp.float32).astype(jnp.bfloat16)
    pre_ca = jnp.dot(state, w_up[0], preferred_element_type=jnp.float32)
    grad_ca = (scaled * silu_slope(pre_ca)).astype(jnp.bfloat16)
    up_ca = contract(state, grad_ca)
    grad_own = jnp.dot(grad_ca, w_up[0].T, preferred_element_type=jnp.float32)
    reverse = rev_src[0]
    has_rev = reverse >= 0
    rev_index = jnp.maximum(reverse, 0)
    mirror = jnp.where(has_rev[:, None], pool_cot[rev_index], jnp.zeros((), jnp.bfloat16))
    pre_ac = jnp.dot(state, w_up[1], preferred_element_type=jnp.float32)
    grad_ac = (mirror.astype(jnp.float32) * inv_root * silu_slope(pre_ac)).astype(jnp.bfloat16)
    up_ac = contract(state, grad_ac)
    back_rev = jnp.dot(grad_ac, w_up[1].T, preferred_element_type=jnp.float32).astype(jnp.bfloat16)
    grad_state = (grad_own + back_rev.astype(jnp.float32)).astype(jnp.bfloat16)
    grad_outer = jnp.dot(grad_state, w_flat.T, preferred_element_type=jnp.float32).astype(
        jnp.bfloat16
    )
    bil = contract(outer, grad_state)
    grad_trip = jnp.einsum(
        "ebc,ekb->ekc",
        grad_outer.reshape(edges, basis_count, narrow),
        basis,
        preferred_element_type=jnp.float32,
    )
    grad_trip = jnp.where(valid[:, :, None], grad_trip, 0.0)
    grad_pool = (
        jnp.zeros((pool_size, narrow), jnp.float32)
        .at[trip_index.reshape(-1)]
        .add(grad_trip.reshape(-1, narrow))
    )
    grad_send = grad_pool[edges:].astype(jnp.bfloat16).reshape(list_count, capacity, narrow)
    grad_arrived = deliver(packed([grad_send], list_count), -1)
    (grad_back,) = unpacked(grad_arrived, [narrow], list_count, capacity)
    grad_red = (
        grad_pool[:edges]
        .at[list_rows.reshape(-1)]
        .add(jnp.where(filled[:, :, None], grad_back.astype(jnp.float32), 0.0).reshape(-1, narrow))
    )
    grad_down = (grad_red * silu_slope(pre_down)).astype(jnp.bfloat16)
    down_sum = contract(hidden, grad_down)
    grad_hidden = jnp.dot(grad_down, w_down.T, preferred_element_type=jnp.float32)
    grad_edge = (grad_hidden * silu_slope(pre_edge)).astype(jnp.bfloat16)
    edge_sum = contract(source, grad_edge)
    grad_messages = jnp.dot(grad_edge, w_edge.T, preferred_element_type=jnp.float32).astype(
        jnp.bfloat16
    )[None]
    factor = 1.0 / math.sqrt(lax.axis_size("dp") * lax.axis_size("graph") * edges)
    shares = (
        lax.psum_scatter(
            (edge_sum * factor).astype(jnp.bfloat16), "graph", scatter_dimension=0, tiled=True
        ).astype(jnp.float32),
        lax.psum_scatter(
            (down_sum * factor).astype(jnp.bfloat16), "graph", scatter_dimension=0, tiled=True
        ).astype(jnp.float32),
        lax.psum_scatter(
            (bil.reshape(basis_count, narrow * narrow) * factor).astype(jnp.bfloat16),
            "graph",
            scatter_dimension=1,
            tiled=True,
        ).astype(jnp.float32),
        lax.psum_scatter(
            (jnp.stack([up_ca, up_ac]) * factor).astype(jnp.bfloat16),
            "graph",
            scatter_dimension=2,
            tiled=True,
        ).astype(jnp.float32),
    )
    totals = (
        lax.psum(shares[0].astype(jnp.bfloat16), "dp").astype(jnp.float32),
        lax.psum(shares[1].astype(jnp.bfloat16), "dp").astype(jnp.float32),
        lax.psum(shares[2].astype(jnp.bfloat16), "dp").astype(jnp.float32),
        lax.psum(shares[3].astype(jnp.bfloat16), "dp").astype(jnp.float32),
    )
    return (grad_messages, totals[0], totals[1], totals[2], totals[3])


def solution(mesh):
    return jax.shard_map(
        body,
        mesh=mesh,
        in_specs=(
            P("dp", "graph", None),
            P("dp", "graph", None),
            P("dp", "graph", None),
            P(),
            P(),
            P(),
            P(),
            P("dp", "graph", None),
            P("dp", "graph", None),
            P("dp", "graph"),
            P("dp", "graph"),
            P("dp", "graph"),
        ),
        out_specs=(
            P("dp", "graph", None),
            P("graph", None),
            P("graph", None),
            P(None, "graph"),
            P(None, None, "graph"),
        ),
        check_vma=False,
    )
```

profile of v0, /device:TPU:0, one launch (start us, length us, event | category | flops | bytes accessed | tf_op | source)
XLA Modules:
  0.0 715.7 jit_solution(4398739669748465062)
XLA Ops:
  9.3 5.4 gather_fusion.1
  15.3 3.3 multiply_convert_fusion.3
  18.7 1.1 multiply_convert_fusion.5
  20.7 3.2 gather_fusion
  24.3 1.0 broadcast_select_fusion
  25.3 1.1 fusion.19
  26.9 4.0 collective-permute-start.1
  30.9 2.3 collective-permute-start.3
  34.7 3.8 reshape.197
  38.5 10.4 %copy.45 = bf16[1,1024,3584]{1,2,0:T(8,128)(2,1)} copy(bf16[1,1024,3584]{2,1,0:T(8,128)(2,1)} %param.14) | data formatting | bytes 14680064 | tf_op args[2]
  48.9 12.2 %copy.46 = bf16[1024,32,112]{2,1,0:T(8,128)(2,1)} copy(bf16[1024,32,112]{0,2,1:T(8,128)(2,1)} %bitcast.103) | data formatting | bytes 14680064 | tf_op jit(solution)/shard_map/reshape;squeeze | solution.py:102
  62.6 1.2 pad_maximum_fusion.1
  63.8 1.4 reshape_reshape.8
  66.7 2.8 pad_maximum_fusion
  69.5 114.1 %gather_fusion.2 = bf16[32768,64]{1,0:T(8,128)(2,1)} fusion(bf16[2048,64]{1,0:T(8,128)(2,1)S(1)} %copy.44, s32[32768]{0:T(1024)S(1)} %broadcast_clamp_fusion), kind=kCustom, calls=%fused_computation.2 | custom fusion | bytes 8519680 | tf_op jit(solution)/shard_map/gather | solution.py:101
  183.6 16.3 %convert_bitcast_fusion = bf16[1024,112,64]{1,2,0:T(8,128)(2,1)} fusion(bf16[1024,32,112]{2,1,0:T(8,128)(2,1)} %copy.46, bf16[1024,32,64]{2,1,0:T(8,128)(2,1)} %bitcast.102, pred[1024,32]{1,0:T(8,128)(4,1)S(1)} %copy.40), kind=kOutput, calls=%fused_computation.6 | convolution fusion | flops 479199232 | bytes 26247168 | tf_op jit(solution)/shard_map/ekb,ekc->ebc/dot_general | solution.py:103
  199.9 25.6 %copy.47 = bf16[1024,112,64]{0,2,1:T(8,128)(2,1)} copy(bf16[1024,112,64]{1,2,0:T(8,128)(2,1)} %convert_bitcast_fusion) | data formatting | bytes 29360128 | tf_op jit(solution)/shard_map/convert_element_type | solution.py:104
  225.4 5.8 gather_fusion.3
  231.3 8.4 %convolution_convert_fusion.3 = bf16[1024,64]{0,1:T(8,128)(2,1)S(1)} fusion(bf16[1024,7168]{0,1:T(8,128)(2,1)} %bitcast.99, bf16[7168,64]{1,0:T(8,128)(2,1)} %reshape.197), kind=kOutput, calls=%fused_computation.34 | convolution fusion | flops 939589632 | bytes 15728640 | tf_op jit(solution)/shard_map/dot_general | solution.py:106
  239.8 1.1 multiply_convert_fusion.1
  241.3 1.1 multiply_convert_fusion.2
  243.4 7.3 %convolution_convert_fusion = bf16[1024,7168]{1,0:T(8,128)(2,1)} fusion(bf16[1024,64]{0,1:T(8,128)(2,1)S(1)} %fusion.8, bf16[7168,64]{1,0:T(8,128)(2,1)S(1)} %copy-done.2), kind=kOutput, calls=%fused_computation.7 | convolution fusion | flops 946864128 | bytes 15728640 | tf_op jit(solution)/shard_map/dot_general | solution.py:120
  250.7 19.9 %copy.48 = bf16[1024,7168]{0,1:T(8,128)(2,1)} copy(bf16[1024,7168]{1,0:T(8,128)(2,1)} %convolution_convert_fusion) | data formatting | bytes 29360128 | tf_op jit(solution)/shard_map/convert_element_type | solution.py:120
  270.7 25.3 %copy.49 = bf16[1024,112,64]{1,2,0:T(8,128)(2,1)} copy(bf16[1024,112,64]{0,2,1:T(8,128)(2,1)} %bitcast.101) | data formatting | bytes 29360128 | tf_op jit(solution)/shard_map/reshape | solution.py:126
  295.9 20.1 %convolution_select_fusion = f32[1024,64,32]{1,2,0:T(8,128)} fusion(bf16[1024,112,64]{1,2,0:T(8,128)(2,1)} %copy.49, bf16[1024,32,112]{2,1,0:T(8,128)(2,1)} %copy.46, pred[1024,32]{1,0:T(8,128)(4,1)S(1)} %copy.40), kind=kOutput, calls=%fused_computation.8 | convolution fusion | flops 471859200 | bytes 30441472 | tf_op jit(solution)/shard_map/ebc,ekb->ekc/dot_general | solution.py:124
  316.1 179.3 %scatter_custom_fusion = f32[2048,64]{1,0:T(8,128)S(1)} fusion(s32[32768]{0:T(1024)} %copy-done.9, f32[32768,64]{1,0:T(8,128)} %bitcast.104, f32[]{:T(128)} %constant.7.clone.1), kind=kCustom, calls=%fused_computation.49 | custom fusion | flops 2097152 | bytes 524800 | tf_op jit(solution)/shard_map/scatter-add | solution.py:134
  495.8 1.6 collective-permute-start.5
  497.4 18.4 %collective-permute-start.6 = (bf16[128,128]{1,0:T(8,128)(2,1)S(1)}, bf16[128,128]{1,0:T(8,128)(2,1)S(1)}, u32[]{:S(2)}, u32[]{:S(2)}) collective-permute-start(bf16[128,128]{1,0:T(8,128)(2,1)S(1)} %squeeze.58), channel_id=1, source_target_pairs={{2,0},{3,1},{4,2},{5,3},{6,4},{7,5},{0,6},{1,7},{10,8},{11,9},{12,... | collective-permute-start | bytes 98312 | tf_op jit(solution)/shard_map/ppermute | solution.py:14
  515.8 1.4 collective-permute-start.4
  517.5 4.0 collective-permute-done.7
  521.8 6.8 scatter_custom_fusion.1
  529.0 2.5 multiply_convert_fusion
  532.4 1.0 copy.54
  533.7 10.7 %fusion.2 = bf16[7168,64]{0,1:T(8,128)(2,1)} fusion(bf16[1024,7168]{0,1:T(8,128)(2,1)} %bitcast.100, bf16[1024,64]{0,1:T(8,128)(2,1)S(1)} %fusion.8), kind=kOutput, calls=%fused_computation.12 | convolution fusion | flops 940441600 | bytes 15728640 | tf_op jit(solution)/shard_map/dot_general | solution.py:27
  544.4 1.9 copy.52
  546.3 2.3 convert_element_type.118
  548.7 1.6 convolution_bitcast_fusion
  551.7 2.4 fusion.9
  554.1 11.8 %reduce-scatter.13.cloned.1.call-done = bf16[64,512]{1,0:T(8,128)(2,1)} async-done(((bf16[512,512]{1,0:T(8,128)(2,1)}), bf16[64,512]{1,0:T(8,128)(2,1)}) %reduce-scatter.13.cloned.1.call-update) | async-done | bytes 65552
  565.9 1.6 copy.55
  567.5 31.1 %reduce-scatter.11.cloned.1.call-done = bf16[112,512]{1,0:T(8,128)(2,1)} async-done(((bf16[112,4096]{1,0:T(8,128)(2,1)}), bf16[112,512]{1,0:T(8,128)(2,1)}) %reduce-scatter.11.cloned.1.call-update) | async-done | bytes 114704 | tf_op jit(solution)/shard_map/reduce_scatter | solution.py:160
  598.6 2.9 fusion.4
  601.6 28.1 %reduce-scatter.15.cloned.1.call-done = bf16[64,128]{1,0:T(8,128)(2,1)} async-done(((bf16[512,128]{1,0:T(8,128)(2,1)}), bf16[64,128]{1,0:T(8,128)(2,1)}) %reduce-scatter.15.cloned.1.call-update) | async-done | bytes 16400
  630.6 30.5 %reduce-scatter.9.cloned.1.call-done = bf16[64,64]{1,0:T(8,128)(2,1)} async-done(((bf16[512,64]{1,0:T(8,128)(2,1)}), bf16[64,64]{1,0:T(8,128)(2,1)}) %reduce-scatter.9.cloned.1.call-update) | async-done | bytes 8208 | tf_op jit(solution)/shard_map/reduce_scatter | solution.py:157
  661.1 17.3 %all-reduce = (bf16[64,64]{1,0:T(8,128)(2,1)S(1)}, bf16[2,64,64]{2,1,0:T(8,128)(2,1)S(1)}) all-reduce(bf16[64,64]{1,0:T(8,128)(2,1)} %reduce-scatter.9.cloned.1.call-done, bf16[2,64,64]{2,1,0:T(8,128)(2,1)S(1)} %copy.57), channel_id=1, replica_groups=mesh['dp'=4,'graph'=8] {'dp'}, use_global_device_ids=true, to_apply=%region_5.6 | all-reduce | flops 12288 | bytes 49152 | tf_op jit(solution)/shard_map/psum | solution.py:175
  679.6 26.3 %all-reduce.4.cloned.1.call-done = (bf16[64,512]{0,1:T(8,128)(2,1)}, bf16[112,512]{1,0:T(8,128)(2,1)}) async-done(((bf16[64,512]{0,1:T(8,128)(2,1)}, bf16[112,512]{1,0:T(8,128)(2,1)}), (bf16[64,512]{0,1:T(8,128)(2,1)}, bf16[112,512]{1,0:T(8,128)(2,1)})) %all-reduce.4.cloned.1.call-update) | async-done | bytes 180240 | tf_op jit(solution)/shard_map/psum | solution.py:174
  706.0 1.6 copy.53
  707.6 1.6 convert_element_type.119
  (117 shorter events, 15.7 us)
Async XLA Ops:
  7.2 8.2 %copy-start = (bf16[1,1024,512]{2,1,0:T(8,128)(2,1)S(1)}, bf16[1,1024,512]{2,1,0:T(8,128)(2,1)}, u32[]{:S(2)}) copy-start(bf16[1,1024,512]{2,1,0:T(8,128)(2,1)} %param.12) | copy-start | bytes 3145732
  7.2 558.7 %reduce-scatter.13.cloned.1.call-start = ((), (), s32[]{:S(2)}) async-start(), calls=%async_computation.6 | async-start | bytes 589824
  15.3 3.4 copy-start.17
  18.7 1.1 copy-start.20
  19.8 0.7 copy-start.11
  24.2 9.0 %copy-start.14 = (s32[1,1024]{1,0:T(1,128)S(1)}, s32[1,1024]{1,0:T(1,128)}, u32[]{:S(2)}) copy-start(s32[1,1024]{1,0:T(1,128)} %param.22) | copy-start | bytes 12292
  24.3 9.0 %copy-start.10 = (s32[1,1024,32]{1,2,0:T(8,128)S(1)}, s32[1,1024,32]{1,2,0:T(8,128)}, u32[]{:S(2)}) copy-start(s32[1,1024,32]{1,2,0:T(8,128)} %param.19) | copy-start | bytes 393220
  24.3 9.7 %copy-start.15 = (s32[1,4,256]{2,1,0:T(4,128)S(1)}, s32[1,4,256]{2,1,0:T(4,128)}, u32[]{:S(2)}) copy-start(s32[1,4,256]{2,1,0:T(4,128)} %param.20) | copy-start | bytes 12292
  26.4 35.2 %collective-permute-start = (bf16[1152,128]{1,0:T(8,128)(2,1)}, bf16[1152,128]{1,0:T(8,128)(2,1)S(1)}, u32[]{:S(2)}, u32[]{:S(2)}) collective-permute-start(bf16[1152,128]{1,0:T(8,128)(2,1)} %get-tuple-element.24), channel_id=1, source_target_pairs={{7,0},{0,1},{1,2},{2,3},{3,4},{4,5},{5,6},{6,7},{15,8},{8,9},{9,10... | collective-permute-start | bytes 884744 | tf_op jit(solution)/shard_map/ppermute | solution.py:14
  26.9 34.8 %collective-permute-start.1 = (bf16[1152,128]{1,0:T(8,128)(2,1)}, bf16[1152,128]{1,0:T(8,128)(2,1)S(1)}, u32[]{:S(2)}, u32[]{:S(2)}) collective-permute-start(bf16[1152,128]{1,0:T(8,128)(2,1)} %get-tuple-element.25), channel_id=1, source_target_pairs={{1,0},{2,1},{3,2},{4,3},{5,4},{6,5},{7,6},{0,7},{9,8},{10,9},{11,1... | collective-permute-start | bytes 884744 | tf_op jit(solution)/shard_map/ppermute | solution.py:14
  30.9 30.7 %collective-permute-start.3 = (bf16[1152,128]{1,0:T(8,128)(2,1)}, bf16[1152,128]{1,0:T(8,128)(2,1)S(1)}, u32[]{:S(2)}, u32[]{:S(2)}) collective-permute-start(bf16[1152,128]{1,0:T(8,128)(2,1)} %get-tuple-element.26), channel_id=1, source_target_pairs={{2,0},{3,1},{4,2},{5,3},{6,4},{7,5},{0,6},{1,7},{10,8},{11,9},{12,... | collective-permute-start | bytes 884744 | tf_op jit(solution)/shard_map/ppermute | solution.py:14
  33.2 28.5 %collective-permute-start.2 = (bf16[1152,128]{1,0:T(8,128)(2,1)}, bf16[1152,128]{1,0:T(8,128)(2,1)S(1)}, u32[]{:S(2)}, u32[]{:S(2)}) collective-permute-start(bf16[1152,128]{1,0:T(8,128)(2,1)} %get-tuple-element.27), channel_id=1, source_target_pairs={{6,0},{7,1},{0,2},{1,3},{2,4},{3,5},{4,6},{5,7},{14,8},{15,9},{8,1... | collective-permute-start | bytes 884744 | tf_op jit(solution)/shard_map/ppermute | solution.py:14
  34.6 14.2 %copy-start.9 = (s32[32768]{0:T(1024)}, s32[32768]{0:T(1024)S(1)}, u32[]{:S(2)}) copy-start(s32[32768]{0:T(1024)S(1)} %reshape.235) | copy-start | bytes 393220
  61.6 0.7 copy-start.6
  61.7 0.8 copy-start.7
  61.7 0.9 copy-start.8
  63.8 2.9 copy-start.1
  231.3 8.4 %copy-start.13 = (bf16[2,64,512]{2,1,0:T(8,128)(2,1)S(1)}, bf16[2,64,512]{2,1,0:T(8,128)(2,1)}, u32[]{:S(2)}) copy-start(bf16[2,64,512]{2,1,0:T(8,128)(2,1)} %param.18) | copy-start | bytes 393220
  239.7 1.5 copy-start.19
  240.8 1.5 copy-start.3
  241.3 2.1 copy-start.2
  242.4 1.0 copy-start.4
  495.4 33.4 %copy-start.12 = (f32[1024,64]{0,1:T(8,128)S(1)}, f32[1024,64]{0,1:T(8,128)}, u32[]{:S(2)}) copy-start(f32[1024,64]{0,1:T(8,128)} %get-tuple-element.35) | copy-start | bytes 786436
  495.8 21.4 %collective-permute-start.5 = (bf16[128,128]{1,0:T(8,128)(2,1)S(1)}, bf16[128,128]{1,0:T(8,128)(2,1)S(1)}, u32[]{:S(2)}, u32[]{:S(2)}) collective-permute-start(bf16[128,128]{1,0:T(8,128)(2,1)S(1)} %squeeze.57), channel_id=1, source_target_pairs={{7,0},{0,1},{1,2},{2,3},{3,4},{4,5},{5,6},{6,7},{15,8},{8,9},{9,10... | collective-permute-start | bytes 98312 | tf_op jit(solution)/shard_map/ppermute | solution.py:14
  497.4 20.0 %collective-permute-start.6 = (bf16[128,128]{1,0:T(8,128)(2,1)S(1)}, bf16[128,128]{1,0:T(8,128)(2,1)S(1)}, u32[]{:S(2)}, u32[]{:S(2)}) collective-permute-start(bf16[128,128]{1,0:T(8,128)(2,1)S(1)} %squeeze.58), channel_id=1, source_target_pairs={{2,0},{3,1},{4,2},{5,3},{6,4},{7,5},{0,6},{1,7},{10,8},{11,9},{12,... | collective-permute-start | bytes 98312 | tf_op jit(solution)/shard_map/ppermute | solution.py:14
  515.8 5.7 collective-permute-start.7
  515.8 5.8 collective-permute-start.4
  517.2 11.7 %copy-start.18 = (bf16[512,64]{0,1:T(8,128)(2,1)S(1)}, bf16[512,64]{0,1:T(8,128)(2,1)}, u32[]{:S(2)}) copy-start(bf16[512,64]{0,1:T(8,128)(2,1)} %param.16) | copy-start | bytes 196612
  531.4 1.0 copy-start.21
  533.4 65.2 %reduce-scatter.11.cloned.1.call-start = ((), (), s32[]{:S(2)}) async-start(), calls=%async_computation.5 | async-start | bytes 1032192 | tf_op jit(solution)/shard_map/reduce_scatter | solution.py:160
  548.6 1.7 copy-start.5
  548.6 81.1 %reduce-scatter.15.cloned.1.call-start = ((), (), s32[]{:S(2)}) async-start(), calls=%async_computation.7 | async-start | bytes 147456
  550.3 48.4 %copy-start.16 = (bf16[512,512]{1,0:T(8,128)(2,1)S(1)}, bf16[512,512]{1,0:T(8,128)(2,1)}, u32[]{:S(2)}) copy-start(bf16[512,512]{1,0:T(8,128)(2,1)} %param.15) | copy-start | bytes 1572868
  551.6 109.5 %reduce-scatter.9.cloned.1.call-start = ((), (), s32[]{:S(2)}) async-start(), calls=%async_computation.4 | async-start | bytes 147456 | tf_op jit(solution)/shard_map/reduce_scatter | solution.py:157
  554.1 151.9 %all-reduce.4.cloned.1.call-start = ((), (), s32[]{:S(2)}) async-start(), calls=%async_computation.8 | async-start | bytes 491520 | tf_op jit(solution)/shard_map/psum | solution.py:174
Sparse Core Ops, SparseCore 0:
  533.5 32.2 reduce-scatter.12
  568.1 30.3 reduce-scatter.10
  600.8 28.7 reduce-scatter.14
  632.3 28.7 reduce-scatter.8
  664.5 41.4 all-reduce.3
where the time goes:
time: 716 us
  local copies, waits for them, and re-layouts  243 us (34%)
  other arithmetic  199 us (28%)
  waiting for transfers between devices  132 us (18%)
  matrix products  80.8 us (11%)
  starting transfers between devices  28.7 us (4%)
  blocking collectives  17.3 us (2%)
  between operations  15.1 us (2%)
    scatter-add x1, other arithmetic, body(): grad_pool = jnp.zeros((pool_size, narrow), jnp.float32).at[trip_index.res...  179 us
    gather x1, local copies, waits for them, and re-layouts, body(): pool_red[trip_index]  114 us
    unnamed x7, waiting for transfers between devices  39.9 us
    reduce_scatter x1, waiting for transfers between devices, body(): lax.psum_scatter((bil.reshape(basis_count, narrow * narrow) * factor).ast...  31.1 us
    reduce_scatter x1, waiting for transfers between devices, body(): lax.psum_scatter((down_sum * factor).astype(jnp.bfloat16), 'graph', scatt...  30.5 us
    ppermute x8, starting transfers between devices, shifted(): return lax.ppermute(block, axis, route)  28.2 us
    psum x1, waiting for transfers between devices, body(): lax.psum(shares[0].astype(jnp.bfloat16), 'dp').astype(jnp.float32)  26.3 us
    convert_element_type x1, local copies, waits for them, and re-layouts, body(): outer = outer.astype(jnp.bfloat16).reshape(edges, basis_count * narrow)  25.6 us
  transfers between devices with their start and end apart: 13, of which 6 were waited for; matrix products, arithmetic and copies ran while one was open for 8% of the time, Pallas kernels for 0%

commit v1 on v0

v1 whole, which is shorter than its diff:
```python
import functools
import math

import jax
import jax.numpy as jnp
from jax import lax
from jax.experimental import pallas as pl
from jax.experimental.pallas import tpu as pltpu
from jax.sharding import PartitionSpec as P

inv_root = 0.7071067811865476
bf16 = jnp.bfloat16
f32 = jnp.float32
GROUP = 8
NN = (((1,), (0,)), ((), ()))
NT = (((1,), (1,)), ((), ()))
TN = (((0,), (0,)), ((), ()))


def mm(left, right, dims=NN):
    return lax.dot_general(left, right, dims, preferred_element_type=f32)


def silu_slope(values):
    sigma = jax.nn.sigmoid(values)
    return sigma * (1.0 + values * (1.0 - sigma))


def offsets(count):
    return [(which // 2 + 1) * (1 - 2 * (which % 2)) for which in range(count)]


def shifted(block, axis, distance):
    devices = range(lax.axis_size(axis))
    route = [((i - distance) % len(devices), i) for i in devices]
    return lax.ppermute(block, axis, route)


def iota(shape, dim):
    return lax.broadcasted_iota(jnp.int32, shape, dim)


def one_hot(index, shape, dim):
    return jnp.where(index == iota(shape, dim), 1.0, 0.0).astype(bf16)


def vmem():
    return pl.BlockSpec(memory_space=pltpu.VMEM)


def params(**extra):
    return pltpu.CompilerParams(vmem_limit_bytes=60 * 1024 * 1024, **extra)


def send_hot(rows_ref, count_ref, which, edges):
    capacity = rows_ref.shape[2]
    rows = rows_ref[0, which : which + 1, :]
    used = iota((1, capacity), 1) < count_ref[0, which]
    return one_hot(jnp.where(used, rows, -1), (edges, capacity), 0)


def front_kernel(
    count_ref, x_ref, we_ref, wd_ref, rows_ref, pre_ref, hid_ref, pdt_ref, red_ref, *send_refs
):
    edges = x_ref.shape[1]
    step = 256
    for start in range(0, edges, step):
        pre = mm(x_ref[0, start : start + step, :], we_ref[...])
        pre_ref[start : start + step, :] = pre
        hidden = (pre * jax.nn.sigmoid(pre)).astype(bf16)
        hid_ref[start : start + step, :] = hidden
        down = lax.dot_general(
            wd_ref[...], hidden, (((0,), (1,)), ((), ())), preferred_element_type=f32
        )
        pdt_ref[:, start : start + step] = down
        red_ref[:, start : start + step] = (down * jax.nn.sigmoid(down)).astype(bf16)
    for which, send_ref in enumerate(send_refs):
        hot = send_hot(rows_ref, count_ref, which, edges)
        send_ref[...] = mm(red_ref[...], hot).astype(bf16)


def smem():
    return pl.BlockSpec(memory_space=pltpu.SMEM)


def front(messages, w_edge, w_down, rows, counts):
    _, edges, model = messages.shape
    narrow = w_down.shape[1]
    _, lists, capacity = rows.shape
    return pl.pallas_call(
        front_kernel,
        out_shape=(
            jax.ShapeDtypeStruct((edges, model), f32),
            jax.ShapeDtypeStruct((edges, model), bf16),
            jax.ShapeDtypeStruct((narrow, edges), f32),
            jax.ShapeDtypeStruct((narrow, edges), bf16),
        )
        + (jax.ShapeDtypeStruct((narrow, capacity), bf16),) * lists,
        in_specs=[smem()] + [vmem()] * 4,
        out_specs=(vmem(),) * (4 + lists),
        compiler_params=params(),
        name="front",
    )(counts, messages, w_edge, w_down, rows)


def pick_kernel(count_ref, cot_ref, rows_ref, after_ref, *send_refs):
    edges = cot_ref.shape[1]
    for which, send_ref in enumerate(send_refs):
        hot = send_hot(rows_ref, count_ref, which, edges)
        send_ref[...] = mm(hot, cot_ref[0], TN).astype(bf16)


def pick(cotangent, rows, counts, after):
    _, edges, model = cotangent.shape
    _, lists, capacity = rows.shape
    return pl.pallas_call(
        pick_kernel,
        out_shape=(jax.ShapeDtypeStruct((capacity, model), bf16),) * lists,
        in_specs=[smem(), vmem(), vmem(), pl.BlockSpec(memory_space=pl.ANY)],
        out_specs=(vmem(),) * lists,
        compiler_params=params(),
        name="pick",
    )(counts, cotangent, rows, after)


def widen_weights(wb_ref, wide):
    basis, _ = wb_ref.shape
    narrow = wide.shape[1]
    padded = wide.shape[0] // narrow
    zeros = jnp.zeros((padded - basis, narrow), bf16)
    for c in range(0, narrow, 2):
        pair = wb_ref[:, c * narrow : (c + 2) * narrow]
        wide[c * padded : (c + 1) * padded, :] = jnp.concatenate(
            [pair[:, :narrow], zeros], axis=0
        )
        wide[(c + 1) * padded : (c + 2) * padded, :] = jnp.concatenate(
            [pair[:, narrow:], zeros], axis=0
        )


def split_index(trip, capacity):
    return jnp.bitwise_and(trip, capacity - 1), jnp.right_shift(
        trip, capacity.bit_length() - 1
    )


def forward_kernel(
    basis_count, sub, lists, basis_ref, trip_ref, red_ref, wb_ref, *rest
):
    recv_refs = rest[:lists]
    outer_ref, bas_ref, state_ref, pool, wide, slot_s, turn_s = rest[lists:]
    narrow, edges = red_ref.shape
    capacity = recv_refs[0].shape[1]
    rho = trip_ref.shape[1]
    slots = rho // GROUP
    padded = bas_ref.shape[1]
    locals_ = edges // capacity
    half = GROUP // 2

    @pl.when(pl.program_id(0) == 0)
    def _():
        for h in range(locals_):
            pool[h * narrow : (h + 1) * narrow, :] = red_ref[:, h * capacity : (h + 1) * capacity]
        for h in range(lists):
            pool[(locals_ + h) * narrow : (locals_ + h + 1) * narrow, :] = recv_refs[h][...]
        widen_weights(wb_ref, wide)

    groups = sub // GROUP
    lane = iota((1, rho), 1) % half
    row_half = iota((rho, padded), 0) % GROUP < half

    def body(index, carry):
        first = pl.multiple_of(index * sub, sub)
        first_group = pl.multiple_of(index * groups, groups)
        x = basis_ref[0, pl.ds(first, sub), :].astype(f32)
        for k in range(slots):
            tile, off = divmod(k * basis_count, 128)
            if off + basis_count <= 128:
                part = x[:, tile * 128 : tile * 128 + 128]
                if off:
                    part = pltpu.roll(part, 128 - off, 1)
            else:
                part = pltpu.roll(x[:, tile * 128 : tile * 128 + 256], 256 - off, 1)[:, :128]
            for g in range(groups):
                slot_s[g, k * GROUP : (k + 1) * GROUP, :] = part[g * GROUP : (g + 1) * GROUP, :]
        for g in range(groups):
            bas = slot_s[g].astype(bf16)
            bas_ref[pl.ds((first_group + g) * rho, rho), :] = bas
            lo, hi = split_index(trip_ref[pl.ds(first_group + g, 1), :], capacity)
            hot = one_hot(lo, (capacity, rho), 0)
            found = mm(pool[...], hot)
            gathered = jnp.zeros((narrow, rho), f32)
            for h in range(locals_ + lists):
                gathered = gathered + jnp.where(
                    hi == h, found[h * narrow : (h + 1) * narrow, :], 0.0
                )
            spread = jnp.concatenate(
                [jnp.where(lane == e, gathered, 0.0).astype(bf16) for e in range(half)], axis=0
            )
            zero = jnp.zeros_like(bas)
            pairs = jnp.concatenate(
                [jnp.where(row_half, bas, zero), jnp.where(row_half, zero, bas)], axis=1
            )
            outer = mm(spread, pairs)
            turn_s[g, : half * narrow, :] = outer[:, :padded]
            turn_s[g, half * narrow :, :] = outer[:, padded:]
        for g in range(0, groups, 2):
            for c in range(narrow):
                block = jnp.concatenate(
                    [
                        turn_s[g, pl.ds(c, GROUP, stride=narrow), :],
                        turn_s[g + 1, pl.ds(c, GROUP, stride=narrow), :],
                    ],
                    axis=0,
                )
                outer_ref[
                    pl.ds(pl.multiple_of(first + g * GROUP, 2 * GROUP), 2 * GROUP),
                    c * padded : (c + 1) * padded,
                ] = block.astype(bf16)
        return carry

    lax.fori_loop(0, outer_ref.shape[0] // sub, body, 0)
    state_ref[...] = mm(outer_ref[...], wide[...]).astype(bf16)


def forward(triplet_basis, trips, red, recv, w_bil):
    narrow, edges = red.shape
    lists = len(recv)
    capacity = recv[0].shape[1]
    basis_count = w_bil.shape[0]
    rho = trips.shape[1]
    padded = 128
    block = 256
    sub = 64
    steps = edges // block
    resident = lambda *shape: pl.BlockSpec(shape, lambda i: (0,) * len(shape))
    return pl.pallas_call(
        functools.partial(forward_kernel, basis_count, sub, lists),
        grid=(steps,),
        out_shape=(
            jax.ShapeDtypeStruct((edges, narrow * padded), bf16),
            jax.ShapeDtypeStruct((edges * rho // GROUP, padded), bf16),
            jax.ShapeDtypeStruct((edges, narrow), bf16),
        ),
        in_specs=[
            pl.BlockSpec((1, block, triplet_basis.shape[2]), lambda i: (0, i, 0)),
            pl.BlockSpec((block // GROUP, rho), lambda i: (i, 0)),
            resident(narrow, edges),
            resident(*w_bil.shape),
        ]
        + [resident(narrow, capacity)] * lists,
        out_specs=(
            pl.BlockSpec((block, narrow * padded), lambda i: (i, 0)),
            pl.BlockSpec((block * rho // GROUP, padded), lambda i: (i, 0)),
            pl.BlockSpec((block, narrow), lambda i: (i, 0)),
        ),
        scratch_shapes=[
            pltpu.VMEM((edges // capacity * narrow + lists * narrow, capacity), bf16),
            pltpu.VMEM((narrow * padded, narrow), bf16),
            pltpu.VMEM((sub // GROUP, rho, padded), f32),
            pltpu.VMEM((sub // GROUP, GROUP * narrow, padded), f32),
        ],
        compiler_params=params(),
        name="forward",
    )(triplet_basis, trips, red, w_bil, *recv)


def state_kernel(
    scale, parts, lists,
    count_ref, outer_ref, state_ref, cot_ref, rev_ref, own_ref, wu_ref, *rest
):
    recv_refs = rest[:lists]
    grad_ref, share_ref, ca_s, ac_s, bil_s = rest[lists:]
    block, narrow = state_ref.shape
    edges = own_ref.shape[1]
    capacity, model = recv_refs[0].shape
    columns = outer_ref.shape[1]
    pid = pl.program_id(0)

    @pl.when(pid == 0)
    def _():
        ca_s[...] = jnp.zeros_like(ca_s)
        ac_s[...] = jnp.zeros_like(ac_s)
        bil_s[...] = jnp.zeros_like(bil_s)

    state = state_ref[...]
    alive = pid * block + iota((block, 1), 0) < count_ref[0, 0]
    scaled = jnp.where(alive, cot_ref[0].astype(f32) * inv_root, 0.0)
    pre_ca = mm(state, wu_ref[0])
    grad_ca = (scaled * silu_slope(pre_ca)).astype(bf16)
    reverse = rev_ref[...]
    mirror = mm(one_hot(reverse, (edges, block), 0), own_ref[0], TN)
    for which, recv_ref in enumerate(recv_refs):
        base = edges + which * capacity
        mirror = mirror + mm(one_hot(reverse - base, (capacity, block), 0), recv_ref[...], TN)
    pre_ac = mm(state, wu_ref[1])
    grad_ac = (mirror * inv_root * silu_slope(pre_ac)).astype(bf16)
    ca_s[...] += mm(grad_ca, state, TN)
    ac_s[...] += mm(grad_ac, state, TN)
    back_rev = mm(grad_ac, wu_ref[1], NT).astype(bf16).astype(f32)
    grad_state = (mm(grad_ca, wu_ref[0], NT) + back_rev).astype(bf16)
    grad_ref[...] = grad_state
    wide_step = 1024
    for start in range(0, columns, wide_step):
        bil_s[:, start : start + wide_step] += mm(
            grad_state, outer_ref[:, start : start + wide_step], TN
        )

    @pl.when(pid == pl.num_programs(0) - 1)
    def _():
        dests, height, _ = share_ref.shape
        slabs = dests // parts
        span = columns // parts
        thin = model // dests
        both = jnp.concatenate([ca_s[...], ac_s[...]], axis=1) * scale
        for slab in range(slabs):
            for part in range(parts):
                dest = slab * parts + part
                share_ref[dest, :, :span] = (
                    bil_s[slab * height : (slab + 1) * height, part * span : (part + 1) * span]
                    * scale
                ).astype(bf16)
                first = (part * slabs + slab) * thin
                piece = both[first : first + thin, :]
                if thin < height:
                    piece = jnp.concatenate(
                        [piece, jnp.zeros((height - thin, 2 * narrow), f32)], axis=0
                    )
                share_ref[dest, :, span:] = piece.astype(bf16)


def state_grads(count, outer, state, cotangent, rev, recv_cot, w_up, scale, parts, slabs):
    edges, narrow = state.shape
    model = cotangent.shape[2]
    columns = outer.shape[1]
    block = 256
    lists = len(recv_cot)
    height = narrow // slabs
    share = (parts * slabs, height, columns // parts + 2 * narrow)
    resident = lambda *shape: pl.BlockSpec(shape, lambda i: (0,) * len(shape))
    return pl.pallas_call(
        functools.partial(state_kernel, scale, parts, lists),
        grid=(edges // block,),
        out_shape=(
            jax.ShapeDtypeStruct((edges, narrow), bf16),
            jax.ShapeDtypeStruct(share, bf16),
        ),
        in_specs=[
            smem(),
            pl.BlockSpec((block, columns), lambda i: (i, 0)),
            pl.BlockSpec((block, narrow), lambda i: (i, 0)),
            pl.BlockSpec((1, block, model), lambda i: (0, i, 0)),
            pl.BlockSpec((1, block), lambda i: (0, i)),
            resident(1, edges, model),
            resident(*w_up.shape),
        ]
        + [resident(*recv_cot[0].shape)] * lists,
        out_specs=(
            pl.BlockSpec((block, narrow), lambda i: (i, 0)),
            resident(*share),
        ),
        scratch_shapes=[
            pltpu.VMEM((model, narrow), f32),
            pltpu.VMEM((model, narrow), f32),
            pltpu.VMEM((narrow, columns), f32),
        ],
        compiler_params=params(),
        name="state_grads",
    )(count, outer, state, cotangent, rev, cotangent, w_up, *recv_cot)


def backward_kernel(
    sub, lists, bas_ref, grad_ref, trip_ref, wb_ref, home_ref, *rest
):
    back_refs = rest[:lists]
    pool_s, wide, turn_s, cast_s, hot_s = rest[lists:]
    block, narrow = grad_ref.shape
    padded = bas_ref.shape[1]
    rho = trip_ref.shape[1]
    rows, capacity = pool_s.shape
    half = GROUP // 2
    pid = pl.program_id(0)

    @pl.when(pid == 0)
    def _():
        widen_weights(wb_ref, wide)
        pool_s[...] = jnp.zeros_like(pool_s)

    grad_state = grad_ref[...]

    def spread(pair, carry):
        start = pl.multiple_of(pair * 2 * padded, 2 * padded)
        grad = mm(grad_state, wide[pl.ds(start, 2 * padded), :], NT)
        for g in range(block // GROUP):
            for side in range(2):
                turn_s[pl.ds(g * GROUP * narrow + 2 * pair + side, GROUP, stride=narrow), :] = grad[
                    g * GROUP : (g + 1) * GROUP, side * padded : (side + 1) * padded
                ]
        return carry

    lax.fori_loop(0, narrow // 2, spread, 0)
    groups = sub // GROUP
    lane = iota((1, rho), 1) % half
    row_half = iota((rho, padded), 0) % GROUP < half

    def body(index, carry):
        first_group = pl.multiple_of(index * groups, groups)
        for g in range(groups):
            here = first_group + g
            base = pl.multiple_of(here * GROUP * narrow, GROUP * narrow)
            bas = bas_ref[pl.ds(pl.multiple_of(here * rho, rho), rho), :]
            zero = jnp.zeros_like(bas)
            pairs = jnp.concatenate(
                [jnp.where(row_half, bas, zero), jnp.where(row_half, zero, bas)], axis=1
            )
            grads = jnp.concatenate(
                [
                    turn_s[pl.ds(base, half * narrow), :],
                    turn_s[pl.ds(base + half * narrow, half * narrow), :],
                ],
                axis=1,
            ).astype(bf16)
            mixed = mm(grads, pairs, NT)
            trip_grad = jnp.zeros((narrow, rho), f32)
            for e in range(half):
                trip_grad = trip_grad + jnp.where(
                    lane == e, mixed[e * narrow : (e + 1) * narrow, :], 0.0
                )
            lo, hi = split_index(trip_ref[pl.ds(here, 1), :], capacity)
            hot_s[:, g * rho : (g + 1) * rho] = one_hot(lo, (capacity, rho), 0)
            for h in range(rows // narrow):
                cast_s[h * narrow : (h + 1) * narrow, g * rho : (g + 1) * rho] = jnp.where(
                    hi == h, trip_grad, 0.0
                ).astype(bf16)
        pool_s[...] += mm(cast_s[...], hot_s[...], NT)
        return carry

    lax.fori_loop(0, block // sub, body, 0)

    @pl.when(pid == pl.num_programs(0) - 1)
    def _():
        home = home_ref.shape[0]
        home_ref[...] = pool_s[:home, :]
        for which, back_ref in enumerate(back_refs):
            first = home + which * narrow
            back_ref[...] = pool_s[first : first + narrow, :].astype(bf16)


def backward(bas, grad_state, trips, w_bil, capacity, lists):
    edges, narrow = grad_state.shape
    rho = trips.shape[1]
    padded = bas.shape[1]
    block = 256
    sub = 64
    home = edges // capacity * narrow
    rows = home + lists * narrow
    resident = lambda *shape: pl.BlockSpec(shape, lambda i: (0,) * len(shape))
    return pl.pallas_call(
        functools.partial(backward_kernel, sub, lists),
        grid=(edges // block,),
        out_shape=(jax.ShapeDtypeStruct((home, capacity), f32),)
        + (jax.ShapeDtypeStruct((narrow, capacity), bf16),) * lists,
        in_specs=[
            pl.BlockSpec((block * rho // GROUP, padded), lambda i: (i, 0)),
            pl.BlockSpec((block, narrow), lambda i: (i, 0)),
            pl.BlockSpec((block // GROUP, rho), lambda i: (i, 0)),
            resident(*w_bil.shape),
        ],
        out_specs=(resident(home, capacity),) + (resident(narrow, capacity),) * lists,
        scratch_shapes=[
            pltpu.VMEM((rows, capacity), f32),
            pltpu.VMEM((narrow * padded, narrow), bf16),
            pltpu.VMEM((block * narrow, padded), f32),
            pltpu.VMEM((rows, sub // GROUP * rho), bf16),
            pltpu.VMEM((capacity, sub // GROUP * rho), bf16),
        ],
        compiler_params=params(),
        name="backward",
    )(bas, grad_state, trips, w_bil)


def tail_kernel(
    scale, parts, lists,
    count_ref, pool_ref, rows_ref, pdt_ref, pre_ref, hid_ref, x_ref, we_ref, wd_ref, *rest
):
    back_refs = rest[:lists]
    out_ref, share_ref, grad_s = rest[lists:]
    narrow, edges = pdt_ref.shape
    capacity = back_refs[0].shape[1]
    model = pre_ref.shape[1]
    grad = jnp.concatenate(
        [pool_ref[h * narrow : (h + 1) * narrow, :] for h in range(edges // capacity)], axis=1
    )
    for which, back_ref in enumerate(back_refs):
        grad = grad + mm(back_ref[...], send_hot(rows_ref, count_ref, which, edges), NT)
    grad_down = (grad * silu_slope(pdt_ref[...])).astype(bf16)
    step = 256
    for start in range(0, edges, step):
        part = slice(start, start + step)
        grad_hidden = lax.dot_general(
            grad_down[:, part], wd_ref[...], (((0,), (1,)), ((), ())), preferred_element_type=f32
        )
        grad_edge = (grad_hidden * silu_slope(pre_ref[part, :])).astype(bf16)
        grad_s[part, :] = grad_edge
        out_ref[0, part, :] = mm(grad_edge, we_ref[...], NT).astype(bf16)
    dests, height, _ = share_ref.shape
    slabs = dests // parts
    down = lax.dot_general(
        hid_ref[...], grad_down, (((0,), (1,)), ((), ())), preferred_element_type=f32
    )
    down = jnp.concatenate([down, jnp.zeros_like(down)], axis=1)
    span = model // parts
    for start in range(0, model, step):
        both = (
            jnp.concatenate(
                [
                    mm(x_ref[0, :, start : start + step], grad_s[...], TN),
                    down[start : start + step, :],
                ],
                axis=1,
            )
            * scale
        ).astype(bf16)
        for first in range(start, start + step, height):
            part, slab = first // span, first % span // height
            share_ref[slab * parts + part] = both[first - start : first - start + height, :]


def tail(pool, back, rows, counts, pdt, pre, hidden, messages, w_edge, w_down, scale, parts, slabs):
    _, edges, model = messages.shape
    narrow = w_down.shape[1]
    dests = parts * slabs
    return pl.pallas_call(
        functools.partial(tail_kernel, scale, parts, len(back)),
        out_shape=(
            jax.ShapeDtypeStruct((1, edges, model), bf16),
            jax.ShapeDtypeStruct((dests, model // dests, model + 2 * narrow), bf16),
        ),
        in_specs=[smem()] + [vmem()] * (8 + len(back)),
        out_specs=(vmem(),) * 2,
        scratch_shapes=[pltpu.VMEM((edges, model), bf16)],
        compiler_params=params(),
        name="tail",
    )(counts, pool, rows, pdt, pre, hidden, messages, w_edge, w_down, *back)


def add_kernel(thin, *refs):
    *in_refs, out_ref = refs
    copies = out_ref.shape[0]
    at = 0
    for in_ref in in_refs:
        dests, height, wide = in_ref.shape
        total = in_ref[0].astype(f32)
        for dest in range(1, dests):
            total = total + in_ref[dest].astype(f32)
        total = total.astype(bf16)
        for copy in range(copies):
            out_ref[copy, :height, at : at + wide] = total
            if height < out_ref.shape[1]:
                out_ref[copy, height:, at : at + wide] = jnp.zeros(
                    (out_ref.shape[1] - height, wide), bf16
                )
        at += wide


def add_shares(early, late, copies):
    height = max(early.shape[1], late.shape[1])
    return pl.pallas_call(
        functools.partial(add_kernel, 0),
        out_shape=jax.ShapeDtypeStruct((copies, height, early.shape[2] + late.shape[2]), bf16),
        in_specs=[vmem()] * 2,
        out_specs=vmem(),
        compiler_params=params(),
        name="add_shares",
    )(early, late)


def finish_kernel(thin, in_ref, edge_ref, down_ref, bil_ref, up_ref):
    slabs, height, _ = in_ref.shape
    basis = bil_ref.shape[0]
    _, narrow, _ = up_ref.shape
    padded = 128
    span = bil_ref.shape[1] // narrow * padded
    model = edge_ref.shape[1]
    taken = narrow // slabs
    for c in range(bil_ref.shape[1] // narrow):
        block = jnp.concatenate(
            [in_ref[s, :taken, c * padded : (c + 1) * padded] for s in range(slabs)], axis=0
        ).astype(f32)
        bil_ref[:, c * narrow : (c + 1) * narrow] = block.T[:basis, :]
    both = jnp.concatenate([in_ref[s, :thin, span : span + 2 * narrow] for s in range(slabs)], axis=0)
    both = both.astype(f32).T
    up_ref[0] = both[:narrow, :]
    up_ref[1] = both[narrow:, :]
    at = span + 2 * narrow
    for s in range(slabs):
        part = slice(s * thin, (s + 1) * thin)
        edge_ref[part, :] = in_ref[s, :thin, at : at + model].astype(f32)
        down_ref[part, :] = in_ref[s, :thin, at + model : at + model + narrow].astype(f32)


def finish(shares, basis, narrow, model, parts):
    slabs = shares.shape[0]
    rows = model // parts
    return pl.pallas_call(
        functools.partial(finish_kernel, rows // slabs),
        out_shape=(
            jax.ShapeDtypeStruct((rows, model), f32),
            jax.ShapeDtypeStruct((rows, narrow), f32),
            jax.ShapeDtypeStruct((basis, narrow * narrow // parts), f32),
            jax.ShapeDtypeStruct((2, narrow, rows), f32),
        ),
        in_specs=[vmem()],
        out_specs=(vmem(),) * 4,
        compiler_params=params(),
        name="finish",
    )(shares)


def body(
    messages,
    cotangent,
    triplet_basis,
    w_edge,
    w_down,
    w_bil,
    w_up,
    trip_src,
    send_rows,
    send_count,
    rev_src,
    edge_count,
):
    _, edges, model = messages.shape
    narrow = w_down.shape[1]
    slots = trip_src.shape[2]
    _, lists, capacity = send_rows.shape
    basis_count = w_bil.shape[0]
    parts = lax.axis_size("graph")
    slabs = lax.axis_size("dp")
    scale = 1.0 / math.sqrt(slabs * parts * edges)
    shifts = offsets(lists)
    trips = (
        trip_src[0]
        .reshape(edges // GROUP, GROUP, slots)
        .transpose(0, 2, 1)
        .reshape(edges // GROUP, GROUP * slots)
    )
    pre, hidden, pdt, red, *send_red = front(messages, w_edge, w_down, send_rows, send_count)
    recv_red = [shifted(send_red[w], "graph", shifts[w]) for w in range(lists)]
    send_cot = pick(cotangent, send_rows, send_count, red)
    recv_cot = [shifted(send_cot[w], "graph", shifts[w]) for w in range(lists)]
    outer, bas, state = forward(triplet_basis, trips, red, recv_red, w_bil)
    grad_state, early = state_grads(
        edge_count, outer, state, cotangent, rev_src, recv_cot, w_up, scale, parts, slabs
    )
    early = lax.all_to_all(early, ("dp", "graph"), 0, 0)
    home, *returned = backward(bas, grad_state, trips, w_bil, capacity, lists)
    back = [shifted(returned[w], "graph", -shifts[w]) for w in range(lists)]
    grad_messages, late = tail(
        home, back, send_rows, send_count, pdt, pre, hidden, messages, w_edge, w_down,
        scale, parts, slabs,
    )
    late = lax.all_to_all(late, ("dp", "graph"), 0, 0)
    shares = lax.all_to_all(add_shares(early, late, slabs), "dp", 0, 0)
    edge_out, down_out, bil_out, up_out = finish(shares, basis_count, narrow, model, parts)
    return (grad_messages, edge_out, down_out, bil_out, up_out)


def solution(mesh):
    return jax.shard_map(
        body,
        mesh=mesh,
        in_specs=(
            P("dp", "graph", None),
            P("dp", "graph", None),
            P("dp", "graph", None),
            P(),
            P(),
            P(),
            P(),
            P("dp", "graph", None),
            P("dp", "graph", None),
            P("dp", "graph"),
            P("dp", "graph"),
            P("dp", "graph"),
        ),
        out_specs=(
            P("dp", "graph", None),
            P("graph", None),
            P("graph", None),
            P(None, "graph"),
            P(None, None, "graph"),
        ),
        check_vma=False,
    )
```

time: 716 us -> 281 us (0.39)
  local copies, waits for them, and re-layouts: 243 us -> 5.8 us
  other arithmetic: 199 us -> 0 us
  Pallas kernels: 0 us -> 167 us
  waiting for transfers between devices: 132 us -> 26.3 us
  matrix products: 80.8 us -> 0 us
  blocking collectives: 17.3 us -> 65.3 us
  starting transfers between devices: 28.7 us -> 15 us
  between operations: 15.1 us -> 1.42 us
    scatter-add x2 -> x0, other arithmetic: 186 us -> none  [the longest x1 179 us: body(): grad_pool = jnp.zeros((pool_size, narrow), jnp.float32).at[trip_index.res...]
    pallas_call x0 -> x8, Pallas kernels: none -> 167 us  [the longest x1 67.9 us: backward(): pl.pallas_call(functools.partial(backward_kernel, sub, lists), grid=(edge...]
    gather x5 -> x0, local copies, waits for them, and re-layouts: 129 us -> none  [the longest x1 114 us: body(): pool_red[trip_index]]
    dot_general x17 -> x0, matrix products: 80.8 us -> none  [the longest x1 20.1 us: body(): jnp.einsum('ebc,ekb->ekc', grad_outer.reshape(edges, basis_count, narrow)...]
    all_to_all x0 -> x3, blocking collectives: none -> 65.3 us  [the longest x1 32.8 us: body(): early = lax.all_to_all(early, ('dp', 'graph'), 0, 0)]
    reduce_scatter x2 -> x0, waiting for transfers between devices: 61.6 us -> none  [the longest x1 31.1 us: body(): lax.psum_scatter((bil.reshape(basis_count, narrow * narrow) * factor).ast...]
    convert_element_type x5 -> x0, local copies, waits for them, and re-layouts: 49.8 us -> none  [the longest x1 25.6 us: body(): outer = outer.astype(jnp.bfloat16).reshape(edges, basis_count * narrow)]
    unnamed x7 -> x0, waiting for transfers between devices: 39.9 us -> none
  transfers between devices with their start and end apart: 13 -> 12, of which waited for: 6 -> 5; matrix products, arithmetic and copies ran while one was open for 8% -> 1% of each run, Pallas kernels for 0% -> 23%
where the time goes in v1:
time: 281 us; the launch traced here: 280 us
  Pallas kernels  167 us (59%)
  blocking collectives  65.3 us (23%)
  waiting for transfers between devices  26.3 us (9%)
  starting transfers between devices  15 us (5%)
  local copies, waits for them, and re-layouts  5.8 us (2%)
    pallas_call x1, Pallas kernels, backward(): pl.pallas_call(functools.partial(backward_kernel, sub, lists), grid=(edge...  67.9 us
    pallas_call x1, Pallas kernels, forward(): pl.pallas_call(functools.partial(forward_kernel, basis_count, sub, lists)...  65.6 us
    all_to_all x1, blocking collectives, body(): early = lax.all_to_all(early, ('dp', 'graph'), 0, 0)  32.8 us
    ppermute x12, waiting for transfers between devices, shifted(): return lax.ppermute(block, axis, route)  26.3 us
    all_to_all x1, blocking collectives, body(): late = lax.all_to_all(late, ('dp', 'graph'), 0, 0)  22.4 us
    ppermute x12, starting transfers between devices, shifted(): return lax.ppermute(block, axis, route)  15 us
    pallas_call x1, Pallas kernels, state_grads(): pl.pallas_call(functools.partial(state_kernel, scale, parts, lists), grid...  14.9 us
    all_to_all x1, blocking collectives, body(): shares = lax.all_to_all(add_shares(early, late, slabs), 'dp', 0, 0)  10.1 us
  transfers between devices with their start and end apart: 12, of which 5 were waited for; matrix products, arithmetic and copies ran while one was open for 1% of the time, Pallas kernels for 23%

profile of v1, /device:TPU:0, one launch (start us, length us, event | category | flops | bytes accessed | tf_op | source)
XLA Modules:
  0.0 280.4 jit_solution(8477824034602137893)
XLA Ops:
  0.6 1.6 copy.22.wd_ref
  2.2 4.5 %front.1 = (f32[1024,512]{1,0:T(8,128)}, bf16[1024,512]{1,0:T(8,128)(2,1)}, f32[64,1024]{1,0:T(8,128)}, bf16[64,1024]{1,0:T(8,128)(2,1)}, bf16[64,256]{1,0:T(8,1...) custom-call(s32[1,4]{1,0:T(1,128)} %count_ref.6, ...), custom_call_target="tpu_custom_call" | custom-call | tf_op jit(solution)/shard_map/front/pallas_call | solution.py:90
  6.8 3.2 %pick.1 = (bf16[256,512]{1,0:T(8,128)(2,1)}, bf16[256,512]{1,0:T(8,128)(2,1)}, bf16[256,512]{1,0:T(8,128)(2,1)}, bf16[256,512]{1,0:T(8,128)(2,1)}) custom-call(s32[1,4]{1,0:T(1,128)} %count_ref.6, bf16[1,1024,512]{2,1,0:T(8,128)(2,1)} %own_ref.1, s32[1,4,256]{2,1,0:T(4,128)} %rows_ref.5, bf16[64,1024]{1,0:T(8,128)(2,1)} %get-tuple-element.33.red_ref.after_ref), custom_call_target="tpu_custom_call" | custom-call | tf_op jit(solution)/shard_map/pick/pallas_call | solution.py:116
  10.0 0.5 collective-permute-start.4
  10.5 4.0 %collective-permute-start.5 = (bf16[256,512]{1,0:T(8,128)(2,1)}, bf16[256,512]{1,0:T(8,128)(2,1)S(1)}, u32[]{:S(2)}, u32[]{:S(2)}) collective-permute-start(bf16[256,512]{1,0:T(8,128)(2,1)} %get-tuple-element.42), channel_id=1, source_target_pairs={{1,0},{2,1},{3,2},{4,3},{5,4},{6,5},{7,6},{0,7},{9,8},{10,9},{11,1... | collective-permute-start | bytes 786440 | tf_op jit(solution)/shard_map/ppermute | solution.py:36
  14.5 0.3 collective-permute-start.6
  14.8 3.5 %collective-permute-start.7 = (bf16[256,512]{1,0:T(8,128)(2,1)}, bf16[256,512]{1,0:T(8,128)(2,1)S(1)}, u32[]{:S(2)}, u32[]{:S(2)}) collective-permute-start(bf16[256,512]{1,0:T(8,128)(2,1)} %get-tuple-element.44), channel_id=1, source_target_pairs={{2,0},{3,1},{4,2},{5,3},{6,4},{7,5},{0,6},{1,7},{10,8},{11,9},{12,... | collective-permute-start | bytes 786440 | tf_op jit(solution)/shard_map/ppermute | solution.py:36
  18.4 0.0 collective-permute-start
  18.4 12.6 %collective-permute-done.rest_0_ = bf16[64,256]{1,0:T(8,128)(2,1)S(1)} collective-permute-done((bf16[64,256]{1,0:T(8,128)(2,1)}, bf16[64,256]{1,0:T(8,128)(2,1)S(1)}, u32[]{:S(2)}, u32[]{:S(2)}) %collective-permute-start) | collective-permute-done | bytes 32800 | tf_op jit(solution)/shard_map/ppermute | solution.py:36
  31.0 0.0 collective-permute-start.1
  31.0 1.9 collective-permute-done.1.rest_1_
  32.9 0.9 collective-permute-start.2
  33.8 5.8 %collective-permute-done.2.rest_2_ = bf16[64,256]{1,0:T(8,128)(2,1)S(1)} collective-permute-done((bf16[64,256]{1,0:T(8,128)(2,1)}, bf16[64,256]{1,0:T(8,128)(2,1)S(1)}, u32[]{:S(2)}, u32[]{:S(2)}) %collective-permute-start.2) | collective-permute-done | bytes 32800 | tf_op jit(solution)/shard_map/ppermute | solution.py:36
  39.5 2.0 collective-permute-start.3
  42.2 1.1 copy.20
  43.3 0.2 copy.21
  43.5 0.8 copy.23.trip_ref
  44.3 0.0 collective-permute-done.3.rest_3_
  44.3 0.0 copy-done.8
  44.3 0.0 copy-done.11
  44.3 0.0 copy-start.12
  44.3 0.6 copy-done.12
  44.9 65.6 %forward.1 = (bf16[1024,8192]{1,0:T(8,128)(2,1)}, bf16[32768,128]{1,0:T(8,128)(2,1)}, bf16[1024,64]{1,0:T(8,128)(2,1)}) custom-call(bf16[1,1024,3584]{2,1,0:T(8,128)(2,1)} %basis_ref.1, s32[128,256]{1,0:T(8,128)} %copy.23.trip_ref, bf16[64,1024]{1,0:T(8,128)(2,1)} %get-tuple-element.33.red_ref.after_ref, bf16[112,4096]{1,0:T(8,128)(2,1)} %wb_ref.3, ...), custom_call_target="tpu_custom_call" | custom-call | tf_op jit(solution)/shard_map/forward/pallas_call | solution.py:237
  110.5 0.0 collective-permute-done.4.rest_0_
  110.5 0.0 collective-permute-done.5.rest_1_
  110.5 0.0 collective-permute-done.6.rest_2_
  110.5 0.0 collective-permute-done.7.rest_3_
  110.6 0.6 copy-done.1
  111.2 0.1 copy-done.2
  111.3 0.1 copy-done.3
  111.4 0.1 copy-done.4
  111.5 14.9 %state_grads.1 = (bf16[1024,64]{1,0:T(8,128)(2,1)}, bf16[32,16,1152]{2,1,0:T(8,128)(2,1)}) custom-call(s32[1,1]{1,0:T(1,128)S(6)} %copy.26.count_ref, bf16[1024,8192]{1,0:T(8,128)(2,1)} %get-tuple-element.39.outer_ref, bf16[1024,64]{1,0:T(8,128)(2,1)} %get-tuple-element.40.state_ref, bf16[1,1024,512]{2,1,0:T(8,128)(2,1)} %own_ref.1, s32[1,1024]{1,0:T(1,128)} %rev_ref.1, ...), custom_call_target="tpu_custom_call" | custom-call | tf_op jit(solution)/shard_map/state_grads/pallas_call | solution.py:341
  126.4 67.9 %backward.1 = (f32[256,256]{1,0:T(8,128)}, bf16[64,256]{1,0:T(8,128)(2,1)}, bf16[64,256]{1,0:T(8,128)(2,1)}, bf16[64,256]{1,0:T(8,128)(2,1)}, bf16[64,256]{1,0:T(8,128)(2,1)}) custom-call(bf16[32768,128]{1,0:T(8,128)(2,1)} %get-tuple-element.38.bas_ref, bf16[1024,64]{1,0:T(8,128)(2,1)} %get-tuple-element.45.grad_ref, s32[128,256]{1,0:T(8,128)} %copy.23.trip_ref, ...), custom_call_target="tpu_custom_call" | custom-call | tf_op jit(solution)/shard_map/backward/pallas_call | solution.py:458
  194.3 0.8 collective-permute-start.8
  195.1 0.0 collective-permute-start.9
  195.1 2.9 %collective-permute-start.10 = (bf16[64,256]{1,0:T(8,128)(2,1)}, bf16[64,256]{1,0:T(8,128)(2,1)S(1)}, u32[]{:S(2)}, u32[]{:S(2)}) collective-permute-start(bf16[64,256]{1,0:T(8,128)(2,1)} %get-tuple-element.52), channel_id=1, source_target_pairs={{2,0},{3,1},{4,2},{5,3},{6,4},{7,5},{0,6},{1,7},{10,8},{11,9},{12,... | collective-permute-start | bytes 98312 | tf_op jit(solution)/shard_map/ppermute | solution.py:36
  198.0 0.0 collective-permute-start.11
  198.0 0.0 collective-permute-done.8.rest_0_
  198.0 2.4 collective-permute-done.9.rest_1_
  200.4 0.0 collective-permute-done.10.rest_2_
  200.4 3.6 %collective-permute-done.11.rest_3_ = bf16[64,256]{1,0:T(8,128)(2,1)S(1)} collective-permute-done((bf16[64,256]{1,0:T(8,128)(2,1)}, bf16[64,256]{1,0:T(8,128)(2,1)S(1)}, u32[]{:S(2)}, u32[]{:S(2)}) %collective-permute-start.11) | collective-permute-done | bytes 32800 | tf_op jit(solution)/shard_map/ppermute | solution.py:36
  204.1 0.6 copy-done.10
  204.6 6.3 %tail.1 = (bf16[1,1024,512]{2,1,0:T(8,128)(2,1)}, bf16[32,16,640]{2,1,0:T(8,128)(2,1)}) custom-call(s32[1,4]{1,0:T(1,128)} %count_ref.6, f32[256,256]{1,0:T(8,128)} %get-tuple-element.46.pool_ref, s32[1,4,256]{2,1,0:T(4,128)} %rows_ref.5, f32[64,1024]{1,0:T(8,128)} %get-tuple-element.47.pdt_ref, f32[1024,512]{1,0:T(8,128)} %get-tuple-element.48.pre_ref, ...), custom_call_target="tpu_custom_call" | custom-call | tf_op jit(solution)/shard_map/tail/pallas_call | solution.py:533
  210.9 22.4 %all_to_all.15.refs_1_ = bf16[32,16,640]{2,1,0:T(8,128)(2,1)} all-to-all(bf16[32,16,640]{2,1,0:T(8,128)(2,1)} %get-tuple-element.56), channel_id=1, replica_groups=mesh['dp'=4,'graph'=8] {'dp','graph'}, dimensions={0} | all-to-all | bytes 1310720 | tf_op jit(solution)/shard_map/all_to_all | solution.py:664
  233.3 32.8 %all_to_all.16.refs_0_ = bf16[32,16,1152]{2,1,0:T(8,128)(2,1)} all-to-all(bf16[32,16,1152]{2,1,0:T(8,128)(2,1)S(1)} %copy-done), channel_id=1, replica_groups=mesh['dp'=4,'graph'=8] {'dp','graph'}, dimensions={0} | all-to-all | bytes 2359296 | tf_op jit(solution)/shard_map/all_to_all | solution.py:657
  266.0 2.4 add_shares.1
  268.4 10.1 %all_to_all.17.in_ref = bf16[4,16,1792]{2,1,0:T(8,128)(2,1)} all-to-all(bf16[4,16,1792]{2,1,0:T(8,128)(2,1)} %add_shares.1), channel_id=1, replica_groups=mesh['dp'=4,'graph'=8] {'dp'}, dimensions={0} | all-to-all | bytes 458752 | tf_op jit(solution)/shard_map/all_to_all | solution.py:665
  278.6 1.9 finish.1
  (17 shorter events, 0.0 us)
Async XLA Ops:
  10.0 100.5 %collective-permute-start.4 = (bf16[256,512]{1,0:T(8,128)(2,1)}, bf16[256,512]{1,0:T(8,128)(2,1)S(1)}, u32[]{:S(2)}, u32[]{:S(2)}) collective-permute-start(bf16[256,512]{1,0:T(8,128)(2,1)} %get-tuple-element.41), channel_id=1, source_target_pairs={{7,0},{0,1},{1,2},{2,3},{3,4},{4,5},{5,6},{6,7},{15,8},{8,9},{9,10... | collective-permute-start | bytes 786440 | tf_op jit(solution)/shard_map/ppermute | solution.py:36
  10.5 100.0 %collective-permute-start.5 = (bf16[256,512]{1,0:T(8,128)(2,1)}, bf16[256,512]{1,0:T(8,128)(2,1)S(1)}, u32[]{:S(2)}, u32[]{:S(2)}) collective-permute-start(bf16[256,512]{1,0:T(8,128)(2,1)} %get-tuple-element.42), channel_id=1, source_target_pairs={{1,0},{2,1},{3,2},{4,3},{5,4},{6,5},{7,6},{0,7},{9,8},{10,9},{11,1... | collective-permute-start | bytes 786440 | tf_op jit(solution)/shard_map/ppermute | solution.py:36
  14.5 96.0 %collective-permute-start.6 = (bf16[256,512]{1,0:T(8,128)(2,1)}, bf16[256,512]{1,0:T(8,128)(2,1)S(1)}, u32[]{:S(2)}, u32[]{:S(2)}) collective-permute-start(bf16[256,512]{1,0:T(8,128)(2,1)} %get-tuple-element.43), channel_id=1, source_target_pairs={{6,0},{7,1},{0,2},{1,3},{2,4},{3,5},{4,6},{5,7},{14,8},{15,9},{8,1... | collective-permute-start | bytes 786440 | tf_op jit(solution)/shard_map/ppermute | solution.py:36
  14.8 95.7 %collective-permute-start.7 = (bf16[256,512]{1,0:T(8,128)(2,1)}, bf16[256,512]{1,0:T(8,128)(2,1)S(1)}, u32[]{:S(2)}, u32[]{:S(2)}) collective-permute-start(bf16[256,512]{1,0:T(8,128)(2,1)} %get-tuple-element.44), channel_id=1, source_target_pairs={{2,0},{3,1},{4,2},{5,3},{6,4},{7,5},{0,6},{1,7},{10,8},{11,9},{12,... | collective-permute-start | bytes 786440 | tf_op jit(solution)/shard_map/ppermute | solution.py:36
  18.4 12.6 %collective-permute-start = (bf16[64,256]{1,0:T(8,128)(2,1)}, bf16[64,256]{1,0:T(8,128)(2,1)S(1)}, u32[]{:S(2)}, u32[]{:S(2)}) collective-permute-start(bf16[64,256]{1,0:T(8,128)(2,1)} %get-tuple-element.34), channel_id=1, source_target_pairs={{7,0},{0,1},{1,2},{2,3},{3,4},{4,5},{5,6},{6,7},{15,8},{8,9},{9,10... | collective-permute-start | bytes 98312 | tf_op jit(solution)/shard_map/ppermute | solution.py:36
  31.0 13.4 %copy-start.5 = (bf16[64,256]{1,0:T(8,128)(2,1)}, bf16[64,256]{1,0:T(8,128)(2,1)S(1)}, u32[]{:S(2)}) copy-start(bf16[64,256]{1,0:T(8,128)(2,1)S(1)} %collective-permute-done.rest_0_) | copy-start | bytes 98308
  31.0 1.9 collective-permute-start.1
  32.9 11.4 %copy-start.8 = (bf16[64,256]{1,0:T(8,128)(2,1)}, bf16[64,256]{1,0:T(8,128)(2,1)S(1)}, u32[]{:S(2)}) copy-start(bf16[64,256]{1,0:T(8,128)(2,1)S(1)} %collective-permute-done.1.rest_1_) | copy-start | bytes 98308
  32.9 6.7 %collective-permute-start.2 = (bf16[64,256]{1,0:T(8,128)(2,1)}, bf16[64,256]{1,0:T(8,128)(2,1)S(1)}, u32[]{:S(2)}, u32[]{:S(2)}) collective-permute-start(bf16[64,256]{1,0:T(8,128)(2,1)} %get-tuple-element.36), channel_id=1, source_target_pairs={{6,0},{7,1},{0,2},{1,3},{2,4},{3,5},{4,6},{5,7},{14,8},{15,9},{8,1... | collective-permute-start | bytes 98312 | tf_op jit(solution)/shard_map/ppermute | solution.py:36
  39.5 4.8 %copy-start.11 = (bf16[64,256]{1,0:T(8,128)(2,1)}, bf16[64,256]{1,0:T(8,128)(2,1)S(1)}, u32[]{:S(2)}) copy-start(bf16[64,256]{1,0:T(8,128)(2,1)S(1)} %collective-permute-done.2.rest_2_) | copy-start | bytes 98308
  39.5 4.8 %collective-permute-start.3 = (bf16[64,256]{1,0:T(8,128)(2,1)}, bf16[64,256]{1,0:T(8,128)(2,1)S(1)}, u32[]{:S(2)}, u32[]{:S(2)}) collective-permute-start(bf16[64,256]{1,0:T(8,128)(2,1)} %get-tuple-element.37), channel_id=1, source_target_pairs={{2,0},{3,1},{4,2},{5,3},{6,4},{7,5},{0,6},{1,7},{10,8},{11,9},{12,... | collective-permute-start | bytes 98312 | tf_op jit(solution)/shard_map/ppermute | solution.py:36
  44.3 0.6 copy-start.12
  110.5 0.7 copy-start.1
  110.5 0.8 copy-start.2
  110.5 0.9 copy-start.3
  110.5 0.9 copy-start.4
  126.3 106.9 %copy-start = (bf16[32,16,1152]{2,1,0:T(8,128)(2,1)S(1)}, bf16[32,16,1152]{2,1,0:T(8,128)(2,1)}, u32[]{:S(2)}) copy-start(bf16[32,16,1152]{2,1,0:T(8,128)(2,1)} %get-tuple-element.55) | copy-start | bytes 3538948
  194.3 3.7 %collective-permute-start.8 = (bf16[64,256]{1,0:T(8,128)(2,1)}, bf16[64,256]{1,0:T(8,128)(2,1)S(1)}, u32[]{:S(2)}, u32[]{:S(2)}) collective-permute-start(bf16[64,256]{1,0:T(8,128)(2,1)} %get-tuple-element.50), channel_id=1, source_target_pairs={{1,0},{2,1},{3,2},{4,3},{5,4},{6,5},{7,6},{0,7},{9,8},{10,9},{11,1... | collective-permute-start | bytes 98312 | tf_op jit(solution)/shard_map/ppermute | solution.py:36
  195.1 5.4 %collective-permute-start.9 = (bf16[64,256]{1,0:T(8,128)(2,1)}, bf16[64,256]{1,0:T(8,128)(2,1)S(1)}, u32[]{:S(2)}, u32[]{:S(2)}) collective-permute-start(bf16[64,256]{1,0:T(8,128)(2,1)} %get-tuple-element.51), channel_id=1, source_target_pairs={{7,0},{0,1},{1,2},{2,3},{3,4},{4,5},{5,6},{6,7},{15,8},{8,9},{9,10... | collective-permute-start | bytes 98312 | tf_op jit(solution)/shard_map/ppermute | solution.py:36
  195.1 5.4 %collective-permute-start.10 = (bf16[64,256]{1,0:T(8,128)(2,1)}, bf16[64,256]{1,0:T(8,128)(2,1)S(1)}, u32[]{:S(2)}, u32[]{:S(2)}) collective-permute-start(bf16[64,256]{1,0:T(8,128)(2,1)} %get-tuple-element.52), channel_id=1, source_target_pairs={{2,0},{3,1},{4,2},{5,3},{6,4},{7,5},{0,6},{1,7},{10,8},{11,9},{12,... | collective-permute-start | bytes 98312 | tf_op jit(solution)/shard_map/ppermute | solution.py:36
  198.0 6.0 %collective-permute-start.11 = (bf16[64,256]{1,0:T(8,128)(2,1)}, bf16[64,256]{1,0:T(8,128)(2,1)S(1)}, u32[]{:S(2)}, u32[]{:S(2)}) collective-permute-start(bf16[64,256]{1,0:T(8,128)(2,1)} %get-tuple-element.53), channel_id=1, source_target_pairs={{6,0},{7,1},{0,2},{1,3},{2,4},{3,5},{4,6},{5,7},{14,8},{15,9},{8,1... | collective-permute-start | bytes 98312 | tf_op jit(solution)/shard_map/ppermute | solution.py:36
  198.0 6.0 %copy-start.6 = (bf16[64,256]{1,0:T(8,128)(2,1)}, bf16[64,256]{1,0:T(8,128)(2,1)S(1)}, u32[]{:S(2)}) copy-start(bf16[64,256]{1,0:T(8,128)(2,1)S(1)} %collective-permute-done.8.rest_0_) | copy-start | bytes 98308
  200.4 3.6 %copy-start.7 = (bf16[64,256]{1,0:T(8,128)(2,1)}, bf16[64,256]{1,0:T(8,128)(2,1)S(1)}, u32[]{:S(2)}) copy-start(bf16[64,256]{1,0:T(8,128)(2,1)S(1)} %collective-permute-done.9.rest_1_) | copy-start | bytes 98308
  200.4 3.6 %copy-start.9 = (bf16[64,256]{1,0:T(8,128)(2,1)}, bf16[64,256]{1,0:T(8,128)(2,1)S(1)}, u32[]{:S(2)}) copy-start(bf16[64,256]{1,0:T(8,128)(2,1)S(1)} %collective-permute-done.10.rest_2_) | copy-start | bytes 98308
  204.0 0.6 copy-start.10

commit v2 on v1

v2 whole, which is shorter than its diff:
```python
import functools
import math

import jax
import jax.numpy as jnp
from jax import lax
from jax.experimental import pallas as pl
from jax.experimental.pallas import tpu as pltpu
from jax.sharding import PartitionSpec as P


inv_root = 0.7071067811865476
bf16 = jnp.bfloat16
f32 = jnp.float32
GROUP = 8
NN = (((1,), (0,)), ((), ()))
NT = (((1,), (1,)), ((), ()))
TN = (((0,), (0,)), ((), ()))


def mm(left, right, dims=NN):
    return lax.dot_general(left, right, dims, preferred_element_type=f32)


def silu_slope(values):
    sigma = jax.nn.sigmoid(values)
    return sigma * (1.0 + values * (1.0 - sigma))


def offsets(count):
    return [(which // 2 + 1) * (1 - 2 * (which % 2)) for which in range(count)]


def shifted(block, axis, distance):
    devices = range(lax.axis_size(axis))
    route = [((i - distance) % len(devices), i) for i in devices]
    return lax.ppermute(block, axis, route)


def iota(shape, dim):
    return lax.broadcasted_iota(jnp.int32, shape, dim)


def one_hot(index, shape, dim):
    return jnp.where(index == iota(shape, dim), 1.0, 0.0).astype(bf16)


def vmem():
    return pl.BlockSpec(memory_space=pltpu.VMEM)


def params(**extra):
    return pltpu.CompilerParams(vmem_limit_bytes=60 * 1024 * 1024, **extra)


def send_hot(rows_ref, count_ref, which, edges):
    capacity = rows_ref.shape[2]
    rows = rows_ref[0, which : which + 1, :]
    used = iota((1, capacity), 1) < count_ref[0, which]
    return one_hot(jnp.where(used, rows, -1), (edges, capacity), 0)


def front_kernel(
    count_ref, x_ref, we_ref, wd_ref, rows_ref, pre_ref, hid_ref, pdt_ref, red_ref, *send_refs
):
    edges = x_ref.shape[1]
    step = 256
    for start in range(0, edges, step):
        pre = mm(x_ref[0, start : start + step, :], we_ref[...])
        pre_ref[start : start + step, :] = pre
        hidden = (pre * jax.nn.sigmoid(pre)).astype(bf16)
        hid_ref[start : start + step, :] = hidden
        down = lax.dot_general(
            wd_ref[...], hidden, (((0,), (1,)), ((), ())), preferred_element_type=f32
        )
        pdt_ref[:, start : start + step] = down
        red_ref[:, start : start + step] = (down * jax.nn.sigmoid(down)).astype(bf16)
    for which, send_ref in enumerate(send_refs):
        hot = send_hot(rows_ref, count_ref, which, edges)
        send_ref[...] = mm(red_ref[...], hot).astype(bf16)


def smem():
    return pl.BlockSpec(memory_space=pltpu.SMEM)


def front(messages, w_edge, w_down, rows, counts):
    _, edges, model = messages.shape
    narrow = w_down.shape[1]
    _, lists, capacity = rows.shape
    return pl.pallas_call(
        front_kernel,
        out_shape=(
            jax.ShapeDtypeStruct((edges, model), f32),
            jax.ShapeDtypeStruct((edges, model), bf16),
            jax.ShapeDtypeStruct((narrow, edges), f32),
            jax.ShapeDtypeStruct((narrow, edges), bf16),
        )
        + (jax.ShapeDtypeStruct((narrow, capacity), bf16),) * lists,
        in_specs=[smem()] + [vmem()] * 4,
        out_specs=(vmem(),) * (4 + lists),
        compiler_params=params(),
        name="front",
    )(counts, messages, w_edge, w_down, rows)


def pick_kernel(count_ref, cot_ref, rows_ref, after_ref, *send_refs):
    edges = cot_ref.shape[1]
    for which, send_ref in enumerate(send_refs):
        hot = send_hot(rows_ref, count_ref, which, edges)
        send_ref[...] = mm(hot, cot_ref[0], TN).astype(bf16)


def pick(cotangent, rows, counts, after):
    _, _, model = cotangent.shape
    _, lists, capacity = rows.shape
    return pl.pallas_call(
        pick_kernel,
        out_shape=(jax.ShapeDtypeStruct((capacity, model), bf16),) * lists,
        in_specs=[smem(), vmem(), vmem(), pl.BlockSpec(memory_space=pl.ANY)],
        out_specs=(vmem(),) * lists,
        compiler_params=params(),
        name="pick",
    )(counts, cotangent, rows, after)


def widen_weights(wb_ref, wide):
    basis, _ = wb_ref.shape
    narrow = wide.shape[1]
    padded = wide.shape[0] // narrow
    zeros = jnp.zeros((padded - basis, narrow), bf16)
    for c in range(0, narrow, 2):
        pair = wb_ref[:, c * narrow : (c + 2) * narrow]
        wide[c * padded : (c + 1) * padded, :] = jnp.concatenate(
            [pair[:, :narrow], zeros], axis=0
        )
        wide[(c + 1) * padded : (c + 2) * padded, :] = jnp.concatenate(
            [pair[:, narrow:], zeros], axis=0
        )


def split_index(trip, capacity):
    low = jnp.bitwise_and(trip, capacity - 1).astype(f32).astype(bf16)
    return low, jnp.right_shift(trip, capacity.bit_length() - 1)


def low_iota(capacity, rho):
    return iota((capacity, rho), 0).astype(f32).astype(bf16)


def low_hot(low, numbers):
    one, zero = jnp.ones((), bf16), jnp.zeros((), bf16)
    return jnp.where(low == numbers, one, zero)


def align_kernel(basis_count, sub, after_ref, basis_ref, bas_ref, slot_s):
    groups, rho, _ = slot_s.shape
    slots = rho // GROUP

    def body(index, carry):
        x = basis_ref[0, pl.ds(pl.multiple_of(index * sub, sub), sub), :].astype(f32)
        for k in range(slots):
            tile, off = divmod(k * basis_count, 128)
            if off + basis_count <= 128:
                part = x[:, tile * 128 : tile * 128 + 128]
                if off:
                    part = pltpu.roll(part, 128 - off, 1)
            else:
                part = pltpu.roll(x[:, tile * 128 : tile * 128 + 256], 256 - off, 1)[:, :128]
            for g in range(groups):
                slot_s[g, k * GROUP : (k + 1) * GROUP, :] = part[g * GROUP : (g + 1) * GROUP, :]
        for g in range(groups):
            first = pl.multiple_of((index * groups + g) * rho, rho)
            bas_ref[pl.ds(first, rho), :] = slot_s[g].astype(bf16)
        return carry

    lax.fori_loop(0, basis_ref.shape[1] // sub, body, 0)


def align(triplet_basis, basis_count, slots, after):
    _, edges, wide = triplet_basis.shape
    rho = slots * GROUP
    padded = 128
    block = 128
    sub = 64
    return pl.pallas_call(
        functools.partial(align_kernel, basis_count, sub),
        grid=(edges // block,),
        out_shape=jax.ShapeDtypeStruct((edges * slots, padded), bf16),
        in_specs=[
            pl.BlockSpec(memory_space=pl.ANY),
            pl.BlockSpec((1, block, wide), lambda i: (0, i, 0)),
        ],
        out_specs=pl.BlockSpec((block * slots, padded), lambda i: (i, 0)),
        scratch_shapes=[pltpu.VMEM((sub // GROUP, rho, padded), f32)],
        compiler_params=params(),
        cost_estimate=pl.CostEstimate(
            flops=0, transcendentals=0, bytes_accessed=edges * slots * padded * 10
        ),
        name="align",
    )(after, triplet_basis)


def forward_kernel(sub, lists, bas_ref, trip_ref, red_ref, wb_ref, *rest):
    recv_refs = rest[:lists]
    outer_ref, state_ref, pool, wide, gat_s, num_s = rest[lists:]
    narrow, edges = red_ref.shape
    capacity = recv_refs[0].shape[1]
    rho = trip_ref.shape[1]
    padded = bas_ref.shape[1]
    locals_ = edges // capacity

    @pl.when(pl.program_id(0) == 0)
    def _():
        for h in range(locals_):
            pool[h * narrow : (h + 1) * narrow, :] = red_ref[:, h * capacity : (h + 1) * capacity]
        for h in range(lists):
            pool[(locals_ + h) * narrow : (locals_ + h + 1) * narrow, :] = recv_refs[h][...]
        widen_weights(wb_ref, wide)
        num_s[...] = low_iota(capacity, rho)

    groups = sub // GROUP
    own = iota((GROUP, rho), 1) % GROUP == iota((GROUP, rho), 0)

    def body(index, carry):
        first = pl.multiple_of(index * sub, sub)
        first_group = pl.multiple_of(index * groups, groups)

        def gather(g):
            low, high = split_index(trip_ref[pl.ds(first_group + g, 1), :], capacity)
            found = mm(pool[...], low_hot(low, num_s[...]))
            gathered = jnp.zeros((narrow, rho), f32)
            for h in range(locals_ + lists):
                gathered = jnp.where(high == h, found[h * narrow : (h + 1) * narrow, :], gathered)
            gat_s[g] = gathered

        def product(g):
            spread = jnp.concatenate(
                [
                    jnp.where(own, gat_s[g, pl.ds(c, GROUP, stride=0), :], 0.0)
                    for c in range(narrow)
                ],
                axis=0,
            ).astype(bf16)
            bas = bas_ref[pl.ds(pl.multiple_of((first_group + g) * rho, rho), rho), :]
            return mm(spread, bas)

        gather(0)
        held = None
        for g in range(groups):
            if g + 1 < groups:
                gather(g + 1)
            outer = product(g)
            if g % 2 == 0:
                held = outer
                continue
            rows = pl.ds(pl.multiple_of(first + (g - 1) * GROUP, 2 * GROUP), 2 * GROUP)
            for c in range(narrow):
                part = slice(c * GROUP, (c + 1) * GROUP)
                outer_ref[rows, c * padded : (c + 1) * padded] = jnp.concatenate(
                    [held[part, :], outer[part, :]], axis=0
                ).astype(bf16)
        return carry

    lax.fori_loop(0, outer_ref.shape[0] // sub, body, 0)
    state_ref[...] = mm(outer_ref[...], wide[...]).astype(bf16)


def forward(bas, trips, red, recv, w_bil):
    narrow, edges = red.shape
    lists = len(recv)
    capacity = recv[0].shape[1]
    rho = trips.shape[1]
    padded = bas.shape[1]
    block = 256
    sub = 64
    resident = lambda *shape: pl.BlockSpec(shape, lambda i: (0,) * len(shape))
    return pl.pallas_call(
        functools.partial(forward_kernel, sub, lists),
        grid=(edges // block,),
        out_shape=(
            jax.ShapeDtypeStruct((edges, narrow * padded), bf16),
            jax.ShapeDtypeStruct((edges, narrow), bf16),
        ),
        in_specs=[
            pl.BlockSpec((block * rho // GROUP, padded), lambda i: (i, 0)),
            pl.BlockSpec((block // GROUP, rho), lambda i: (i, 0)),
            resident(narrow, edges),
            resident(*w_bil.shape),
        ]
        + [resident(narrow, capacity)] * lists,
        out_specs=(
            pl.BlockSpec((block, narrow * padded), lambda i: (i, 0)),
            pl.BlockSpec((block, narrow), lambda i: (i, 0)),
        ),
        scratch_shapes=[
            pltpu.VMEM((edges // capacity * narrow + lists * narrow, capacity), bf16),
            pltpu.VMEM((narrow * padded, narrow), bf16),
            pltpu.VMEM((sub // GROUP, narrow, rho), f32),
            pltpu.VMEM((capacity, rho), bf16),
        ],
        compiler_params=params(),
        name="forward",
    )(bas, trips, red, w_bil, *recv)


def settle(core_ref, keep_ref, give_ref, pair, part, even, odd):
    is_odd = core_ref[0, 0] == 1
    keep_ref[pair, :, part] = jnp.where(is_odd, odd, even).astype(bf16)
    give_ref[pair, :, part] = jnp.where(is_odd, even, odd).astype(bf16)


def state_kernel(
    scale, parts, lists,
    count_ref, core_ref, outer_ref, state_ref, cot_ref, rev_ref, own_ref, wu_ref, *rest
):
    recv_refs = rest[:lists]
    grad_ref, keep_ref, give_ref, ca_s, ac_s, bil_s = rest[lists:]
    block, narrow = state_ref.shape
    edges = own_ref.shape[1]
    capacity, model = recv_refs[0].shape
    columns = outer_ref.shape[1]
    pid = pl.program_id(0)

    @pl.when(pid == 0)
    def _():
        ca_s[...] = jnp.zeros_like(ca_s)
        ac_s[...] = jnp.zeros_like(ac_s)
        bil_s[...] = jnp.zeros_like(bil_s)

    state = state_ref[...]
    alive = pid * block + iota((block, 1), 0) < count_ref[0, 0]
    scaled = jnp.where(alive, cot_ref[0].astype(f32) * inv_root, 0.0)
    pre_ca = mm(state, wu_ref[0])
    grad_ca = (scaled * silu_slope(pre_ca)).astype(bf16)
    reverse = rev_ref[...]
    mirror = mm(one_hot(reverse, (edges, block), 0), own_ref[0], TN)
    for which, recv_ref in enumerate(recv_refs):
        base = edges + which * capacity
        mirror = mirror + mm(one_hot(reverse - base, (capacity, block), 0), recv_ref[...], TN)
    pre_ac = mm(state, wu_ref[1])
    grad_ac = (mirror * inv_root * silu_slope(pre_ac)).astype(bf16)
    ca_s[...] += mm(grad_ca, state, TN)
    ac_s[...] += mm(grad_ac, state, TN)
    back_rev = mm(grad_ac, wu_ref[1], NT).astype(bf16).astype(f32)
    grad_state = (mm(grad_ca, wu_ref[0], NT) + back_rev).astype(bf16)
    grad_ref[...] = grad_state
    wide_step = 1024
    for start in range(0, columns, wide_step):
        bil_s[:, start : start + wide_step] += mm(
            grad_state, outer_ref[:, start : start + wide_step], TN
        )

    @pl.when(pid == pl.num_programs(0) - 1)
    def _():
        span = columns // parts
        thin = model // parts
        both = jnp.concatenate([ca_s[...], ac_s[...]], axis=1)
        if thin < narrow:
            spare = jnp.zeros((narrow - thin, 2 * narrow), f32)
        for pair in range(parts // 2):
            even = slice(2 * pair * span, (2 * pair + 1) * span)
            odd = slice((2 * pair + 1) * span, (2 * pair + 2) * span)
            settle(core_ref, keep_ref, give_ref, pair, slice(0, span),
                   bil_s[:, even] * scale, bil_s[:, odd] * scale)
            sides = []
            for dest in (2 * pair, 2 * pair + 1):
                piece = both[dest * thin : (dest + 1) * thin, :] * scale
                if thin < narrow:
                    piece = jnp.concatenate([piece, spare], axis=0)
                sides.append(piece)
            settle(core_ref, keep_ref, give_ref, pair, slice(span, span + 2 * narrow), *sides)


def state_grads(count, core, outer, state, cotangent, rev, recv_cot, w_up, scale, parts):
    edges, narrow = state.shape
    model = cotangent.shape[2]
    columns = outer.shape[1]
    block = 256
    lists = len(recv_cot)
    share = (parts // 2, narrow, columns // parts + 2 * narrow)
    resident = lambda *shape: pl.BlockSpec(shape, lambda i: (0,) * len(shape))
    return pl.pallas_call(
        functools.partial(state_kernel, scale, parts, lists),
        grid=(edges // block,),
        out_shape=(
            jax.ShapeDtypeStruct((edges, narrow), bf16),
            jax.ShapeDtypeStruct(share, bf16),
            jax.ShapeDtypeStruct(share, bf16),
        ),
        in_specs=[
            smem(),
            smem(),
            pl.BlockSpec((block, columns), lambda i: (i, 0)),
            pl.BlockSpec((block, narrow), lambda i: (i, 0)),
            pl.BlockSpec((1, block, model), lambda i: (0, i, 0)),
            pl.BlockSpec((1, block), lambda i: (0, i)),
            resident(1, edges, model),
            resident(*w_up.shape),
        ]
        + [resident(*recv_cot[0].shape)] * lists,
        out_specs=(
            pl.BlockSpec((block, narrow), lambda i: (i, 0)),
            resident(*share),
            resident(*share),
        ),
        scratch_shapes=[
            pltpu.VMEM((model, narrow), f32),
            pltpu.VMEM((model, narrow), f32),
            pltpu.VMEM((narrow, columns), f32),
        ],
        compiler_params=params(),
        name="state_grads",
    )(count, core, outer, state, cotangent, rev, cotangent, w_up, *recv_cot)


def own_rows(mixed, narrow):
    rho = mixed.shape[1]
    value = mixed.reshape(narrow // GROUP, GROUP, GROUP, rho)
    shape = (1, 1, GROUP, rho)
    row, lane = iota(shape, 2), iota(shape, 3)
    step = GROUP // 2
    while step:
        low, high = value[:, :step], value[:, step:]
        upper = jnp.bitwise_and(row, step) > 0
        kept = jnp.bitwise_and(row, step) == jnp.bitwise_and(lane, step)
        straight = jnp.where(upper, high, low)
        other = jnp.where(upper, low, high)
        moved = pltpu.roll(other, step, 2)
        if 2 * step != GROUP:
            moved = jnp.where(upper, moved, pltpu.roll(other, GROUP - step, 2))
        value = jnp.where(kept, straight, moved)
        step //= 2
    return value.reshape(narrow, rho)


def backward_kernel(sub, lists, bas_ref, grad_ref, trip_ref, wb_ref, home_ref, *rest):
    back_refs = rest[:lists]
    pool_s, wide, turn_s, cast_s, hot_s, num_s = rest[lists:]
    block, narrow = grad_ref.shape
    padded = bas_ref.shape[1]
    rho = trip_ref.shape[1]
    rows, capacity = pool_s.shape
    pid = pl.program_id(0)

    @pl.when(pid == 0)
    def _():
        widen_weights(wb_ref, wide)
        pool_s[...] = jnp.zeros_like(pool_s)
        num_s[...] = low_iota(capacity, rho)

    grad_state = grad_ref[...]
    height = narrow * GROUP

    def spread(pair, carry):
        start = pl.multiple_of(pair * 2 * padded, 2 * padded)
        grad = mm(grad_state, wide[pl.ds(start, 2 * padded), :], NT)
        for g in range(block // GROUP):
            for side in range(2):
                at = pl.multiple_of(g * height + pair * 2 * GROUP + side * GROUP, GROUP)
                turn_s[pl.ds(at, GROUP), :] = grad[
                    g * GROUP : (g + 1) * GROUP, side * padded : (side + 1) * padded
                ]
        return carry

    lax.fori_loop(0, narrow // 2, spread, 0, unroll=4)
    groups = sub // GROUP

    def body(index, carry):
        first_group = pl.multiple_of(index * groups, groups)

        def mix(g):
            here = first_group + g
            bas = bas_ref[pl.ds(pl.multiple_of(here * rho, rho), rho), :]
            grads = turn_s[pl.ds(pl.multiple_of(here * height, height), height), :]
            return mm(grads.astype(bf16), bas, NT)

        def cast(g, mixed):
            trip_grad = own_rows(mixed, narrow).astype(bf16)
            low, high = split_index(trip_ref[pl.ds(first_group + g, 1), :], capacity)
            part = slice(g * rho, (g + 1) * rho)
            hot_s[:, part] = low_hot(low, num_s[...])
            zero = jnp.zeros_like(trip_grad)
            wide_high = jnp.broadcast_to(high.astype(f32).astype(bf16), trip_grad.shape)
            for h in range(rows // narrow):
                cast_s[h * narrow : (h + 1) * narrow, part] = jnp.where(
                    wide_high == jnp.asarray(h, bf16), trip_grad, zero
                )

        ready = mix(0)
        for g in range(groups):
            mixed = ready
            if g + 1 < groups:
                ready = mix(g + 1)
            cast(g, mixed)
        pool_s[...] += mm(cast_s[...], hot_s[...], NT)
        return carry

    lax.fori_loop(0, block // sub, body, 0)

    @pl.when(pid == pl.num_programs(0) - 1)
    def _():
        home = home_ref.shape[0]
        home_ref[...] = pool_s[:home, :]
        for which, back_ref in enumerate(back_refs):
            first = home + which * narrow
            back_ref[...] = pool_s[first : first + narrow, :].astype(bf16)


def backward(bas, grad_state, trips, w_bil, capacity, lists):
    edges, narrow = grad_state.shape
    rho = trips.shape[1]
    padded = bas.shape[1]
    block = 256
    sub = 64
    home = edges // capacity * narrow
    rows = home + lists * narrow
    resident = lambda *shape: pl.BlockSpec(shape, lambda i: (0,) * len(shape))
    return pl.pallas_call(
        functools.partial(backward_kernel, sub, lists),
        grid=(edges // block,),
        out_shape=(jax.ShapeDtypeStruct((home, capacity), f32),)
        + (jax.ShapeDtypeStruct((narrow, capacity), bf16),) * lists,
        in_specs=[
            pl.BlockSpec((block * rho // GROUP, padded), lambda i: (i, 0)),
            pl.BlockSpec((block, narrow), lambda i: (i, 0)),
            pl.BlockSpec((block // GROUP, rho), lambda i: (i, 0)),
            resident(*w_bil.shape),
        ],
        out_specs=(resident(home, capacity),) + (resident(narrow, capacity),) * lists,
        scratch_shapes=[
            pltpu.VMEM((rows, capacity), f32),
            pltpu.VMEM((narrow * padded, narrow), bf16),
            pltpu.VMEM((block * narrow, padded), f32),
            pltpu.VMEM((rows, sub // GROUP * rho), bf16),
            pltpu.VMEM((capacity, sub // GROUP * rho), bf16),
            pltpu.VMEM((capacity, rho), bf16),
        ],
        compiler_params=params(),
        name="backward",
    )(bas, grad_state, trips, w_bil)


def tail_kernel(
    scale, parts, lists,
    count_ref, core_ref, pool_ref, rows_ref, pdt_ref, pre_ref, hid_ref, x_ref, we_ref, wd_ref, *rest
):
    back_refs = rest[:lists]
    out_ref, keep_ref, give_ref, grad_s = rest[lists:]
    narrow, edges = pdt_ref.shape
    capacity = back_refs[0].shape[1]
    model = pre_ref.shape[1]
    grad = jnp.concatenate(
        [pool_ref[h * narrow : (h + 1) * narrow, :] for h in range(edges // capacity)], axis=1
    )
    for which, back_ref in enumerate(back_refs):
        grad = grad + mm(back_ref[...], send_hot(rows_ref, count_ref, which, edges), NT)
    grad_down = (grad * silu_slope(pdt_ref[...])).astype(bf16)
    step = 256
    for start in range(0, edges, step):
        part = slice(start, start + step)
        grad_hidden = lax.dot_general(
            grad_down[:, part], wd_ref[...], (((0,), (1,)), ((), ())), preferred_element_type=f32
        )
        grad_edge = (grad_hidden * silu_slope(pre_ref[part, :])).astype(bf16)
        grad_s[part, :] = grad_edge
        out_ref[0, part, :] = mm(grad_edge, we_ref[...], NT).astype(bf16)
    down = lax.dot_general(
        hid_ref[...], grad_down, (((0,), (1,)), ((), ())), preferred_element_type=f32
    )
    down = jnp.concatenate([down, jnp.zeros_like(down)], axis=1)
    span = model // parts
    for start in range(0, model, step):
        edge = mm(x_ref[0, :, start : start + step], grad_s[...], TN)
        both = jnp.concatenate([edge, down[start : start + step, :]], axis=1) * scale
        for first in range(0, step, 2 * span):
            settle(
                core_ref, keep_ref, give_ref, (start + first) // (2 * span), slice(None),
                both[first : first + span, :], both[first + span : first + 2 * span, :],
            )


def tail(pool, back, rows, counts, core, pdt, pre, hidden, messages, w_edge, w_down, scale, parts):
    _, edges, model = messages.shape
    narrow = w_down.shape[1]
    share = jax.ShapeDtypeStruct((parts // 2, model // parts, model + 2 * narrow), bf16)
    return pl.pallas_call(
        functools.partial(tail_kernel, scale, parts, len(back)),
        out_shape=(
            jax.ShapeDtypeStruct((1, edges, model), bf16),
            share,
            share,
        ),
        in_specs=[smem(), smem()] + [vmem()] * (8 + len(back)),
        out_specs=(vmem(),) * 3,
        scratch_shapes=[pltpu.VMEM((edges, model), bf16)],
        compiler_params=params(),
        name="tail",
    )(counts, core, pool, rows, pdt, pre, hidden, messages, w_edge, w_down, *back)


def add_pair_kernel(chip_ref, keep_ref, got_ref, mine_ref, *out_refs):
    chips = keep_ref.shape[0]
    chip = chip_ref[0, 0]
    for step, out_ref in enumerate((mine_ref,) + out_refs):
        at = lax.rem(chip + step, chips)
        out_ref[...] = (keep_ref[at].astype(f32) + got_ref[at].astype(f32)).astype(bf16)


def add_kernel(*refs):
    *in_refs, out_ref = refs
    total = in_refs[0][...].astype(f32)
    for in_ref in in_refs[1:]:
        total = total + in_ref[...].astype(f32)
    out_ref[...] = total.astype(bf16)


def over_graph(keep, give, chip):
    chips, height, wide = keep.shape
    devices = 2 * chips
    piece = jax.ShapeDtypeStruct((height, wide), bf16)
    got = lax.ppermute(give, "graph", [(i, i ^ 1) for i in range(devices)])
    mine, *sends = pl.pallas_call(
        add_pair_kernel,
        out_shape=(piece,) * chips,
        in_specs=[smem(), vmem(), vmem()],
        out_specs=(vmem(),) * chips,
        compiler_params=params(),
    )(chip, keep, got)
    arrived = []
    for step, send in enumerate(sends):
        route = [(i, (i + 2 * (step + 1)) % devices) for i in range(devices)]
        arrived.append(lax.ppermute(send, "graph", route))
    return pl.pallas_call(
        add_kernel,
        out_shape=piece,
        in_specs=[vmem()] * chips,
        out_specs=vmem(),
        compiler_params=params(),
    )(mine, *arrived)


def over_dp(share):
    slabs = lax.axis_size("dp")
    copies = [share]
    for step in range(1, slabs):
        copies.append(lax.ppermute(share, "dp", [(i, i ^ step) for i in range(slabs)]))
    return copies


def paired_sum(values):
    while len(values) > 1:
        values = [values[i] + values[i + 1] for i in range(0, len(values), 2)]
    return values[0]


def finish_kernel(slabs, *refs):
    early_refs, late_refs = refs[:slabs], refs[slabs : 2 * slabs]
    edge_ref, down_ref, bil_ref, up_ref = refs[2 * slabs :]
    rows, model = edge_ref.shape
    basis = bil_ref.shape[0]
    _, narrow, _ = up_ref.shape
    padded = 128
    span = bil_ref.shape[1] // narrow * padded

    def total(in_refs, *part):
        return paired_sum([in_ref[part].astype(f32) for in_ref in in_refs])

    every = slice(None)
    for c in range(bil_ref.shape[1] // narrow):
        block = total(early_refs, every, slice(c * padded, (c + 1) * padded))
        bil_ref[:, c * narrow : (c + 1) * narrow] = block.T[:basis, :]
    both = total(early_refs, slice(0, rows), slice(span, span + 2 * narrow)).T
    up_ref[0] = both[:narrow, :]
    up_ref[1] = both[narrow:, :]
    edge_ref[...] = total(late_refs, every, slice(0, model))
    down_ref[...] = total(late_refs, every, slice(model, model + 2 * narrow))[:, :narrow]


def finish(early, late, basis, narrow, model, parts):
    rows = model // parts
    return pl.pallas_call(
        functools.partial(finish_kernel, len(early)),
        out_shape=(
            jax.ShapeDtypeStruct((rows, model), f32),
            jax.ShapeDtypeStruct((rows, narrow), f32),
            jax.ShapeDtypeStruct((basis, narrow * narrow // parts), f32),
            jax.ShapeDtypeStruct((2, narrow, rows), f32),
        ),
        in_specs=[vmem()] * (len(early) + len(late)),
        out_specs=(vmem(),) * 4,
        compiler_params=params(),
        name="finish",
    )(*early, *late)


def body(
    messages,
    cotangent,
    triplet_basis,
    w_edge,
    w_down,
    w_bil,
    w_up,
    trip_src,
    send_rows,
    send_count,
    rev_src,
    edge_count,
):
    _, edges, model = messages.shape
    narrow = w_down.shape[1]
    slots = trip_src.shape[2]
    _, lists, capacity = send_rows.shape
    basis_count = w_bil.shape[0]
    parts = lax.axis_size("graph")
    scale = 1.0 / math.sqrt(lax.axis_size("dp") * parts * edges)
    shifts = offsets(lists)
    place = lax.axis_index("graph").reshape(1, 1)
    core, chip = place % 2, place // 2
    trips = (
        trip_src[0]
        .reshape(edges // GROUP, GROUP, slots)
        .transpose(0, 2, 1)
        .reshape(edges // GROUP, GROUP * slots)
    )

    def exchange(blocks, sign):
        moved = []
        for which in range(lists):
            moved.append(shifted(blocks[which], "graph", sign * shifts[which]))
        return moved

    pre, hidden, pdt, red, *send_red = front(messages, w_edge, w_down, send_rows, send_count)
    recv_red = exchange(send_red, 1)
    send_cot = pick(cotangent, send_rows, send_count, red)
    recv_cot = exchange(send_cot, 1)
    bas = align(triplet_basis, basis_count, slots, send_cot[0])
    outer, state = forward(bas, trips, red, recv_red, w_bil)
    grad_state, keep, give = state_grads(
        edge_count, core, outer, state, cotangent, rev_src, recv_cot, w_up, scale, parts
    )
    early = over_graph(keep, give, chip)
    home, *returned = backward(bas, grad_state, trips, w_bil, capacity, lists)
    back = exchange(returned, -1)
    early = over_dp(early)
    grad_messages, keep, give = tail(
        home, back, send_rows, send_count, core, pdt, pre, hidden, messages, w_edge, w_down,
        scale, parts,
    )
    late = over_dp(over_graph(keep, give, chip))
    edge_out, down_out, bil_out, up_out = finish(early, late, basis_count, narrow, model, parts)
    return (grad_messages, edge_out, down_out, bil_out, up_out)


def solution(mesh):
    return jax.shard_map(
        body,
        mesh=mesh,
        in_specs=(
            P("dp", "graph", None),
            P("dp", "graph", None),
            P("dp", "graph", None),
            P(),
            P(),
            P(),
            P(),
            P("dp", "graph", None),
            P("dp", "graph", None),
            P("dp", "graph"),
            P("dp", "graph"),
            P("dp", "graph"),
        ),
        out_specs=(
            P("dp", "graph", None),
            P("graph", None),
            P("graph", None),
            P(None, "graph"),
            P(None, None, "graph"),
        ),
        check_vma=False,
    )
```

time: 281 us -> 206 us (0.73)
  blocking collectives: 65.3 us -> 0 us
  Pallas kernels: 167 us -> 117 us
  waiting for transfers between devices: 26.3 us -> 47.9 us
  starting transfers between devices: 15 us -> 29 us
  local copies, waits for them, and re-layouts: 5.8 us -> 10.2 us
    all_to_all x3 -> x0, blocking collectives: 65.3 us -> none  [the longest x1 32.8 us: body(): early = lax.all_to_all(early, ('dp', 'graph'), 0, 0)]
    pallas_call x1, Pallas kernels: 67.9 us -> 37.1 us  [backward(): pl.pallas_call(functools.partial(backward_kernel, sub, lists), grid=(edge...]
    ppermute x0 -> x14, waiting for transfers between devices: none -> 20.2 us  [the longest x6 12.5 us: over_graph(): arrived.append(lax.ppermute(send, 'graph', route))]
    pallas_call x3 -> x7, Pallas kernels: 69.8 us -> 50.7 us  [the longest x1 30.7 us: forward(): pl.pallas_call(functools.partial(forward_kernel, sub, lists), grid=(edges...]
    ppermute x0 -> x14, starting transfers between devices: none -> 18 us  [the longest x6 8.77 us: over_graph(): arrived.append(lax.ppermute(send, 'graph', route))]
    unnamed x28 -> x54, local copies, waits for them, and re-layouts: 4.83 us -> 9.18 us
    ppermute x12, starting transfers between devices: 15 us -> 10.9 us  [shifted(): return lax.ppermute(block, axis, route)]
  transfers between devices with their start and end apart: 12 -> 26, of which waited for: 5 -> 8; matrix products, arithmetic and copies ran while one was open for 1% -> 1% of each run, Pallas kernels for 23% -> 45%
where the time goes in v2:
time: 206 us
  Pallas kernels  117 us (57%)
  waiting for transfers between devices  47.9 us (23%)
  starting transfers between devices  29 us (14%)
  local copies, waits for them, and re-layouts  10.2 us (5%)
    pallas_call x1, Pallas kernels, backward(): pl.pallas_call(functools.partial(backward_kernel, sub, lists), grid=(edge...  37.1 us
    pallas_call x1, Pallas kernels, forward(): pl.pallas_call(functools.partial(forward_kernel, sub, lists), grid=(edges...  30.7 us
    ppermute x12, waiting for transfers between devices, shifted(): return lax.ppermute(block, axis, route)  27.7 us
    pallas_call x1, Pallas kernels, state_grads(): pl.pallas_call(functools.partial(state_kernel, scale, parts, lists), grid...  15.3 us
    ppermute x6, waiting for transfers between devices, over_graph(): arrived.append(lax.ppermute(send, 'graph', route))  12.5 us
    ppermute x12, starting transfers between devices, shifted(): return lax.ppermute(block, axis, route)  10.9 us
    pallas_call x1, Pallas kernels, align(): pl.pallas_call(functools.partial(align_kernel, basis_count, sub), grid=(e...  10.2 us
    unnamed x54, local copies, waits for them, and re-layouts  9.18 us
  transfers between devices with their start and end apart: 26, of which 8 were waited for; matrix products, arithmetic and copies ran while one was open for 1% of the time, Pallas kernels for 45%

profile of v2, /device:TPU:0, one launch (start us, length us, event | category | flops | bytes accessed | tf_op | source)
XLA Modules:
  0.0 205.7 jit_solution(17070993972679164471)
XLA Ops:
  0.6 1.6 copy.20.wd_ref
  2.2 4.5 %front.1 = (f32[1024,512]{1,0:T(8,128)}, bf16[1024,512]{1,0:T(8,128)(2,1)}, f32[64,1024]{1,0:T(8,128)}, bf16[64,1024]{1,0:T(8,128)(2,1)}, bf16[64,256]{1,0:T(8,1...) custom-call(s32[1,4]{1,0:T(1,128)} %count_ref.6, ...), custom_call_target="tpu_custom_call" | custom-call | tf_op jit(solution)/shard_map/front/pallas_call | solution.py:91
  6.7 3.2 %pick.1 = (bf16[256,512]{1,0:T(8,128)(2,1)}, bf16[256,512]{1,0:T(8,128)(2,1)}, bf16[256,512]{1,0:T(8,128)(2,1)}, bf16[256,512]{1,0:T(8,128)(2,1)}) custom-call(s32[1,4]{1,0:T(1,128)} %count_ref.6, bf16[1,1024,512]{2,1,0:T(8,128)(2,1)} %own_ref.1, s32[1,4,256]{2,1,0:T(4,128)} %rows_ref.5, bf16[64,1024]{1,0:T(8,128)(2,1)} %get-tuple-element.42.after_ref.red_ref), custom_call_target="tpu_custom_call" | custom-call | tf_op jit(solution)/shard_map/pick/pallas_call | solution.py:117
  9.9 4.5 %collective-permute-start.5 = (bf16[256,512]{1,0:T(8,128)(2,1)}, bf16[256,512]{1,0:T(8,128)(2,1)S(1)}, u32[]{:S(2)}, u32[]{:S(2)}) collective-permute-start(bf16[256,512]{1,0:T(8,128)(2,1)} %get-tuple-element.50), channel_id=1, source_target_pairs={{1,0},{2,1},{3,2},{4,3},{5,4},{6,5},{7,6},{0,7},{9,8},{10,9},{11,1... | collective-permute-start | bytes 786440 | tf_op jit(solution)/shard_map/ppermute | solution.py:37
  14.5 3.8 %collective-permute-start.7 = (bf16[256,512]{1,0:T(8,128)(2,1)}, bf16[256,512]{1,0:T(8,128)(2,1)S(1)}, u32[]{:S(2)}, u32[]{:S(2)}) collective-permute-start(bf16[256,512]{1,0:T(8,128)(2,1)} %get-tuple-element.52), channel_id=1, source_target_pairs={{2,0},{3,1},{4,2},{5,3},{6,4},{7,5},{0,6},{1,7},{10,8},{11,9},{12,... | collective-permute-start | bytes 786440 | tf_op jit(solution)/shard_map/ppermute | solution.py:37
  18.3 15.5 %collective-permute-done.rest_0_ = bf16[64,256]{1,0:T(8,128)(2,1)S(1)} collective-permute-done((bf16[64,256]{1,0:T(8,128)(2,1)}, bf16[64,256]{1,0:T(8,128)(2,1)S(1)}, u32[]{:S(2)}, u32[]{:S(2)}) %collective-permute-start) | collective-permute-done | bytes 32800 | tf_op jit(solution)/shard_map/ppermute | solution.py:37
  33.8 1.9 collective-permute-done.1.rest_1_
  35.7 5.9 %collective-permute-done.2.rest_2_ = bf16[64,256]{1,0:T(8,128)(2,1)S(1)} collective-permute-done((bf16[64,256]{1,0:T(8,128)(2,1)}, bf16[64,256]{1,0:T(8,128)(2,1)S(1)}, u32[]{:S(2)}, u32[]{:S(2)}) %collective-permute-start.2) | collective-permute-done | bytes 32800 | tf_op jit(solution)/shard_map/ppermute | solution.py:37
  42.3 1.1 copy.21
  43.6 0.8 copy.23.trip_ref
  44.4 10.2 %align.1.bas_ref = bf16[32768,128]{1,0:T(8,128)(2,1)} custom-call(bf16[256,512]{1,0:T(8,128)(2,1)} %get-tuple-element.43.after_ref, bf16[1,1024,3584]{2,1,0:T(8,128)(2,1)} %basis_ref.1), custom_call_target="tpu_custom_call" | custom-call | bytes 41943040 | tf_op jit(solution)/shard_map/align/pallas_call | solution.py:186
  54.6 0.6 copy-done.21
  55.2 30.7 %forward.1 = (bf16[1024,8192]{1,0:T(8,128)(2,1)}, bf16[1024,64]{1,0:T(8,128)(2,1)}) custom-call(bf16[32768,128]{1,0:T(8,128)(2,1)} %align.1.bas_ref, s32[128,256]{1,0:T(8,128)} %copy.23.trip_ref, bf16[64,1024]{1,0:T(8,128)(2,1)} %get-tuple-element.42.after_ref.red_ref, bf16[112,4096]{1,0:T(8,128)(2,1)} %wb_ref.3, bf16[64,256]{1,0:T(8,128)(2,1)} %copy-done.18, ...), custom_call_target="tpu_custom_call" | custom-call | tf_op jit(solution)/shard_map/forward/pallas_call | solution.py:278
  86.0 0.6 copy-done.2
  86.9 15.3 %state_grads.1 = (bf16[1024,64]{1,0:T(8,128)(2,1)}, bf16[4,64,1152]{2,1,0:T(8,128)(2,1)}, bf16[4,64,1152]{2,1,0:T(8,128)(2,1)}) custom-call(s32[1,1]{1,0:T(1,128)S(6)} %copy.26.count_ref, s32[1,1]{1,0:T(1,128)S(6)} %select_n.12.core_ref, bf16[1024,8192]{1,0:T(8,128)(2,1)} %get-tuple-element.48.outer_ref, bf16[1024,64]{1,0:T(8,128)(2,1)} %get-tuple-element.49.state_ref, ...), custom_call_target="tpu_custom_call" | custom-call | tf_op jit(solution)/shard_map/state_grads/pallas_call | solution.py:383
  102.2 0.7 collective-permute-start.12
  102.9 37.1 %backward.1 = (f32[256,256]{1,0:T(8,128)}, bf16[64,256]{1,0:T(8,128)(2,1)}, bf16[64,256]{1,0:T(8,128)(2,1)}, bf16[64,256]{1,0:T(8,128)(2,1)}, bf16[64,256]{1,0:T(8,128)(2,1)}) custom-call(bf16[32768,128]{1,0:T(8,128)(2,1)} %align.1.bas_ref, bf16[1024,64]{1,0:T(8,128)(2,1)} %get-tuple-element.53.grad_ref, s32[128,256]{1,0:T(8,128)} %copy.23.trip_ref, ...), custom_call_target="tpu_custom_call" | custom-call | tf_op jit(solution)/shard_map/backward/pallas_call | solution.py:519
  140.1 0.5 collective-permute-start.9
  140.6 0.3 collective-permute-start.10
  140.8 1.7 collective-permute-start.11
  142.6 2.9 %collective-permute-done.9.rest_1_ = bf16[64,256]{1,0:T(8,128)(2,1)S(1)} collective-permute-done((bf16[64,256]{1,0:T(8,128)(2,1)}, bf16[64,256]{1,0:T(8,128)(2,1)S(1)}, u32[]{:S(2)}, u32[]{:S(2)}) %collective-permute-start.9) | collective-permute-done | bytes 32800 | tf_op jit(solution)/shard_map/ppermute | solution.py:37
  145.5 1.4 collective-permute-done.11.rest_3_
  146.9 0.6 copy-done.25
  147.5 6.3 %tail.1 = (bf16[1,1024,512]{2,1,0:T(8,128)(2,1)}, bf16[4,64,640]{2,1,0:T(8,128)(2,1)}, bf16[4,64,640]{2,1,0:T(8,128)(2,1)}) custom-call(s32[1,4]{1,0:T(1,128)} %count_ref.6, s32[1,1]{1,0:T(1,128)S(6)} %select_n.12.core_ref, f32[256,256]{1,0:T(8,128)} %get-tuple-element.54.pool_ref, s32[1,4,256]{2,1,0:T(4,128)} %rows_ref.5, ...), custom_call_target="tpu_custom_call" | custom-call | tf_op jit(solution)/shard_map/tail/pallas_call | solution.py:587
  153.9 1.6 collective-permute-start.19
  155.5 1.5 collective-permute-done.19.got_ref
  156.9 0.7 copy-done.1
  157.7 1.8 shard_map.157
  159.5 0.8 copy-done
  160.3 2.1 %shard_map.155 = (bf16[64,1152]{1,0:T(8,128)(2,1)}, bf16[64,1152]{1,0:T(8,128)(2,1)}, bf16[64,1152]{1,0:T(8,128)(2,1)}, bf16[64,1152]{1,0:T(8,128)(2,1)}) custom-call(s32[1,1]{1,0:T(1,128)S(6)} %select_n.13.chip_ref, bf16[4,64,1152]{2,1,0:T(8,128)(2,1)} %get-tuple-element.63.keep_ref, bf16[4,64,1152]{2,1,0:T(8,128)(2,1)} %copy-done), custom_call_target="tpu_custom_call" | custom-call | tf_op jit(solution)/shard_map/pallas_call | solution.py:623
  162.6 4.2 %collective-permute-start.14 = (bf16[64,1152]{1,0:T(8,128)(2,1)}, bf16[64,1152]{1,0:T(8,128)(2,1)S(1)}, u32[]{:S(2)}, u32[]{:S(2)}) collective-permute-start(bf16[64,1152]{1,0:T(8,128)(2,1)} %get-tuple-element.67), channel_id=1, source_target_pairs={{0,4},{1,5},{2,6},{3,7},{4,0},{5,1},{6,2},{7,3},{8,12},{9,13},{10,... | collective-permute-start | bytes 442376 | tf_op jit(solution)/shard_map/ppermute | solution.py:633
  166.8 1.5 collective-permute-start.21
  168.3 2.9 %collective-permute-start.22 = (bf16[64,640]{1,0:T(8,128)(2,1)}, bf16[64,640]{1,0:T(8,128)(2,1)S(1)}, u32[]{:S(2)}, u32[]{:S(2)}) collective-permute-start(bf16[64,640]{1,0:T(8,128)(2,1)} %get-tuple-element.74), channel_id=1, source_target_pairs={{0,6},{1,7},{2,0},{3,1},{4,2},{5,3},{6,4},{7,5},{8,14},{9,15},{10,... | collective-permute-start | bytes 245768 | tf_op jit(solution)/shard_map/ppermute | solution.py:633
  171.2 12.5 %collective-permute-done.21.refs_2_ = bf16[64,640]{1,0:T(8,128)(2,1)S(1)} collective-permute-done((bf16[64,640]{1,0:T(8,128)(2,1)}, bf16[64,640]{1,0:T(8,128)(2,1)S(1)}, u32[]{:S(2)}, u32[]{:S(2)}) %collective-permute-start.21) | collective-permute-done | bytes 81952 | tf_op jit(solution)/shard_map/ppermute | solution.py:633
  183.7 0.6 copy-done.16
  184.3 1.7 shard_map.158.refs_4_
  186.0 2.4 %collective-permute-start.25 = (bf16[64,640]{1,0:T(8,128)(2,1)}, bf16[64,640]{1,0:T(8,128)(2,1)S(1)}, u32[]{:S(2)}, u32[]{:S(2)}) collective-permute-start(bf16[64,640]{1,0:T(8,128)(2,1)} %shard_map.158.refs_4_), channel_id=1, source_target_pairs={{0,24},{8,16},{16,8},{24,0},{1,25},{9,17},{17,9},{25,1},{2,26},{10... | collective-permute-start | bytes 245768 | tf_op jit(solution)/shard_map/ppermute | solution.py:647
  188.5 0.6 copy-done.9
  189.2 1.9 shard_map.156.refs_0_
  191.1 0.5 collective-permute-start.18
  191.6 1.5 collective-permute-start.17
  193.1 1.5 collective-permute-start.16
  194.6 0.5 collective-permute-start.24
  195.1 0.5 collective-permute-start.23
  195.6 6.2 %collective-permute-done.24.refs_6_ = bf16[64,640]{1,0:T(8,128)(2,1)S(1)} collective-permute-done((bf16[64,640]{1,0:T(8,128)(2,1)}, bf16[64,640]{1,0:T(8,128)(2,1)S(1)}, u32[]{:S(2)}, u32[]{:S(2)}) %collective-permute-start.24) | collective-permute-done | bytes 81952 | tf_op jit(solution)/shard_map/ppermute | solution.py:647
  201.9 0.6 copy-done.13
  202.6 0.7 copy-done.8
  203.3 2.4 %finish.1 = (f32[64,512]{1,0:T(8,128)}, f32[64,64]{1,0:T(8,128)}, f32[112,512]{1,0:T(8,128)}, f32[2,64,64]{2,1,0:T(8,128)}) custom-call(bf16[64,1152]{1,0:T(8,128)(2,1)} %shard_map.156.refs_0_, bf16[64,1152]{1,0:T(8,128)(2,1)} %copy-done.8, bf16[64,1152]{1,0:T(8,128)(2,1)} %copy-done.7, bf16[64,1152]{1,0:T(8,128)(2,1)} %copy-done.6, ...), custom_call_target="tpu_custom_call" | custom-call | tf_op jit(solution)/shard_map/finish/pallas_call | solution.py:682
  (72 shorter events, 1.2 us)
Async XLA Ops:
  9.9 76.0 %collective-permute-start.5 = (bf16[256,512]{1,0:T(8,128)(2,1)}, bf16[256,512]{1,0:T(8,128)(2,1)S(1)}, u32[]{:S(2)}, u32[]{:S(2)}) collective-permute-start(bf16[256,512]{1,0:T(8,128)(2,1)} %get-tuple-element.50), channel_id=1, source_target_pairs={{1,0},{2,1},{3,2},{4,3},{5,4},{6,5},{7,6},{0,7},{9,8},{10,9},{11,1... | collective-permute-start | bytes 786440 | tf_op jit(solution)/shard_map/ppermute | solution.py:37
  14.5 71.5 %collective-permute-start.6 = (bf16[256,512]{1,0:T(8,128)(2,1)}, bf16[256,512]{1,0:T(8,128)(2,1)S(1)}, u32[]{:S(2)}, u32[]{:S(2)}) collective-permute-start(bf16[256,512]{1,0:T(8,128)(2,1)} %get-tuple-element.51), channel_id=1, source_target_pairs={{6,0},{7,1},{0,2},{1,3},{2,4},{3,5},{4,6},{5,7},{14,8},{15,9},{8,1... | collective-permute-start | bytes 786440 | tf_op jit(solution)/shard_map/ppermute | solution.py:37
  14.5 71.5 %collective-permute-start.7 = (bf16[256,512]{1,0:T(8,128)(2,1)}, bf16[256,512]{1,0:T(8,128)(2,1)S(1)}, u32[]{:S(2)}, u32[]{:S(2)}) collective-permute-start(bf16[256,512]{1,0:T(8,128)(2,1)} %get-tuple-element.52), channel_id=1, source_target_pairs={{2,0},{3,1},{4,2},{5,3},{6,4},{7,5},{0,6},{1,7},{10,8},{11,9},{12,... | collective-permute-start | bytes 786440 | tf_op jit(solution)/shard_map/ppermute | solution.py:37
  18.3 67.7 %collective-permute-start.4 = (bf16[256,512]{1,0:T(8,128)(2,1)}, bf16[256,512]{1,0:T(8,128)(2,1)S(1)}, u32[]{:S(2)}, u32[]{:S(2)}) collective-permute-start(bf16[256,512]{1,0:T(8,128)(2,1)} %get-tuple-element.43.after_ref), channel_id=1, source_target_pairs={{7,0},{0,1},{1,2},{2,3},{3,4},{4,5},{5,6},{6,7},{15,8},{8,9},{9,10... | collective-permute-start | bytes 786440 | tf_op jit(solution)/shard_map/ppermute | solution.py:37
  18.3 15.5 %collective-permute-start = (bf16[64,256]{1,0:T(8,128)(2,1)}, bf16[64,256]{1,0:T(8,128)(2,1)S(1)}, u32[]{:S(2)}, u32[]{:S(2)}) collective-permute-start(bf16[64,256]{1,0:T(8,128)(2,1)} %get-tuple-element.44), channel_id=1, source_target_pairs={{7,0},{0,1},{1,2},{2,3},{3,4},{4,5},{5,6},{6,7},{15,8},{8,9},{9,10... | collective-permute-start | bytes 98312 | tf_op jit(solution)/shard_map/ppermute | solution.py:37
  33.8 20.8 %copy-start.18 = (bf16[64,256]{1,0:T(8,128)(2,1)}, bf16[64,256]{1,0:T(8,128)(2,1)S(1)}, u32[]{:S(2)}) copy-start(bf16[64,256]{1,0:T(8,128)(2,1)S(1)} %collective-permute-done.rest_0_) | copy-start | bytes 98308
  33.8 1.9 collective-permute-start.1
  35.7 18.9 %copy-start.19 = (bf16[64,256]{1,0:T(8,128)(2,1)}, bf16[64,256]{1,0:T(8,128)(2,1)S(1)}, u32[]{:S(2)}) copy-start(bf16[64,256]{1,0:T(8,128)(2,1)S(1)} %collective-permute-done.1.rest_1_) | copy-start | bytes 98308
  35.7 5.9 %collective-permute-start.2 = (bf16[64,256]{1,0:T(8,128)(2,1)}, bf16[64,256]{1,0:T(8,128)(2,1)S(1)}, u32[]{:S(2)}, u32[]{:S(2)}) collective-permute-start(bf16[64,256]{1,0:T(8,128)(2,1)} %get-tuple-element.46), channel_id=1, source_target_pairs={{6,0},{7,1},{0,2},{1,3},{2,4},{3,5},{4,6},{5,7},{14,8},{15,9},{8,1... | collective-permute-start | bytes 98312 | tf_op jit(solution)/shard_map/ppermute | solution.py:37
  41.6 13.0 %copy-start.20 = (bf16[64,256]{1,0:T(8,128)(2,1)}, bf16[64,256]{1,0:T(8,128)(2,1)S(1)}, u32[]{:S(2)}) copy-start(bf16[64,256]{1,0:T(8,128)(2,1)S(1)} %collective-permute-done.2.rest_2_) | copy-start | bytes 98308
  41.6 13.0 %collective-permute-start.3 = (bf16[64,256]{1,0:T(8,128)(2,1)}, bf16[64,256]{1,0:T(8,128)(2,1)S(1)}, u32[]{:S(2)}, u32[]{:S(2)}) collective-permute-start(bf16[64,256]{1,0:T(8,128)(2,1)} %get-tuple-element.47), channel_id=1, source_target_pairs={{2,0},{3,1},{4,2},{5,3},{6,4},{7,5},{0,6},{1,7},{10,8},{11,9},{12,... | collective-permute-start | bytes 98312 | tf_op jit(solution)/shard_map/ppermute | solution.py:37
  85.9 0.7 copy-start.2
  86.0 0.8 copy-start.3
  86.0 0.9 copy-start.4
  86.0 0.9 copy-start.5
  102.2 57.2 %collective-permute-start.12 = (bf16[4,64,1152]{2,1,0:T(8,128)(2,1)}, bf16[4,64,1152]{2,1,0:T(8,128)(2,1)S(1)}, u32[]{:S(2)}, u32[]{:S(2)}) collective-permute-start(bf16[4,64,1152]{2,1,0:T(8,128)(2,1)} %get-tuple-element.64), channel_id=1, source_target_pairs={{0,1},{1,0},{2,3},{3,2},{4,5},{5,4},{6,7},{7,6},{8,9},{9,8},{10,11... | collective-permute-start | bytes 1769480 | tf_op jit(solution)/shard_map/ppermute | solution.py:622
  140.0 2.6 %collective-permute-start.8 = (bf16[64,256]{1,0:T(8,128)(2,1)}, bf16[64,256]{1,0:T(8,128)(2,1)S(1)}, u32[]{:S(2)}, u32[]{:S(2)}) collective-permute-start(bf16[64,256]{1,0:T(8,128)(2,1)} %get-tuple-element.58), channel_id=1, source_target_pairs={{1,0},{2,1},{3,2},{4,3},{5,4},{6,5},{7,6},{0,7},{9,8},{10,9},{11,1... | collective-permute-start | bytes 98312 | tf_op jit(solution)/shard_map/ppermute | solution.py:37
  140.1 5.4 %collective-permute-start.9 = (bf16[64,256]{1,0:T(8,128)(2,1)}, bf16[64,256]{1,0:T(8,128)(2,1)S(1)}, u32[]{:S(2)}, u32[]{:S(2)}) collective-permute-start(bf16[64,256]{1,0:T(8,128)(2,1)} %get-tuple-element.59), channel_id=1, source_target_pairs={{7,0},{0,1},{1,2},{2,3},{3,4},{4,5},{5,6},{6,7},{15,8},{8,9},{9,10... | collective-permute-start | bytes 98312 | tf_op jit(solution)/shard_map/ppermute | solution.py:37
  140.6 4.9 %collective-permute-start.10 = (bf16[64,256]{1,0:T(8,128)(2,1)}, bf16[64,256]{1,0:T(8,128)(2,1)S(1)}, u32[]{:S(2)}, u32[]{:S(2)}) collective-permute-start(bf16[64,256]{1,0:T(8,128)(2,1)} %get-tuple-element.60), channel_id=1, source_target_pairs={{2,0},{3,1},{4,2},{5,3},{6,4},{7,5},{0,6},{1,7},{10,8},{11,9},{12,... | collective-permute-start | bytes 98312 | tf_op jit(solution)/shard_map/ppermute | solution.py:37
  140.8 6.1 %collective-permute-start.11 = (bf16[64,256]{1,0:T(8,128)(2,1)}, bf16[64,256]{1,0:T(8,128)(2,1)S(1)}, u32[]{:S(2)}, u32[]{:S(2)}) collective-permute-start(bf16[64,256]{1,0:T(8,128)(2,1)} %get-tuple-element.61), channel_id=1, source_target_pairs={{6,0},{7,1},{0,2},{1,3},{2,4},{3,5},{4,6},{5,7},{14,8},{15,9},{8,1... | collective-permute-start | bytes 98312 | tf_op jit(solution)/shard_map/ppermute | solution.py:37
  142.6 4.3 %copy-start.22 = (bf16[64,256]{1,0:T(8,128)(2,1)}, bf16[64,256]{1,0:T(8,128)(2,1)S(1)}, u32[]{:S(2)}) copy-start(bf16[64,256]{1,0:T(8,128)(2,1)S(1)} %collective-permute-done.8.rest_0_) | copy-start | bytes 98308
  145.5 1.5 copy-start.23
  145.5 1.4 copy-start.24
  153.9 3.1 %collective-permute-start.19 = (bf16[4,64,640]{2,1,0:T(8,128)(2,1)}, bf16[4,64,640]{2,1,0:T(8,128)(2,1)S(1)}, u32[]{:S(2)}, u32[]{:S(2)}) collective-permute-start(bf16[4,64,640]{2,1,0:T(8,128)(2,1)} %get-tuple-element.70), channel_id=1, source_target_pairs={{0,1},{1,0},{2,3},{3,2},{4,5},{5,4},{6,7},{7,6},{8,9},{9,8},{10,11... | collective-permute-start | bytes 983048 | tf_op jit(solution)/shard_map/ppermute | solution.py:622
  156.9 0.7 copy-start.1
  159.5 8.8 %collective-permute-start.20 = (bf16[64,640]{1,0:T(8,128)(2,1)}, bf16[64,640]{1,0:T(8,128)(2,1)S(1)}, u32[]{:S(2)}, u32[]{:S(2)}) collective-permute-start(bf16[64,640]{1,0:T(8,128)(2,1)} %get-tuple-element.72), channel_id=1, source_target_pairs={{0,2},{1,3},{2,4},{3,5},{4,6},{5,7},{6,0},{7,1},{8,10},{9,11},{10,... | collective-permute-start | bytes 245768 | tf_op jit(solution)/shard_map/ppermute | solution.py:633
  159.5 0.8 copy-start
  162.4 26.0 %collective-permute-start.13 = (bf16[64,1152]{1,0:T(8,128)(2,1)}, bf16[64,1152]{1,0:T(8,128)(2,1)S(1)}, u32[]{:S(2)}, u32[]{:S(2)}) collective-permute-start(bf16[64,1152]{1,0:T(8,128)(2,1)} %get-tuple-element.66), channel_id=1, source_target_pairs={{0,2},{1,3},{2,4},{3,5},{4,6},{5,7},{6,0},{7,1},{8,10},{9,11},{10,... | collective-permute-start | bytes 442376 | tf_op jit(solution)/shard_map/ppermute | solution.py:633
  162.6 25.8 %collective-permute-start.14 = (bf16[64,1152]{1,0:T(8,128)(2,1)}, bf16[64,1152]{1,0:T(8,128)(2,1)S(1)}, u32[]{:S(2)}, u32[]{:S(2)}) collective-permute-start(bf16[64,1152]{1,0:T(8,128)(2,1)} %get-tuple-element.67), channel_id=1, source_target_pairs={{0,4},{1,5},{2,6},{3,7},{4,0},{5,1},{6,2},{7,3},{8,12},{9,13},{10,... | collective-permute-start | bytes 442376 | tf_op jit(solution)/shard_map/ppermute | solution.py:633
  166.8 21.7 %collective-permute-start.15 = (bf16[64,1152]{1,0:T(8,128)(2,1)}, bf16[64,1152]{1,0:T(8,128)(2,1)S(1)}, u32[]{:S(2)}, u32[]{:S(2)}) collective-permute-start(bf16[64,1152]{1,0:T(8,128)(2,1)} %get-tuple-element.68), channel_id=1, source_target_pairs={{0,6},{1,7},{2,0},{3,1},{4,2},{5,3},{6,4},{7,5},{8,14},{9,15},{10,... | collective-permute-start | bytes 442376 | tf_op jit(solution)/shard_map/ppermute | solution.py:633
  166.8 16.9 %collective-permute-start.21 = (bf16[64,640]{1,0:T(8,128)(2,1)}, bf16[64,640]{1,0:T(8,128)(2,1)S(1)}, u32[]{:S(2)}, u32[]{:S(2)}) collective-permute-start(bf16[64,640]{1,0:T(8,128)(2,1)} %get-tuple-element.73), channel_id=1, source_target_pairs={{0,4},{1,5},{2,6},{3,7},{4,0},{5,1},{6,2},{7,3},{8,12},{9,13},{10,... | collective-permute-start | bytes 245768 | tf_op jit(solution)/shard_map/ppermute | solution.py:633
  168.3 15.4 %copy-start.15 = (bf16[64,640]{1,0:T(8,128)(2,1)}, bf16[64,640]{1,0:T(8,128)(2,1)S(1)}, u32[]{:S(2)}) copy-start(bf16[64,640]{1,0:T(8,128)(2,1)S(1)} %collective-permute-done.20.refs_1_) | copy-start | bytes 245764
  168.3 15.4 %collective-permute-start.22 = (bf16[64,640]{1,0:T(8,128)(2,1)}, bf16[64,640]{1,0:T(8,128)(2,1)S(1)}, u32[]{:S(2)}, u32[]{:S(2)}) collective-permute-start(bf16[64,640]{1,0:T(8,128)(2,1)} %get-tuple-element.74), channel_id=1, source_target_pairs={{0,6},{1,7},{2,0},{3,1},{4,2},{5,3},{6,4},{7,5},{8,14},{9,15},{10,... | collective-permute-start | bytes 245768 | tf_op jit(solution)/shard_map/ppermute | solution.py:633
  183.7 0.7 copy-start.17
  186.0 9.1 %collective-permute-start.25 = (bf16[64,640]{1,0:T(8,128)(2,1)}, bf16[64,640]{1,0:T(8,128)(2,1)S(1)}, u32[]{:S(2)}, u32[]{:S(2)}) collective-permute-start(bf16[64,640]{1,0:T(8,128)(2,1)} %shard_map.158.refs_4_), channel_id=1, source_target_pairs={{0,24},{8,16},{16,8},{24,0},{1,25},{9,17},{17,9},{25,1},{2,26},{10... | collective-permute-start | bytes 245768 | tf_op jit(solution)/shard_map/ppermute | solution.py:647
  188.4 0.7 copy-start.9
  188.4 0.7 copy-start.10
  188.5 0.8 copy-start.11
  191.1 10.8 %collective-permute-start.18 = (bf16[64,1152]{1,0:T(8,128)(2,1)}, bf16[64,1152]{1,0:T(8,128)(2,1)S(1)}, u32[]{:S(2)}, u32[]{:S(2)}) collective-permute-start(bf16[64,1152]{1,0:T(8,128)(2,1)} %shard_map.156.refs_0_), channel_id=1, source_target_pairs={{0,24},{8,16},{16,8},{24,0},{1,25},{9,17},{17,9},{25,1},{2,26},{10... | collective-permute-start | bytes 442376 | tf_op jit(solution)/shard_map/ppermute | solution.py:647
  191.6 10.3 %collective-permute-start.17 = (bf16[64,1152]{1,0:T(8,128)(2,1)}, bf16[64,1152]{1,0:T(8,128)(2,1)S(1)}, u32[]{:S(2)}, u32[]{:S(2)}) collective-permute-start(bf16[64,1152]{1,0:T(8,128)(2,1)} %shard_map.156.refs_0_), channel_id=1, source_target_pairs={{0,16},{8,24},{16,0},{24,8},{1,17},{9,25},{17,1},{25,9},{2,18},{10... | collective-permute-start | bytes 442376 | tf_op jit(solution)/shard_map/ppermute | solution.py:647
  193.1 8.8 %collective-permute-start.16 = (bf16[64,1152]{1,0:T(8,128)(2,1)}, bf16[64,1152]{1,0:T(8,128)(2,1)S(1)}, u32[]{:S(2)}, u32[]{:S(2)}) collective-permute-start(bf16[64,1152]{1,0:T(8,128)(2,1)} %shard_map.156.refs_0_), channel_id=1, source_target_pairs={{0,8},{8,0},{16,24},{24,16},{1,9},{9,1},{17,25},{25,17},{2,10},{10... | collective-permute-start | bytes 442376 | tf_op jit(solution)/shard_map/ppermute | solution.py:647
  194.6 7.3 %collective-permute-start.24 = (bf16[64,640]{1,0:T(8,128)(2,1)}, bf16[64,640]{1,0:T(8,128)(2,1)S(1)}, u32[]{:S(2)}, u32[]{:S(2)}) collective-permute-start(bf16[64,640]{1,0:T(8,128)(2,1)} %shard_map.158.refs_4_), channel_id=1, source_target_pairs={{0,16},{8,24},{16,0},{24,8},{1,17},{9,25},{17,1},{25,9},{2,18},{10... | collective-permute-start | bytes 245768 | tf_op jit(solution)/shard_map/ppermute | solution.py:647
  195.1 6.8 %copy-start.12 = (bf16[64,640]{1,0:T(8,128)(2,1)}, bf16[64,640]{1,0:T(8,128)(2,1)S(1)}, u32[]{:S(2)}) copy-start(bf16[64,640]{1,0:T(8,128)(2,1)S(1)} %collective-permute-done.25.refs_7_) | copy-start | bytes 245764
  195.1 6.8 %collective-permute-start.23 = (bf16[64,640]{1,0:T(8,128)(2,1)}, bf16[64,640]{1,0:T(8,128)(2,1)S(1)}, u32[]{:S(2)}, u32[]{:S(2)}) collective-permute-start(bf16[64,640]{1,0:T(8,128)(2,1)} %shard_map.158.refs_4_), channel_id=1, source_target_pairs={{0,8},{8,0},{16,24},{24,16},{1,9},{9,1},{17,25},{25,17},{2,10},{10... | collective-permute-start | bytes 245768 | tf_op jit(solution)/shard_map/ppermute | solution.py:647
  201.8 0.7 copy-start.14
  201.9 0.7 copy-start.6
  201.9 0.8 copy-start.7
  202.6 0.7 copy-start.8
  (4 other events, 2.5 us)

commit v3 on v2

--- a/solution.py
+++ b/solution.py
@@ -49,8 +49,14 @@
     return pl.BlockSpec(memory_space=pltpu.VMEM)
 
 
-def params(**extra):
-    return pltpu.CompilerParams(vmem_limit_bytes=60 * 1024 * 1024, **extra)
+def params(mib=12):
+    return pltpu.CompilerParams(vmem_limit_bytes=mib * 1024 * 1024)
+
+
+def cost(edges, weight):
+    return pl.CostEstimate(
+        flops=weight * edges * 10**6, transcendentals=0, bytes_accessed=weight * edges * 1000
+    )
 
 
 def send_hot(rows_ref, count_ref, which, edges):
@@ -70,9 +76,7 @@
         pre_ref[start : start + step, :] = pre
         hidden = (pre * jax.nn.sigmoid(pre)).astype(bf16)
         hid_ref[start : start + step, :] = hidden
-        down = lax.dot_general(
-            wd_ref[...], hidden, (((0,), (1,)), ((), ())), preferred_element_type=f32
-        )
+        down = mm(wd_ref[...], hidden, NT)
         pdt_ref[:, start : start + step] = down
         red_ref[:, start : start + step] = (down * jax.nn.sigmoid(down)).astype(bf16)
     for which, send_ref in enumerate(send_refs):
@@ -86,7 +90,7 @@
 
 def front(messages, w_edge, w_down, rows, counts):
     _, edges, model = messages.shape
-    narrow = w_down.shape[1]
+    narrow = w_down.shape[0]
     _, lists, capacity = rows.shape
     return pl.pallas_call(
         front_kernel,
@@ -100,28 +104,49 @@
         in_specs=[smem()] + [vmem()] * 4,
         out_specs=(vmem(),) * (4 + lists),
         compiler_params=params(),
+        cost_estimate=cost(edges, 3),
         name="front",
     )(counts, messages, w_edge, w_down, rows)
 
 
-def pick_kernel(count_ref, cot_ref, rows_ref, after_ref, *send_refs):
+def pick_kernel(count_ref, cot_ref, rows_ref, trip_ref, after_ref, low_ref, high_ref, *send_refs):
     edges = cot_ref.shape[1]
+    capacity = rows_ref.shape[2]
+    groups, rho = low_ref.shape
+    slots = rho // GROUP
+    trip = trip_ref[0]
+    repeat = one_hot(iota((slots, rho), 1) // GROUP, (slots, rho), 0)
+    own = iota((edges, rho), 0) % GROUP == iota((edges, rho), 1) % GROUP
+    gather = one_hot(iota((groups, edges), 1) // GROUP, (groups, edges), 0)
+
+    def slot_major(values):
+        spread = mm(values.astype(f32).astype(bf16), repeat)
+        return mm(gather, jnp.where(own, spread, 0.0).astype(bf16))
+
+    low_ref[...] = slot_major(jnp.bitwise_and(trip, capacity - 1))
+    high_ref[...] = slot_major(jnp.right_shift(trip, capacity.bit_length() - 1)).astype(jnp.int32)
     for which, send_ref in enumerate(send_refs):
         hot = send_hot(rows_ref, count_ref, which, edges)
         send_ref[...] = mm(hot, cot_ref[0], TN).astype(bf16)
 
 
-def pick(cotangent, rows, counts, after):
-    _, _, model = cotangent.shape
+def pick(cotangent, rows, counts, trips, after):
+    _, edges, model = cotangent.shape
     _, lists, capacity = rows.shape
+    slot_major = (edges // GROUP, trips.shape[2] * GROUP)
     return pl.pallas_call(
         pick_kernel,
-        out_shape=(jax.ShapeDtypeStruct((capacity, model), bf16),) * lists,
-        in_specs=[smem(), vmem(), vmem(), pl.BlockSpec(memory_space=pl.ANY)],
-        out_specs=(vmem(),) * lists,
+        out_shape=(
+            jax.ShapeDtypeStruct(slot_major, f32),
+            jax.ShapeDtypeStruct(slot_major, jnp.int32),
+        )
+        + (jax.ShapeDtypeStruct((capacity, model), bf16),) * lists,
+        in_specs=[smem(), vmem(), vmem(), vmem(), pl.BlockSpec(memory_space=pl.ANY)],
+        out_specs=(vmem(),) * (2 + lists),
         compiler_params=params(),
+        cost_estimate=cost(edges, 3),
         name="pick",
-    )(counts, cotangent, rows, after)
+    )(counts, cotangent, rows, trips, after)
 
 
 def widen_weights(wb_ref, wide):
@@ -137,11 +162,6 @@
         wide[(c + 1) * padded : (c + 2) * padded, :] = jnp.concatenate(
             [pair[:, narrow:], zeros], axis=0
         )
-
-
-def split_index(trip, capacity):
-    low = jnp.bitwise_and(trip, capacity - 1).astype(f32).astype(bf16)
-    return low, jnp.right_shift(trip, capacity.bit_length() - 1)
 
 
 def low_iota(capacity, rho):
@@ -193,20 +213,18 @@
         ],
         out_specs=pl.BlockSpec((block * slots, padded), lambda i: (i, 0)),
         scratch_shapes=[pltpu.VMEM((sub // GROUP, rho, padded), f32)],
-        compiler_params=params(),
-        cost_estimate=pl.CostEstimate(
-            flops=0, transcendentals=0, bytes_accessed=edges * slots * padded * 10
-        ),
+        compiler_params=params(12),
+        cost_estimate=cost(edges, 6),
         name="align",
     )(after, triplet_basis)
 
 
-def forward_kernel(sub, lists, bas_ref, trip_ref, red_ref, wb_ref, *rest):
+def forward_kernel(sub, lists, bas_ref, low_ref, high_ref, red_ref, wb_ref, *rest):
     recv_refs = rest[:lists]
-    outer_ref, state_ref, pool, wide, gat_s, num_s = rest[lists:]
+    outer_ref, state_ref, wide, pool, gat_s, num_s = rest[lists:]
     narrow, edges = red_ref.shape
     capacity = recv_refs[0].shape[1]
-    rho = trip_ref.shape[1]
+    rho = low_ref.shape[1]
     padded = bas_ref.shape[1]
     locals_ = edges // capacity
 
@@ -227,7 +245,8 @@
         first_group = pl.multiple_of(index * groups, groups)
 
         def gather(g):
-            low, high = split_index(trip_ref[pl.ds(first_group + g, 1), :], capacity)
+            low = low_ref[pl.ds(first_group + g, 1), :].astype(bf16)
+            high = high_ref[pl.ds(first_group + g, 1), :]
             found = mm(pool[...], low_hot(low, num_s[...]))
             gathered = jnp.zeros((narrow, rho), f32)
             for h in range(locals_ + lists):
@@ -266,11 +285,11 @@
     state_ref[...] = mm(outer_ref[...], wide[...]).astype(bf16)
 
 
-def forward(bas, trips, red, recv, w_bil):
+def forward(bas, low, high, red, recv, w_bil):
     narrow, edges = red.shape
     lists = len(recv)
     capacity = recv[0].shape[1]
-    rho = trips.shape[1]
+    rho = low.shape[1]
     padded = bas.shape[1]
     block = 256
     sub = 64
@@ -281,9 +300,11 @@
         out_shape=(
             jax.ShapeDtypeStruct((edges, narrow * padded), bf16),
             jax.ShapeDtypeStruct((edges, narrow), bf16),
+            jax.ShapeDtypeStruct((narrow * padded, narrow), bf16),
         ),
         in_specs=[
             pl.BlockSpec((block * rho // GROUP, padded), lambda i: (i, 0)),
+            pl.BlockSpec((block // GROUP, rho), lambda i: (i, 0)),
             pl.BlockSpec((block // GROUP, rho), lambda i: (i, 0)),
             resident(narrow, edges),
             resident(*w_bil.shape),
@@ -292,16 +313,17 @@
         out_specs=(
             pl.BlockSpec((block, narrow * padded), lambda i: (i, 0)),
             pl.BlockSpec((block, narrow), lambda i: (i, 0)),
+            resident(narrow * padded, narrow),
         ),
         scratch_shapes=[
             pltpu.VMEM((edges // capacity * narrow + lists * narrow, capacity), bf16),
-            pltpu.VMEM((narrow * padded, narrow), bf16),
             pltpu.VMEM((sub // GROUP, narrow, rho), f32),
             pltpu.VMEM((capacity, rho), bf16),
         ],
-        compiler_params=params(),
+        compiler_params=params(32),
+        cost_estimate=cost(edges, 29),
         name="forward",
-    )(bas, trips, red, w_bil, *recv)
+    )(bas, low, high, red, w_bil, *recv)
 
 
 def settle(core_ref, keep_ref, give_ref, pair, part, even, odd):
@@ -311,51 +333,97 @@
 
 
 def state_kernel(
-    scale, parts, lists,
-    count_ref, core_ref, outer_ref, state_ref, cot_ref, rev_ref, own_ref, wu_ref, *rest
+    lists, count_ref, state_ref, cot_ref, rev_ref, own_ref, wu_ref, *rest
 ):
     recv_refs = rest[:lists]
-    grad_ref, keep_ref, give_ref, ca_s, ac_s, bil_s = rest[lists:]
-    block, narrow = state_ref.shape
+    grad_ref, up_ref, mirror_s, cast_s = rest[lists:]
+    block, _ = state_ref.shape
     edges = own_ref.shape[1]
     capacity, model = recv_refs[0].shape
-    columns = outer_ref.shape[1]
     pid = pl.program_id(0)
 
     @pl.when(pid == 0)
     def _():
-        ca_s[...] = jnp.zeros_like(ca_s)
-        ac_s[...] = jnp.zeros_like(ac_s)
-        bil_s[...] = jnp.zeros_like(bil_s)
-
-    state = state_ref[...]
-    alive = pid * block + iota((block, 1), 0) < count_ref[0, 0]
-    scaled = jnp.where(alive, cot_ref[0].astype(f32) * inv_root, 0.0)
-    pre_ca = mm(state, wu_ref[0])
-    grad_ca = (scaled * silu_slope(pre_ca)).astype(bf16)
-    reverse = rev_ref[...]
-    mirror = mm(one_hot(reverse, (edges, block), 0), own_ref[0], TN)
+        up_ref[...] = jnp.zeros_like(up_ref)
+
+    row = rev_ref[...].astype(f32)
+    reverse = jnp.broadcast_to(row, (GROUP, block)).T[:, :1].astype(jnp.int32)
+    mirror = mm(one_hot(reverse, (block, edges), 1), own_ref[0])
     for which, recv_ref in enumerate(recv_refs):
         base = edges + which * capacity
-        mirror = mirror + mm(one_hot(reverse - base, (capacity, block), 0), recv_ref[...], TN)
-    pre_ac = mm(state, wu_ref[1])
-    grad_ac = (mirror * inv_root * silu_slope(pre_ac)).astype(bf16)
-    ca_s[...] += mm(grad_ca, state, TN)
-    ac_s[...] += mm(grad_ac, state, TN)
-    back_rev = mm(grad_ac, wu_ref[1], NT).astype(bf16).astype(f32)
-    grad_state = (mm(grad_ca, wu_ref[0], NT) + back_rev).astype(bf16)
-    grad_ref[...] = grad_state
+        mirror = mirror + mm(one_hot(reverse - base, (block, capacity), 1), recv_ref[...])
+    mirror_s[...] = mirror
+    step = 64
+    for start in range(0, block, step):
+        part = slice(start, start + step)
+        state = state_ref[part, :]
+        alive = pid * block + start + iota((step, 1), 0) < count_ref[0, 0]
+        scaled = jnp.where(alive, cot_ref[0, part, :].astype(f32) * inv_root, 0.0)
+        cast_s[part, :model] = (scaled * silu_slope(mm(state, wu_ref[0]))).astype(bf16)
+        cast_s[part, model:] = (
+            mirror_s[part, :] * inv_root * silu_slope(mm(state, wu_ref[1]))
+        ).astype(bf16)
+    up_ref[...] += mm(state_ref[...], cast_s[...], TN)
+    back_rev = mm(cast_s[:, model:], wu_ref[1], NT).astype(bf16).astype(f32)
+    grad_ref[...] = (mm(cast_s[:, :model], wu_ref[0], NT) + back_rev).astype(bf16)
+
+
+def state_grads(count, state, cotangent, rev, recv_cot, w_up):
+    edges, narrow = state.shape
+    model = cotangent.shape[2]
+    block = 256
+    lists = len(recv_cot)
+    resident = lambda *shape: pl.BlockSpec(shape, lambda i: (0,) * len(shape))
+    return pl.pallas_call(
+        functools.partial(state_kernel, lists),
+        grid=(edges // block,),
+        out_shape=(
+            jax.ShapeDtypeStruct((edges, narrow), bf16),
+            jax.ShapeDtypeStruct((narrow, 2 * model), f32),
+        ),
+        in_specs=[
+            smem(),
+            pl.BlockSpec((block, narrow), lambda i: (i, 0)),
+            pl.BlockSpec((1, block, model), lambda i: (0, i, 0)),
+            pl.BlockSpec((1, block), lambda i: (0, i)),
+            resident(1, edges, model),
+            resident(*w_up.shape),
+        ]
+        + [resident(*recv_cot[0].shape)] * lists,
+        out_specs=(
+            pl.BlockSpec((block, narrow), lambda i: (i, 0)),
+            resident(narrow, 2 * model),
+        ),
+        scratch_shapes=[
+            pltpu.VMEM((block, model), f32),
+            pltpu.VMEM((block, 2 * model), bf16),
+        ],
+        compiler_params=params(16),
+        cost_estimate=cost(edges, 7),
+        name="state_grads",
+    )(count, state, cotangent, rev, cotangent, w_up, *recv_cot)
+
+
+def bil_kernel(scale, parts, core_ref, outer_ref, grad_ref, up_ref, keep_ref, give_ref, bil_s):
+    narrow, columns = bil_s.shape
+    model = up_ref.shape[1] // 2
+    pid = pl.program_id(0)
+
+    @pl.when(pid == 0)
+    def _():
+        bil_s[...] = jnp.zeros_like(bil_s)
+
     wide_step = 1024
     for start in range(0, columns, wide_step):
         bil_s[:, start : start + wide_step] += mm(
-            grad_state, outer_ref[:, start : start + wide_step], TN
+            grad_ref[...], outer_ref[:, start : start + wide_step], TN
         )
 
     @pl.when(pid == pl.num_programs(0) - 1)
     def _():
         span = columns // parts
         thin = model // parts
-        both = jnp.concatenate([ca_s[...], ac_s[...]], axis=1)
+        both = jnp.concatenate([up_ref[:, :model], up_ref[:, model:]], axis=0).T
         if thin < narrow:
             spare = jnp.zeros((narrow - thin, 2 * narrow), f32)
         for pair in range(parts // 2):
@@ -372,46 +440,28 @@
             settle(core_ref, keep_ref, give_ref, pair, slice(span, span + 2 * narrow), *sides)
 
 
-def state_grads(count, core, outer, state, cotangent, rev, recv_cot, w_up, scale, parts):
-    edges, narrow = state.shape
-    model = cotangent.shape[2]
+def bil_shares(core, outer, grad_state, up, scale, parts):
+    edges, narrow = grad_state.shape
     columns = outer.shape[1]
     block = 256
-    lists = len(recv_cot)
     share = (parts // 2, narrow, columns // parts + 2 * narrow)
     resident = lambda *shape: pl.BlockSpec(shape, lambda i: (0,) * len(shape))
     return pl.pallas_call(
-        functools.partial(state_kernel, scale, parts, lists),
+        functools.partial(bil_kernel, scale, parts),
         grid=(edges // block,),
-        out_shape=(
-            jax.ShapeDtypeStruct((edges, narrow), bf16),
-            jax.ShapeDtypeStruct(share, bf16),
-            jax.ShapeDtypeStruct(share, bf16),
-        ),
+        out_shape=(jax.ShapeDtypeStruct(share, bf16),) * 2,
         in_specs=[
-            smem(),
             smem(),
             pl.BlockSpec((block, columns), lambda i: (i, 0)),
             pl.BlockSpec((block, narrow), lambda i: (i, 0)),
-            pl.BlockSpec((1, block, model), lambda i: (0, i, 0)),
-            pl.BlockSpec((1, block), lambda i: (0, i)),
-            resident(1, edges, model),
-            resident(*w_up.shape),
-        ]
-        + [resident(*recv_cot[0].shape)] * lists,
-        out_specs=(
-            pl.BlockSpec((block, narrow), lambda i: (i, 0)),
-            resident(*share),
-            resident(*share),
-        ),
-        scratch_shapes=[
-            pltpu.VMEM((model, narrow), f32),
-            pltpu.VMEM((model, narrow), f32),
-            pltpu.VMEM((narrow, columns), f32),
+            resident(*up.shape),
         ],
-        compiler_params=params(),
-        name="state_grads",
-    )(count, core, outer, state, cotangent, rev, cotangent, w_up, *recv_cot)
+        out_specs=(resident(*share),) * 2,
+        scratch_shapes=[pltpu.VMEM((narrow, columns), f32)],
+        compiler_params=params(20),
+        cost_estimate=cost(edges, 4),
+        name="bil_shares",
+    )(core, outer, grad_state, up)
 
 
 def own_rows(mixed, narrow):
@@ -434,18 +484,17 @@
     return value.reshape(narrow, rho)
 
 
-def backward_kernel(sub, lists, bas_ref, grad_ref, trip_ref, wb_ref, home_ref, *rest):
+def backward_kernel(sub, lists, bas_ref, grad_ref, low_ref, high_ref, wide, home_ref, *rest):
     back_refs = rest[:lists]
-    pool_s, wide, turn_s, cast_s, hot_s, num_s = rest[lists:]
+    pool_s, turn_s, cast_s, hot_s, num_s = rest[lists:]
     block, narrow = grad_ref.shape
     padded = bas_ref.shape[1]
-    rho = trip_ref.shape[1]
+    rho = low_ref.shape[1]
     rows, capacity = pool_s.shape
     pid = pl.program_id(0)
 
     @pl.when(pid == 0)
     def _():
-        widen_weights(wb_ref, wide)
         pool_s[...] = jnp.zeros_like(pool_s)
         num_s[...] = low_iota(capacity, rho)
 
@@ -456,14 +505,14 @@
         start = pl.multiple_of(pair * 2 * padded, 2 * padded)
         grad = mm(grad_state, wide[pl.ds(start, 2 * padded), :], NT)
         for g in range(block // GROUP):
-            for side in range(2):
-                at = pl.multiple_of(g * height + pair * 2 * GROUP + side * GROUP, GROUP)
-                turn_s[pl.ds(at, GROUP), :] = grad[
-                    g * GROUP : (g + 1) * GROUP, side * padded : (side + 1) * padded
-                ]
+            part = slice(g * GROUP, (g + 1) * GROUP)
+            at = pl.multiple_of(g * height + pair * 2 * GROUP, 2 * GROUP)
+            turn_s[pl.ds(at, 2 * GROUP), :] = jnp.concatenate(
+                [grad[part, :padded], grad[part, padded:]], axis=0
+            ).astype(bf16)
         return carry
 
-    lax.fori_loop(0, narrow // 2, spread, 0, unroll=4)
+    lax.fori_loop(0, narrow // 2, spread, 0, unroll=8)
     groups = sub // GROUP
 
     def body(index, carry):
@@ -473,11 +522,12 @@
             here = first_group + g
             bas = bas_ref[pl.ds(pl.multiple_of(here * rho, rho), rho), :]
             grads = turn_s[pl.ds(pl.multiple_of(here * height, height), height), :]
-            return mm(grads.astype(bf16), bas, NT)
+            return mm(grads, bas, NT)
 
         def cast(g, mixed):
             trip_grad = own_rows(mixed, narrow).astype(bf16)
-            low, high = split_index(trip_ref[pl.ds(first_group + g, 1), :], capacity)
+            low = low_ref[pl.ds(first_group + g, 1), :].astype(bf16)
+            high = high_ref[pl.ds(first_group + g, 1), :]
             part = slice(g * rho, (g + 1) * rho)
             hot_s[:, part] = low_hot(low, num_s[...])
             zero = jnp.zeros_like(trip_grad)
@@ -507,9 +557,9 @@
             back_ref[...] = pool_s[first : first + narrow, :].astype(bf16)
 
 
-def backward(bas, grad_state, trips, w_bil, capacity, lists):
+def backward(bas, grad_state, low, high, wide, capacity, lists):
     edges, narrow = grad_state.shape
-    rho = trips.shape[1]
+    rho = low.shape[1]
     padded = bas.shape[1]
     block = 256
     sub = 64
@@ -525,20 +575,21 @@
             pl.BlockSpec((block * rho // GROUP, padded), lambda i: (i, 0)),
             pl.BlockSpec((block, narrow), lambda i: (i, 0)),
             pl.BlockSpec((block // GROUP, rho), lambda i: (i, 0)),
-            resident(*w_bil.shape),
+            pl.BlockSpec((block // GROUP, rho), lambda i: (i, 0)),
+            resident(*wide.shape),
         ],
         out_specs=(resident(home, capacity),) + (resident(narrow, capacity),) * lists,
         scratch_shapes=[
             pltpu.VMEM((rows, capacity), f32),
-            pltpu.VMEM((narrow * padded, narrow), bf16),
-            pltpu.VMEM((block * narrow, padded), f32),
+            pltpu.VMEM((block * narrow, padded), bf16),
             pltpu.VMEM((rows, sub // GROUP * rho), bf16),
             pltpu.VMEM((capacity, sub // GROUP * rho), bf16),
             pltpu.VMEM((capacity, rho), bf16),
         ],
-        compiler_params=params(),
+        compiler_params=params(32),
+        cost_estimate=cost(edges, 32),
         name="backward",
-    )(bas, grad_state, trips, w_bil)
+    )(bas, grad_state, low, high, wide)
 
 
 def tail_kernel(
@@ -559,9 +610,7 @@
     step = 256
     for start in range(0, edges, step):
         part = slice(start, start + step)
-        grad_hidden = lax.dot_general(
-            grad_down[:, part], wd_ref[...], (((0,), (1,)), ((), ())), preferred_element_type=f32
-        )
+        grad_hidden = mm(grad_down[:, part], wd_ref[...], TN)
         grad_edge = (grad_hidden * silu_slope(pre_ref[part, :])).astype(bf16)
         grad_s[part, :] = grad_edge
         out_ref[0, part, :] = mm(grad_edge, we_ref[...], NT).astype(bf16)
@@ -582,7 +631,7 @@
 
 def tail(pool, back, rows, counts, core, pdt, pre, hidden, messages, w_edge, w_down, scale, parts):
     _, edges, model = messages.shape
-    narrow = w_down.shape[1]
+    narrow = w_down.shape[0]
     share = jax.ShapeDtypeStruct((parts // 2, model // parts, model + 2 * narrow), bf16)
     return pl.pallas_call(
         functools.partial(tail_kernel, scale, parts, len(back)),
@@ -595,6 +644,7 @@
         out_specs=(vmem(),) * 3,
         scratch_shapes=[pltpu.VMEM((edges, model), bf16)],
         compiler_params=params(),
+        cost_estimate=cost(edges, 4),
         name="tail",
     )(counts, core, pool, rows, pdt, pre, hidden, messages, w_edge, w_down, *back)
 
@@ -710,6 +760,7 @@
 ):
     _, edges, model = messages.shape
     narrow = w_down.shape[1]
+    w_down = w_down.T
     slots = trip_src.shape[2]
     _, lists, capacity = send_rows.shape
     basis_count = w_bil.shape[0]
@@ -718,12 +769,6 @@
     shifts = offsets(lists)
     place = lax.axis_index("graph").reshape(1, 1)
     core, chip = place % 2, place // 2
-    trips = (
-        trip_src[0]
-        .reshape(edges // GROUP, GROUP, slots)
-        .transpose(0, 2, 1)
-        .reshape(edges // GROUP, GROUP * slots)
-    )
 
     def exchange(blocks, sign):
         moved = []
@@ -733,15 +778,14 @@
 
     pre, hidden, pdt, red, *send_red = front(messages, w_edge, w_down, send_rows, send_count)
     recv_red = exchange(send_red, 1)
-    send_cot = pick(cotangent, send_rows, send_count, red)
+    low, high, *send_cot = pick(cotangent, send_rows, send_count, trip_src, red)
     recv_cot = exchange(send_cot, 1)
     bas = align(triplet_basis, basis_count, slots, send_cot[0])
-    outer, state = forward(bas, trips, red, recv_red, w_bil)
-    grad_state, keep, give = state_grads(
-        edge_count, core, outer, state, cotangent, rev_src, recv_cot, w_up, scale, parts
-    )
+    outer, state, wide = forward(bas, low, high, red, recv_red, w_bil)
+    grad_state, up = state_grads(edge_count, state, cotangent, rev_src, recv_cot, w_up)
+    keep, give = bil_shares(core, outer, grad_state, up, scale, parts)
     early = over_graph(keep, give, chip)
-    home, *returned = backward(bas, grad_state, trips, w_bil, capacity, lists)
+    home, *returned = backward(bas, grad_state, low, high, wide, capacity, lists)
     back = exchange(returned, -1)
     early = over_dp(early)
     grad_messages, keep, give = tail(

time: 206 us -> 173 us (0.84)
  Pallas kernels: 117 us -> 88.5 us
  waiting for transfers between devices: 47.9 us -> 22.2 us
  local copies, waits for them, and re-layouts: 10.2 us -> 24.7 us
  starting transfers between devices: 29 us -> 35.3 us
    ppermute x12, waiting for transfers between devices: 27.7 us -> 0.32 us  [shifted(): return lax.ppermute(block, axis, route)]
    unnamed x54 -> x79, local copies, waits for them, and re-layouts: 9.18 us -> 24.7 us
    ppermute x12, starting transfers between devices: 10.9 us -> 18.4 us  [shifted(): return lax.ppermute(block, axis, route)]
    pallas_call x2 -> x3, Pallas kernels: 18.6 us -> 13 us  [the longest x1 6.24 us: state_grads(): pl.pallas_call(functools.partial(state_kernel, lists), grid=(edges // blo...]
    pallas_call x1, Pallas kernels: 10.2 us -> 5 us  [align(): pl.pallas_call(functools.partial(align_kernel, basis_count, sub), grid=(e...]
    pallas_call x1, Pallas kernels: 37.1 us -> 32.4 us  [backward(): pl.pallas_call(functools.partial(backward_kernel, sub, lists), grid=(edge...]
    pallas_call x2, Pallas kernels: 3.88 us -> 0.24 us  [over_graph(): pl.pallas_call(add_pair_kernel, out_shape=(piece,) * chips, in_specs=[sme...]
    pallas_call x2, Pallas kernels: 3.53 us -> 0.12 us  [over_graph(): pl.pallas_call(add_kernel, out_shape=piece, in_specs=[vmem()] * chips, ou...]
  transfers between devices with their start and end apart: 26 -> 26, of which waited for: 8 -> 5; matrix products, arithmetic and copies ran while one was open for 1% -> 0% of each run, Pallas kernels for 45% -> 27%
where the time goes in v3:
time: 173 us; the launch traced here: 172 us
  Pallas kernels  88.5 us (51%)
  starting transfers between devices  35.3 us (20%)
  local copies, waits for them, and re-layouts  24.7 us (14%)
  waiting for transfers between devices  22.2 us (13%)
    pallas_call x1, Pallas kernels, backward(): pl.pallas_call(functools.partial(backward_kernel, sub, lists), grid=(edge...  32.4 us
    pallas_call x1, Pallas kernels, forward(): pl.pallas_call(functools.partial(forward_kernel, sub, lists), grid=(edges...  29.5 us
    unnamed x79, local copies, waits for them, and re-layouts  24.7 us
    ppermute x12, starting transfers between devices, shifted(): return lax.ppermute(block, axis, route)  18.4 us
    ppermute x6, waiting for transfers between devices, over_graph(): arrived.append(lax.ppermute(send, 'graph', route))  14.2 us
    ppermute x6, starting transfers between devices, over_graph(): arrived.append(lax.ppermute(send, 'graph', route))  8.42 us
    ppermute x6, starting transfers between devices, over_dp(): lax.ppermute(share, 'dp', [(i, i ^ step) for i in range(slabs)])  8.23 us
    ppermute x6, waiting for transfers between devices, over_dp(): lax.ppermute(share, 'dp', [(i, i ^ step) for i in range(slabs)])  6.29 us
  transfers between devices with their start and end apart: 26, of which 5 were waited for; matrix products, arithmetic and copies ran while one was open for 0% of the time, Pallas kernels for 27%

profile of v3, /device:TPU:0, one launch (start us, length us, event | category | flops | bytes accessed | tf_op | source)
XLA Modules:
  0.0 172.4 jit_solution(16404564030763296283)
XLA Ops:
  0.7 1.3 copy-done.2
  2.0 1.0 copy-done.5
  3.0 0.8 copy-done.8
  3.8 0.7 copy-done.11
  4.5 0.7 copy-done.13
  5.2 2.9 %front.1 = (f32[1024,512]{1,0:T(8,128)S(1)}, bf16[1024,512]{1,0:T(8,128)(2,1)S(1)}, f32[64,1024]{1,0:T(8,128)S(1)}, bf16[64,1024]{1,0:T(8,128)(2,1)S(1)}, bf16[6...) custom-call(s32[1,4]{1,0:T(1,128)S(1)} %copy-done.13, ...), custom_call_target="tpu_custom_call" | custom-call | flops 3072000000 | bytes 3072000 | tf_op jit(solution)/shard_map/front/pallas_call | solution.py:95
  8.1 1.3 copy-done.18
  9.4 1.0 copy-done.20
  10.3 0.7 copy-done.22
  11.0 0.5 collective-permute-start
  11.5 4.0 %collective-permute-start.1 = (bf16[64,256]{1,0:T(8,128)(2,1)}, bf16[64,256]{1,0:T(8,128)(2,1)}, u32[]{:S(2)}, u32[]{:S(2)}) collective-permute-start(bf16[64,256]{1,0:T(8,128)(2,1)} %get-tuple-element.51), channel_id=1, source_target_pairs={{1,0},{2,1},{3,2},{4,3},{5,4},{6,5},{7,6},{0,7},{9,8},{10,9},{11,1... | collective-permute-start | bytes 98312 | tf_op jit(solution)/shard_map/ppermute | solution.py:37
  15.8 3.5 %collective-permute-start.3 = (bf16[64,256]{1,0:T(8,128)(2,1)}, bf16[64,256]{1,0:T(8,128)(2,1)}, u32[]{:S(2)}, u32[]{:S(2)}) collective-permute-start(bf16[64,256]{1,0:T(8,128)(2,1)} %get-tuple-element.53), channel_id=1, source_target_pairs={{2,0},{3,1},{4,2},{5,3},{6,4},{7,5},{0,6},{1,7},{10,8},{11,9},{12,... | collective-permute-start | bytes 98312 | tf_op jit(solution)/shard_map/ppermute | solution.py:37
  19.6 2.6 %pick.1 = (f32[128,256]{1,0:T(8,128)S(1)}, s32[128,256]{1,0:T(8,128)S(1)}, bf16[256,512]{1,0:T(8,128)(2,1)S(1)}, bf16[256,512]{1,0:T(8,128)(2,1)S(1)}, bf16[256,...) custom-call(s32[1,4]{1,0:T(1,128)S(1)} %copy-done.14, bf16[1,1024,512]{2,1,0:T(8,128)(2,1)S(1)} %copy-done.1, ...), custom_call_target="tpu_custom_call" | custom-call | flops 3072000000 | bytes 3072000 | tf_op jit(solution)/shard_map/pick/pallas_call | solution.py:137
  22.3 0.6 copy-done.24
  22.9 0.7 copy-done.27
  23.6 3.1 %copy-done = bf16[1,1024,3584]{2,1,0:T(8,128)(2,1)S(1)} copy-done((bf16[1,1024,3584]{2,1,0:T(8,128)(2,1)S(1)}, bf16[1,1024,3584]{2,1,0:T(8,128)(2,1)}, u32[]{:S(2)}) %copy-start) | copy-done | bytes 7340056
  26.7 5.0 %align.1.bas_ref = bf16[32768,128]{1,0:T(8,128)(2,1)S(1)} custom-call(bf16[256,512]{1,0:T(8,128)(2,1)S(1)} %get-tuple-element.47.after_ref, bf16[1,1024,3584]{2,1,0:T(8,128)(2,1)S(1)} %copy-done), custom_call_target="tpu_custom_call" | custom-call | flops 6144000000 | bytes 6144000 | tf_op jit(solution)/shard_map/align/pallas_call | solution.py:206
  31.7 3.3 %copy-done.15 = bf16[32768,128]{1,0:T(8,128)(2,1)} copy-done((bf16[32768,128]{1,0:T(8,128)(2,1)}, bf16[32768,128]{1,0:T(8,128)(2,1)S(1)}, u32[]{:S(2)}) %copy-start.15) | copy-done | bytes 8388632
  35.7 3.6 %collective-permute-start.5 = (bf16[256,512]{1,0:T(8,128)(2,1)S(1)}, bf16[256,512]{1,0:T(8,128)(2,1)S(1)}, u32[]{:S(2)}, u32[]{:S(2)}) collective-permute-start(bf16[256,512]{1,0:T(8,128)(2,1)S(1)} %get-tuple-element.55), channel_id=1, source_target_pairs={{1,0},{2,1},{3,2},{4,3},{5,4},{6,5},{7,6},{0,7},{9,8},{10,9},{11,1... | collective-permute-start | bytes 786440 | tf_op jit(solution)/shard_map/ppermute | solution.py:37
  39.3 3.8 %collective-permute-start.7 = (bf16[256,512]{1,0:T(8,128)(2,1)S(1)}, bf16[256,512]{1,0:T(8,128)(2,1)S(1)}, u32[]{:S(2)}, u32[]{:S(2)}) collective-permute-start(bf16[256,512]{1,0:T(8,128)(2,1)S(1)} %get-tuple-element.57), channel_id=1, source_target_pairs={{2,0},{3,1},{4,2},{5,3},{6,4},{7,5},{0,6},{1,7},{10,8},{11,9},{12,... | collective-permute-start | bytes 786440 | tf_op jit(solution)/shard_map/ppermute | solution.py:37
  43.1 3.4 %copy-done.16 = bf16[32768,128]{1,0:T(8,128)(2,1)S(1)} copy-done((bf16[32768,128]{1,0:T(8,128)(2,1)S(1)}, bf16[32768,128]{1,0:T(8,128)(2,1)}, u32[]{:S(2)}) %copy-start.16) | copy-done | bytes 8388632
  46.5 0.9 copy-done.25
  47.4 0.9 copy-done.28
  48.3 0.9 copy-done.31
  49.2 29.5 %forward.1 = (bf16[1024,8192]{1,0:T(8,128)(2,1)}, bf16[1024,64]{1,0:T(8,128)(2,1)S(1)}, bf16[8192,64]{1,0:T(8,128)(2,1)S(1)}) custom-call(bf16[32768,128]{1,0:T(8,128)(2,1)S(1)} %copy-done.16, f32[128,256]{1,0:T(8,128)S(1)} %copy-done.25, s32[128,256]{1,0:T(8,128)S(1)} %copy-done.28, bf16[64,1024]{1,0:T(8,128)(2,1)S(1)} %copy-done.31, ...), custom_call_target="tpu_custom_call" | custom-call | flops 29696000000 | bytes 29696000 | tf_op jit(solution)/shard_map/forward/pallas_call | solution.py:297
  78.7 1.5 copy-done.32
  80.3 6.2 %state_grads.1 = (bf16[1024,64]{1,0:T(8,128)(2,1)S(1)}, f32[64,1024]{1,0:T(8,128)S(1)}) custom-call(s32[1,1]{1,0:T(1,128)S(6)} %copy.18.count_ref, bf16[1024,64]{1,0:T(8,128)(2,1)S(1)} %get-tuple-element.54.state_ref, bf16[1,1024,512]{2,1,0:T(8,128)(2,1)S(1)} %copy-done.1, s32[1,1024]{1,0:T(1,128)S(1)} %copy-done.10, bf16[1,1024,512]{2,1,0:T(8,128)(2,1)S(1)} %copy-done.1, ...), custom_call_target="tpu_custom_call" | custom-call | flops 7168000000 | bytes 7168000 | tf_op jit(solution)/shard_map/state_grads/pallas_call | solution.py:377
  86.6 1.6 copy-done.33
  88.2 32.4 %backward.1 = (f32[256,256]{1,0:T(8,128)S(1)}, bf16[64,256]{1,0:T(8,128)(2,1)S(1)}, bf16[64,256]{1,0:T(8,128)(2,1)S(1)}, bf16[64,256]{1,0:T(8,128)(2,1)S(1)}, bf16[64,256]{1,0:T(8,128)(2,1)S(1)}) custom-call(bf16[32768,128]{1,0:T(8,128)(2,1)S(1)} %copy-done.17, bf16[1024,64]{1,0:T(8,128)(2,1)S(1)} %get-tuple-element.58.grad_ref, f32[128,256]{1,0:T(8,128)S(1)} %copy-done.26, ...), custom_call_target="tpu_custom_call" | custom-call | flops 32768000000 | bytes 32768000 | tf_op jit(solution)/shard_map/backward/pallas_call | solution.py:569
  120.7 2.0 %collective-permute-start.11 = (bf16[64,256]{1,0:T(8,128)(2,1)S(1)}, bf16[64,256]{1,0:T(8,128)(2,1)S(1)}, u32[]{:S(2)}, u32[]{:S(2)}) collective-permute-start(bf16[64,256]{1,0:T(8,128)(2,1)S(1)} %get-tuple-element.67), channel_id=1, source_target_pairs={{6,0},{7,1},{0,2},{1,3},{2,4},{3,5},{4,6},{5,7},{14,8},{15,9},{8,1... | collective-permute-start | bytes 98312 | tf_op jit(solution)/shard_map/ppermute | solution.py:37
  122.7 0.5 collective-permute-start.9
  123.3 4.1 %bil_shares.1 = (bf16[4,64,1152]{2,1,0:T(8,128)(2,1)S(1)}, bf16[4,64,1152]{2,1,0:T(8,128)(2,1)S(1)}) custom-call(s32[1,1]{1,0:T(1,128)S(6)} %select_n.12.core_ref, bf16[1024,8192]{1,0:T(8,128)(2,1)S(1)} %bitcast.3, bf16[1024,64]{1,0:T(8,128)(2,1)S(1)} %get-tuple-element.58.grad_ref, f32[64,1024]{1,0:T(8,128)S(1)} %get-tuple-element.70.up_ref), custom_call_target="tpu_custom_call" | custom-call | flops 4096000000 | bytes 4096000 | tf_op jit(solution)/shard_map/bil_shares/pallas_call | solution.py:449
  127.5 0.3 collective-permute-done.9.rest_1_
  127.8 4.2 %tail.1 = (bf16[1,1024,512]{2,1,0:T(8,128)(2,1)}, bf16[4,64,640]{2,1,0:T(8,128)(2,1)S(1)}, bf16[4,64,640]{2,1,0:T(8,128)(2,1)S(1)}) custom-call(s32[1,4]{1,0:T(1,128)S(1)} %copy-done.14, s32[1,1]{1,0:T(1,128)S(6)} %select_n.12.core_ref, f32[256,256]{1,0:T(8,128)S(1)} %get-tuple-element.60.pool_ref, s32[1,4,256]{2,1,0:T(4,128)S(1)} %copy-done.12, ...), custom_call_target="tpu_custom_call" | custom-call | flops 4096000000 | bytes 4096000 | tf_op jit(solution)/shard_map/tail/pallas_call | solution.py:636
  132.3 1.4 collective-permute-done.19.got_ref
  134.0 2.3 %collective-permute-start.13 = (bf16[64,1152]{1,0:T(8,128)(2,1)S(1)}, bf16[64,1152]{1,0:T(8,128)(2,1)S(1)}, u32[]{:S(2)}, u32[]{:S(2)}) collective-permute-start(bf16[64,1152]{1,0:T(8,128)(2,1)S(1)} %get-tuple-element.74), channel_id=1, source_target_pairs={{0,2},{1,3},{2,4},{3,5},{4,6},{5,7},{6,0},{7,1},{8,10},{9,11},{10,... | collective-permute-start | bytes 442376 | tf_op jit(solution)/shard_map/ppermute | solution.py:683
  136.3 2.1 %collective-permute-start.14 = (bf16[64,1152]{1,0:T(8,128)(2,1)S(1)}, bf16[64,1152]{1,0:T(8,128)(2,1)S(1)}, u32[]{:S(2)}, u32[]{:S(2)}) collective-permute-start(bf16[64,1152]{1,0:T(8,128)(2,1)S(1)} %get-tuple-element.75), channel_id=1, source_target_pairs={{0,4},{1,5},{2,6},{3,7},{4,0},{5,1},{6,2},{7,3},{8,12},{9,13},{10,... | collective-permute-start | bytes 442376 | tf_op jit(solution)/shard_map/ppermute | solution.py:683
  138.4 2.3 %collective-permute-start.15 = (bf16[64,1152]{1,0:T(8,128)(2,1)S(1)}, bf16[64,1152]{1,0:T(8,128)(2,1)S(1)}, u32[]{:S(2)}, u32[]{:S(2)}) collective-permute-start(bf16[64,1152]{1,0:T(8,128)(2,1)S(1)} %get-tuple-element.76), channel_id=1, source_target_pairs={{0,6},{1,7},{2,0},{3,1},{4,2},{5,3},{6,4},{7,5},{8,14},{9,15},{10,... | collective-permute-start | bytes 442376 | tf_op jit(solution)/shard_map/ppermute | solution.py:683
  140.7 0.4 collective-permute-done.20.refs_1_
  141.1 1.7 collective-permute-start.22
  142.8 13.7 %collective-permute-done.21.refs_2_ = bf16[64,640]{1,0:T(8,128)(2,1)S(1)} collective-permute-done((bf16[64,640]{1,0:T(8,128)(2,1)S(1)}, bf16[64,640]{1,0:T(8,128)(2,1)S(1)}, u32[]{:S(2)}, u32[]{:S(2)}) %collective-permute-start.21) | collective-permute-done | bytes 81952 | tf_op jit(solution)/shard_map/ppermute | solution.py:683
  156.6 2.1 %collective-permute-start.23 = (bf16[64,640]{1,0:T(8,128)(2,1)S(1)}, bf16[64,640]{1,0:T(8,128)(2,1)S(1)}, u32[]{:S(2)}, u32[]{:S(2)}) collective-permute-start(bf16[64,640]{1,0:T(8,128)(2,1)S(1)} %shard_map.158.refs_4_), channel_id=1, source_target_pairs={{0,8},{8,0},{16,24},{24,16},{1,9},{9,1},{17,25},{25,17},{2,10},{10... | collective-permute-start | bytes 245768 | tf_op jit(solution)/shard_map/ppermute | solution.py:697
  158.8 2.0 %collective-permute-start.17 = (bf16[64,1152]{1,0:T(8,128)(2,1)S(1)}, bf16[64,1152]{1,0:T(8,128)(2,1)S(1)}, u32[]{:S(2)}, u32[]{:S(2)}) collective-permute-start(bf16[64,1152]{1,0:T(8,128)(2,1)S(1)} %shard_map.156.refs_0_), channel_id=1, source_target_pairs={{0,16},{8,24},{16,0},{24,8},{1,17},{9,25},{17,1},{25,9},{2,18},{10... | collective-permute-start | bytes 442376 | tf_op jit(solution)/shard_map/ppermute | solution.py:697
  160.9 1.4 collective-permute-start.18
  162.3 1.5 collective-permute-start.24
  163.8 1.1 collective-permute-start.25
  164.9 6.3 %collective-permute-done.24.refs_6_ = bf16[64,640]{1,0:T(8,128)(2,1)S(1)} collective-permute-done((bf16[64,640]{1,0:T(8,128)(2,1)S(1)}, bf16[64,640]{1,0:T(8,128)(2,1)S(1)}, u32[]{:S(2)}, u32[]{:S(2)}) %collective-permute-start.24) | collective-permute-done | bytes 81952 | tf_op jit(solution)/shard_map/ppermute | solution.py:697
  171.2 1.1 finish.1
  (97 shorter events, 1.6 us)
Async XLA Ops:
  0.6 19.0 %copy-start.1 = (bf16[1,1024,512]{2,1,0:T(8,128)(2,1)S(1)}, bf16[1,1024,512]{2,1,0:T(8,128)(2,1)}, u32[]{:S(2)}) copy-start(bf16[1,1024,512]{2,1,0:T(8,128)(2,1)} %own_ref.1) | copy-start | bytes 3145732
  5.2 14.2 %copy-start.34 = (s32[1,1024,32]{1,2,0:T(8,128)S(1)}, s32[1,1024,32]{1,2,0:T(8,128)}, u32[]{:S(2)}) copy-start(s32[1,1024,32]{1,2,0:T(8,128)} %param.19) | copy-start | bytes 393220
  5.2 14.4 %copy-start.12 = (s32[1,4,256]{2,1,0:T(4,128)S(1)}, s32[1,4,256]{2,1,0:T(4,128)}, u32[]{:S(2)}) copy-start(s32[1,4,256]{2,1,0:T(4,128)} %rows_ref.5) | copy-start | bytes 12292
  5.2 14.4 %copy-start.14 = (s32[1,4]{1,0:T(1,128)S(1)}, s32[1,4]{1,0:T(1,128)}, u32[]{:S(2)}) copy-start(s32[1,4]{1,0:T(1,128)} %count_ref.6) | copy-start | bytes 52
  11.0 12.5 %copy-start.30 = (bf16[64,1024]{1,0:T(8,128)(2,1)}, bf16[64,1024]{1,0:T(8,128)(2,1)S(1)}, u32[]{:S(2)}) copy-start(bf16[64,1024]{1,0:T(8,128)(2,1)S(1)} %get-tuple-element.46.after_ref.red_ref) | copy-start | bytes 393220
  11.0 24.6 %collective-permute-start = (bf16[64,256]{1,0:T(8,128)(2,1)}, bf16[64,256]{1,0:T(8,128)(2,1)}, u32[]{:S(2)}, u32[]{:S(2)}) collective-permute-start(bf16[64,256]{1,0:T(8,128)(2,1)} %get-tuple-element.50), channel_id=1, source_target_pairs={{7,0},{0,1},{1,2},{2,3},{3,4},{4,5},{5,6},{6,7},{15,8},{8,9},{9,10... | collective-permute-start | bytes 98312 | tf_op jit(solution)/shard_map/ppermute | solution.py:37
  11.5 27.8 %collective-permute-start.1 = (bf16[64,256]{1,0:T(8,128)(2,1)}, bf16[64,256]{1,0:T(8,128)(2,1)}, u32[]{:S(2)}, u32[]{:S(2)}) collective-permute-start(bf16[64,256]{1,0:T(8,128)(2,1)} %get-tuple-element.51), channel_id=1, source_target_pairs={{1,0},{2,1},{3,2},{4,3},{5,4},{6,5},{7,6},{0,7},{9,8},{10,9},{11,1... | collective-permute-start | bytes 98312 | tf_op jit(solution)/shard_map/ppermute | solution.py:37
  15.6 23.7 %collective-permute-start.2 = (bf16[64,256]{1,0:T(8,128)(2,1)}, bf16[64,256]{1,0:T(8,128)(2,1)}, u32[]{:S(2)}, u32[]{:S(2)}) collective-permute-start(bf16[64,256]{1,0:T(8,128)(2,1)} %get-tuple-element.52), channel_id=1, source_target_pairs={{6,0},{7,1},{0,2},{1,3},{2,4},{3,5},{4,6},{5,7},{14,8},{15,9},{8,1... | collective-permute-start | bytes 98312 | tf_op jit(solution)/shard_map/ppermute | solution.py:37
  15.8 27.3 %collective-permute-start.3 = (bf16[64,256]{1,0:T(8,128)(2,1)}, bf16[64,256]{1,0:T(8,128)(2,1)}, u32[]{:S(2)}, u32[]{:S(2)}) collective-permute-start(bf16[64,256]{1,0:T(8,128)(2,1)} %get-tuple-element.53), channel_id=1, source_target_pairs={{2,0},{3,1},{4,2},{5,3},{6,4},{7,5},{0,6},{1,7},{10,8},{11,9},{12,... | collective-permute-start | bytes 98312 | tf_op jit(solution)/shard_map/ppermute | solution.py:37
  23.6 56.6 %collective-permute-start.4 = (bf16[256,512]{1,0:T(8,128)(2,1)S(1)}, bf16[256,512]{1,0:T(8,128)(2,1)S(1)}, u32[]{:S(2)}, u32[]{:S(2)}) collective-permute-start(bf16[256,512]{1,0:T(8,128)(2,1)S(1)} %get-tuple-element.47.after_ref), channel_id=1, source_target_pairs={{7,0},{0,1},{1,2},{2,3},{3,4},{4,5},{5,6},{6,7},{15,8},{8,9},{9,10... | collective-permute-start | bytes 786440 | tf_op jit(solution)/shard_map/ppermute | solution.py:37
  26.7 16.5 %copy-start.4 = (bf16[112,4096]{1,0:T(8,128)(2,1)S(1)}, bf16[112,4096]{1,0:T(8,128)(2,1)}, u32[]{:S(2)}) copy-start(bf16[112,4096]{1,0:T(8,128)(2,1)} %wb_ref.1) | copy-start | bytes 2752516
  35.7 44.5 %collective-permute-start.5 = (bf16[256,512]{1,0:T(8,128)(2,1)S(1)}, bf16[256,512]{1,0:T(8,128)(2,1)S(1)}, u32[]{:S(2)}, u32[]{:S(2)}) collective-permute-start(bf16[256,512]{1,0:T(8,128)(2,1)S(1)} %get-tuple-element.55), channel_id=1, source_target_pairs={{1,0},{2,1},{3,2},{4,3},{5,4},{6,5},{7,6},{0,7},{9,8},{10,9},{11,1... | collective-permute-start | bytes 786440 | tf_op jit(solution)/shard_map/ppermute | solution.py:37
  39.3 40.9 %collective-permute-start.6 = (bf16[256,512]{1,0:T(8,128)(2,1)S(1)}, bf16[256,512]{1,0:T(8,128)(2,1)S(1)}, u32[]{:S(2)}, u32[]{:S(2)}) collective-permute-start(bf16[256,512]{1,0:T(8,128)(2,1)S(1)} %get-tuple-element.56), channel_id=1, source_target_pairs={{6,0},{7,1},{0,2},{1,3},{2,4},{3,5},{4,6},{5,7},{14,8},{15,9},{8,1... | collective-permute-start | bytes 786440 | tf_op jit(solution)/shard_map/ppermute | solution.py:37
  39.3 40.9 %collective-permute-start.7 = (bf16[256,512]{1,0:T(8,128)(2,1)S(1)}, bf16[256,512]{1,0:T(8,128)(2,1)S(1)}, u32[]{:S(2)}, u32[]{:S(2)}) collective-permute-start(bf16[256,512]{1,0:T(8,128)(2,1)S(1)} %get-tuple-element.57), channel_id=1, source_target_pairs={{2,0},{3,1},{4,2},{5,3},{6,4},{7,5},{0,6},{1,7},{10,8},{11,9},{12,... | collective-permute-start | bytes 786440 | tf_op jit(solution)/shard_map/ppermute | solution.py:37
  43.1 3.4 %copy-start.16 = (bf16[32768,128]{1,0:T(8,128)(2,1)S(1)}, bf16[32768,128]{1,0:T(8,128)(2,1)}, u32[]{:S(2)}) copy-start(bf16[32768,128]{1,0:T(8,128)(2,1)} %copy-done.15) | copy-start | bytes 25165828
  49.2 31.0 %copy-start.7 = (bf16[2,64,512]{2,1,0:T(8,128)(2,1)S(1)}, bf16[2,64,512]{2,1,0:T(8,128)(2,1)}, u32[]{:S(2)}) copy-start(bf16[2,64,512]{2,1,0:T(8,128)(2,1)} %wu_ref.1) | copy-start | bytes 393220
  49.2 31.0 %copy-start.10 = (s32[1,1024]{1,0:T(1,128)S(1)}, s32[1,1024]{1,0:T(1,128)}, u32[]{:S(2)}) copy-start(s32[1,1024]{1,0:T(1,128)} %rev_ref.1) | copy-start | bytes 12292
  80.2 6.3 %copy-start.17 = (bf16[32768,128]{1,0:T(8,128)(2,1)S(1)}, bf16[32768,128]{1,0:T(8,128)(2,1)}, u32[]{:S(2)}) copy-start(bf16[32768,128]{1,0:T(8,128)(2,1)} %copy-done.15) | copy-start | bytes 25165828
  80.2 6.3 %copy-start.26 = (f32[128,256]{1,0:T(8,128)S(1)}, f32[128,256]{1,0:T(8,128)}, u32[]{:S(2)}) copy-start(f32[128,256]{1,0:T(8,128)} %copy-done.24) | copy-start | bytes 393220
  80.3 6.3 %copy-start.29 = (s32[128,256]{1,0:T(8,128)S(1)}, s32[128,256]{1,0:T(8,128)}, u32[]{:S(2)}) copy-start(s32[128,256]{1,0:T(8,128)} %copy-done.27) | copy-start | bytes 393220
  80.3 42.9 %slice-start = ((s8[16777216]{0:T(1024)(128)(4,1)}), s8[4194304]{0:T(1024)(128)(4,1)S(1)}, s32[]{:S(2)}) async-start(s8[16777216]{0:T(1024)(128)(4,1)} %bitcast.2), calls=%async_computation | async-start | bytes 8388608
  88.2 35.0 %slice-start.1 = ((s8[16777216]{0:T(1024)(128)(4,1)}), s8[4194304]{0:T(1024)(128)(4,1)S(1)}, s32[]{:S(2)}) async-start(s8[16777216]{0:T(1024)(128)(4,1)} %bitcast.2), calls=%async_computation.1 | async-start | bytes 8388608
  88.2 35.0 %slice-start.2 = ((s8[16777216]{0:T(1024)(128)(4,1)}), s8[4194304]{0:T(1024)(128)(4,1)S(1)}, s32[]{:S(2)}) async-start(s8[16777216]{0:T(1024)(128)(4,1)} %bitcast.2), calls=%async_computation.2 | async-start | bytes 8388608
  88.2 35.0 %slice-start.3 = ((s8[16777216]{0:T(1024)(128)(4,1)}), s8[4194304]{0:T(1024)(128)(4,1)S(1)}, s32[]{:S(2)}) async-start(s8[16777216]{0:T(1024)(128)(4,1)} %bitcast.2), calls=%async_computation.3 | async-start | bytes 8388608
  120.6 6.9 %collective-permute-start.10 = (bf16[64,256]{1,0:T(8,128)(2,1)S(1)}, bf16[64,256]{1,0:T(8,128)(2,1)S(1)}, u32[]{:S(2)}, u32[]{:S(2)}) collective-permute-start(bf16[64,256]{1,0:T(8,128)(2,1)S(1)} %get-tuple-element.66), channel_id=1, source_target_pairs={{2,0},{3,1},{4,2},{5,3},{6,4},{7,5},{0,6},{1,7},{10,8},{11,9},{12,... | collective-permute-start | bytes 98312 | tf_op jit(solution)/shard_map/ppermute | solution.py:37
  120.7 6.8 %collective-permute-start.11 = (bf16[64,256]{1,0:T(8,128)(2,1)S(1)}, bf16[64,256]{1,0:T(8,128)(2,1)S(1)}, u32[]{:S(2)}, u32[]{:S(2)}) collective-permute-start(bf16[64,256]{1,0:T(8,128)(2,1)S(1)} %get-tuple-element.67), channel_id=1, source_target_pairs={{6,0},{7,1},{0,2},{1,3},{2,4},{3,5},{4,6},{5,7},{14,8},{15,9},{8,1... | collective-permute-start | bytes 98312 | tf_op jit(solution)/shard_map/ppermute | solution.py:37
  122.7 4.8 %collective-permute-start.8 = (bf16[64,256]{1,0:T(8,128)(2,1)S(1)}, bf16[64,256]{1,0:T(8,128)(2,1)S(1)}, u32[]{:S(2)}, u32[]{:S(2)}) collective-permute-start(bf16[64,256]{1,0:T(8,128)(2,1)S(1)} %get-tuple-element.64), channel_id=1, source_target_pairs={{1,0},{2,1},{3,2},{4,3},{5,4},{6,5},{7,6},{0,7},{9,8},{10,9},{11,1... | collective-permute-start | bytes 98312 | tf_op jit(solution)/shard_map/ppermute | solution.py:37
  122.7 5.1 %collective-permute-start.9 = (bf16[64,256]{1,0:T(8,128)(2,1)S(1)}, bf16[64,256]{1,0:T(8,128)(2,1)S(1)}, u32[]{:S(2)}, u32[]{:S(2)}) collective-permute-start(bf16[64,256]{1,0:T(8,128)(2,1)S(1)} %get-tuple-element.65), channel_id=1, source_target_pairs={{7,0},{0,1},{1,2},{2,3},{3,4},{4,5},{5,6},{6,7},{15,8},{8,9},{9,10... | collective-permute-start | bytes 98312 | tf_op jit(solution)/shard_map/ppermute | solution.py:37
  123.2 4.6 %copy-start.3 = (bf16[1,1024,512]{2,1,0:T(8,128)(2,1)S(1)}, bf16[1,1024,512]{2,1,0:T(8,128)(2,1)}, u32[]{:S(2)}) copy-start(bf16[1,1024,512]{2,1,0:T(8,128)(2,1)} %x_ref.3) | copy-start | bytes 3145732
  123.2 4.6 %copy-start.6 = (bf16[512,512]{1,0:T(8,128)(2,1)S(1)}, bf16[512,512]{1,0:T(8,128)(2,1)}, u32[]{:S(2)}) copy-start(bf16[512,512]{1,0:T(8,128)(2,1)} %we_ref.3) | copy-start | bytes 1572868
  123.2 4.6 %copy-start.9 = (bf16[512,64]{0,1:T(8,128)(2,1)S(1)}, bf16[512,64]{0,1:T(8,128)(2,1)}, u32[]{:S(2)}) copy-start(bf16[512,64]{0,1:T(8,128)(2,1)} %param.16) | copy-start | bytes 196612
  123.2 4.6 %copy-start.19 = (f32[1024,512]{1,0:T(8,128)S(1)}, f32[1024,512]{1,0:T(8,128)}, u32[]{:S(2)}) copy-start(f32[1024,512]{1,0:T(8,128)} %copy-done.18) | copy-start | bytes 6291460
  123.2 4.6 %copy-start.21 = (bf16[1024,512]{1,0:T(8,128)(2,1)S(1)}, bf16[1024,512]{1,0:T(8,128)(2,1)}, u32[]{:S(2)}) copy-start(bf16[1024,512]{1,0:T(8,128)(2,1)} %copy-done.20) | copy-start | bytes 3145732
  123.3 4.6 %copy-start.23 = (f32[64,1024]{1,0:T(8,128)S(1)}, f32[64,1024]{1,0:T(8,128)}, u32[]{:S(2)}) copy-start(f32[64,1024]{1,0:T(8,128)} %copy-done.22) | copy-start | bytes 786436
  127.4 6.4 %collective-permute-start.12 = (bf16[4,64,1152]{2,1,0:T(8,128)(2,1)S(1)}, bf16[4,64,1152]{2,1,0:T(8,128)(2,1)S(1)}, u32[]{:S(2)}, u32[]{:S(2)}) collective-permute-start(bf16[4,64,1152]{2,1,0:T(8,128)(2,1)S(1)} %get-tuple-element.72), channel_id=1, source_target_pairs={{0,1},{1,0},{2,3},{3,2},{4,5},{5,4},{6,7},{7,6},{8,9},{9,8},{10,11... | collective-permute-start | bytes 1769480 | tf_op jit(solution)/shard_map/ppermute | solution.py:672
  132.0 1.6 collective-permute-start.19
  133.8 7.3 %collective-permute-start.20 = (bf16[64,640]{1,0:T(8,128)(2,1)S(1)}, bf16[64,640]{1,0:T(8,128)(2,1)S(1)}, u32[]{:S(2)}, u32[]{:S(2)}) collective-permute-start(bf16[64,640]{1,0:T(8,128)(2,1)S(1)} %get-tuple-element.80), channel_id=1, source_target_pairs={{0,2},{1,3},{2,4},{3,5},{4,6},{5,7},{6,0},{7,1},{8,10},{9,11},{10,... | collective-permute-start | bytes 245768 | tf_op jit(solution)/shard_map/ppermute | solution.py:683
  134.0 24.6 %collective-permute-start.13 = (bf16[64,1152]{1,0:T(8,128)(2,1)S(1)}, bf16[64,1152]{1,0:T(8,128)(2,1)S(1)}, u32[]{:S(2)}, u32[]{:S(2)}) collective-permute-start(bf16[64,1152]{1,0:T(8,128)(2,1)S(1)} %get-tuple-element.74), channel_id=1, source_target_pairs={{0,2},{1,3},{2,4},{3,5},{4,6},{5,7},{6,0},{7,1},{8,10},{9,11},{10,... | collective-permute-start | bytes 442376 | tf_op jit(solution)/shard_map/ppermute | solution.py:683
  136.3 22.3 %collective-permute-start.14 = (bf16[64,1152]{1,0:T(8,128)(2,1)S(1)}, bf16[64,1152]{1,0:T(8,128)(2,1)S(1)}, u32[]{:S(2)}, u32[]{:S(2)}) collective-permute-start(bf16[64,1152]{1,0:T(8,128)(2,1)S(1)} %get-tuple-element.75), channel_id=1, source_target_pairs={{0,4},{1,5},{2,6},{3,7},{4,0},{5,1},{6,2},{7,3},{8,12},{9,13},{10,... | collective-permute-start | bytes 442376 | tf_op jit(solution)/shard_map/ppermute | solution.py:683
  138.4 20.2 %collective-permute-start.15 = (bf16[64,1152]{1,0:T(8,128)(2,1)S(1)}, bf16[64,1152]{1,0:T(8,128)(2,1)S(1)}, u32[]{:S(2)}, u32[]{:S(2)}) collective-permute-start(bf16[64,1152]{1,0:T(8,128)(2,1)S(1)} %get-tuple-element.76), channel_id=1, source_target_pairs={{0,6},{1,7},{2,0},{3,1},{4,2},{5,3},{6,4},{7,5},{8,14},{9,15},{10,... | collective-permute-start | bytes 442376 | tf_op jit(solution)/shard_map/ppermute | solution.py:683
  140.7 15.9 %collective-permute-start.21 = (bf16[64,640]{1,0:T(8,128)(2,1)S(1)}, bf16[64,640]{1,0:T(8,128)(2,1)S(1)}, u32[]{:S(2)}, u32[]{:S(2)}) collective-permute-start(bf16[64,640]{1,0:T(8,128)(2,1)S(1)} %get-tuple-element.81), channel_id=1, source_target_pairs={{0,4},{1,5},{2,6},{3,7},{4,0},{5,1},{6,2},{7,3},{8,12},{9,13},{10,... | collective-permute-start | bytes 245768 | tf_op jit(solution)/shard_map/ppermute | solution.py:683
  141.1 15.4 %collective-permute-start.22 = (bf16[64,640]{1,0:T(8,128)(2,1)S(1)}, bf16[64,640]{1,0:T(8,128)(2,1)S(1)}, u32[]{:S(2)}, u32[]{:S(2)}) collective-permute-start(bf16[64,640]{1,0:T(8,128)(2,1)S(1)} %get-tuple-element.82), channel_id=1, source_target_pairs={{0,6},{1,7},{2,0},{3,1},{4,2},{5,3},{6,4},{7,5},{8,14},{9,15},{10,... | collective-permute-start | bytes 245768 | tf_op jit(solution)/shard_map/ppermute | solution.py:683
  156.6 7.2 %collective-permute-start.23 = (bf16[64,640]{1,0:T(8,128)(2,1)S(1)}, bf16[64,640]{1,0:T(8,128)(2,1)S(1)}, u32[]{:S(2)}, u32[]{:S(2)}) collective-permute-start(bf16[64,640]{1,0:T(8,128)(2,1)S(1)} %shard_map.158.refs_4_), channel_id=1, source_target_pairs={{0,8},{8,0},{16,24},{24,16},{1,9},{9,1},{17,25},{25,17},{2,10},{10... | collective-permute-start | bytes 245768 | tf_op jit(solution)/shard_map/ppermute | solution.py:697
  158.7 12.5 %collective-permute-start.16 = (bf16[64,1152]{1,0:T(8,128)(2,1)S(1)}, bf16[64,1152]{1,0:T(8,128)(2,1)S(1)}, u32[]{:S(2)}, u32[]{:S(2)}) collective-permute-start(bf16[64,1152]{1,0:T(8,128)(2,1)S(1)} %shard_map.156.refs_0_), channel_id=1, source_target_pairs={{0,8},{8,0},{16,24},{24,16},{1,9},{9,1},{17,25},{25,17},{2,10},{10... | collective-permute-start | bytes 442376 | tf_op jit(solution)/shard_map/ppermute | solution.py:697
  158.8 12.4 %collective-permute-start.17 = (bf16[64,1152]{1,0:T(8,128)(2,1)S(1)}, bf16[64,1152]{1,0:T(8,128)(2,1)S(1)}, u32[]{:S(2)}, u32[]{:S(2)}) collective-permute-start(bf16[64,1152]{1,0:T(8,128)(2,1)S(1)} %shard_map.156.refs_0_), channel_id=1, source_target_pairs={{0,16},{8,24},{16,0},{24,8},{1,17},{9,25},{17,1},{25,9},{2,18},{10... | collective-permute-start | bytes 442376 | tf_op jit(solution)/shard_map/ppermute | solution.py:697
  160.9 10.3 %collective-permute-start.18 = (bf16[64,1152]{1,0:T(8,128)(2,1)S(1)}, bf16[64,1152]{1,0:T(8,128)(2,1)S(1)}, u32[]{:S(2)}, u32[]{:S(2)}) collective-permute-start(bf16[64,1152]{1,0:T(8,128)(2,1)S(1)} %shard_map.156.refs_0_), channel_id=1, source_target_pairs={{0,24},{8,16},{16,8},{24,0},{1,25},{9,17},{17,9},{25,1},{2,26},{10... | collective-permute-start | bytes 442376 | tf_op jit(solution)/shard_map/ppermute | solution.py:697
  162.3 8.9 %collective-permute-start.24 = (bf16[64,640]{1,0:T(8,128)(2,1)S(1)}, bf16[64,640]{1,0:T(8,128)(2,1)S(1)}, u32[]{:S(2)}, u32[]{:S(2)}) collective-permute-start(bf16[64,640]{1,0:T(8,128)(2,1)S(1)} %shard_map.158.refs_4_), channel_id=1, source_target_pairs={{0,16},{8,24},{16,0},{24,8},{1,17},{9,25},{17,1},{25,9},{2,18},{10... | collective-permute-start | bytes 245768 | tf_op jit(solution)/shard_map/ppermute | solution.py:697
  163.8 7.4 %collective-permute-start.25 = (bf16[64,640]{1,0:T(8,128)(2,1)S(1)}, bf16[64,640]{1,0:T(8,128)(2,1)S(1)}, u32[]{:S(2)}, u32[]{:S(2)}) collective-permute-start(bf16[64,640]{1,0:T(8,128)(2,1)S(1)} %shard_map.158.refs_4_), channel_id=1, source_target_pairs={{0,24},{8,16},{16,8},{24,0},{1,25},{9,17},{17,9},{25,1},{2,26},{10... | collective-permute-start | bytes 245768 | tf_op jit(solution)/shard_map/ppermute | solution.py:697
  (17 other events, 21.0 us)

commit v4 on v3

--- a/solution.py
+++ b/solution.py
@@ -103,7 +103,7 @@
         + (jax.ShapeDtypeStruct((narrow, capacity), bf16),) * lists,
         in_specs=[smem()] + [vmem()] * 4,
         out_specs=(vmem(),) * (4 + lists),
-        compiler_params=params(),
+        compiler_params=params(56),
         cost_estimate=cost(edges, 3),
         name="front",
     )(counts, messages, w_edge, w_down, rows)
@@ -143,7 +143,7 @@
         + (jax.ShapeDtypeStruct((capacity, model), bf16),) * lists,
         in_specs=[smem(), vmem(), vmem(), vmem(), pl.BlockSpec(memory_space=pl.ANY)],
         out_specs=(vmem(),) * (2 + lists),
-        compiler_params=params(),
+        compiler_params=params(12),
         cost_estimate=cost(edges, 3),
         name="pick",
     )(counts, cotangent, rows, trips, after)
@@ -217,6 +217,12 @@
         cost_estimate=cost(edges, 6),
         name="align",
     )(after, triplet_basis)
+
+
+def halves(bas):
+    first = iota(bas.shape, 0) % GROUP < GROUP // 2
+    zero = jnp.zeros_like(bas)
+    return jnp.concatenate([jnp.where(first, bas, zero), jnp.where(first, zero, bas)], axis=1)
 
 
 def forward_kernel(sub, lists, bas_ref, low_ref, high_ref, red_ref, wb_ref, *rest):
@@ -466,19 +472,20 @@
 
 def own_rows(mixed, narrow):
     rho = mixed.shape[1]
-    value = mixed.reshape(narrow // GROUP, GROUP, GROUP, rho)
+    half = GROUP // 2
+    value = mixed.reshape(narrow // GROUP, half, GROUP, rho)
     shape = (1, 1, GROUP, rho)
     row, lane = iota(shape, 2), iota(shape, 3)
-    step = GROUP // 2
+    step = half // 2
     while step:
         low, high = value[:, :step], value[:, step:]
         upper = jnp.bitwise_and(row, step) > 0
         kept = jnp.bitwise_and(row, step) == jnp.bitwise_and(lane, step)
         straight = jnp.where(upper, high, low)
         other = jnp.where(upper, low, high)
-        moved = pltpu.roll(other, step, 2)
-        if 2 * step != GROUP:
-            moved = jnp.where(upper, moved, pltpu.roll(other, GROUP - step, 2))
+        moved = jnp.where(
+            upper, pltpu.roll(other, step, 2), pltpu.roll(other, GROUP - step, 2)
+        )
         value = jnp.where(kept, straight, moved)
         step //= 2
     return value.reshape(narrow, rho)
@@ -499,20 +506,27 @@
         num_s[...] = low_iota(capacity, rho)
 
     grad_state = grad_ref[...]
-    height = narrow * GROUP
-
-    def spread(pair, carry):
-        start = pl.multiple_of(pair * 2 * padded, 2 * padded)
-        grad = mm(grad_state, wide[pl.ds(start, 2 * padded), :], NT)
+    half = GROUP // 2
+    height = narrow * half
+    top = iota((GROUP, 1), 0) < half
+
+    def spread(tile, carry):
+        start = pl.multiple_of(tile * GROUP * padded, GROUP * padded)
+        grad = mm(grad_state, wide[pl.ds(start, GROUP * padded), :], NT)
         for g in range(block // GROUP):
             part = slice(g * GROUP, (g + 1) * GROUP)
-            at = pl.multiple_of(g * height + pair * 2 * GROUP, 2 * GROUP)
-            turn_s[pl.ds(at, 2 * GROUP), :] = jnp.concatenate(
-                [grad[part, :padded], grad[part, padded:]], axis=0
-            ).astype(bf16)
+            sides = []
+            for c in range(half):
+                near = grad[part, c * padded : (c + 1) * padded]
+                far = grad[part, (c + half) * padded : (c + half + 1) * padded]
+                left = jnp.where(top, near, pltpu.roll(far, half, 0))
+                right = jnp.where(top, pltpu.roll(near, half, 0), far)
+                sides.append(jnp.concatenate([left, right], axis=1))
+            at = pl.multiple_of(g * height + tile * GROUP * half, GROUP * half)
+            turn_s[pl.ds(at, GROUP * half), :] = jnp.concatenate(sides, axis=0).astype(bf16)
         return carry
 
-    lax.fori_loop(0, narrow // 2, spread, 0, unroll=8)
+    lax.fori_loop(0, narrow // GROUP, spread, 0, unroll=2)
     groups = sub // GROUP
 
     def body(index, carry):
@@ -522,7 +536,7 @@
             here = first_group + g
             bas = bas_ref[pl.ds(pl.multiple_of(here * rho, rho), rho), :]
             grads = turn_s[pl.ds(pl.multiple_of(here * height, height), height), :]
-            return mm(grads, bas, NT)
+            return mm(grads, halves(bas), NT)
 
         def cast(g, mixed):
             trip_grad = own_rows(mixed, narrow).astype(bf16)
@@ -581,7 +595,7 @@
         out_specs=(resident(home, capacity),) + (resident(narrow, capacity),) * lists,
         scratch_shapes=[
             pltpu.VMEM((rows, capacity), f32),
-            pltpu.VMEM((block * narrow, padded), bf16),
+            pltpu.VMEM((block * narrow // 2, 2 * padded), bf16),
             pltpu.VMEM((rows, sub // GROUP * rho), bf16),
             pltpu.VMEM((capacity, sub // GROUP * rho), bf16),
             pltpu.VMEM((capacity, rho), bf16),

time: 173 us -> 165 us (0.954)
  local copies, waits for them, and re-layouts: 24.7 us -> 18 us
    unnamed x79 -> x63, local copies, waits for them, and re-layouts: 24.7 us -> 18 us
    pallas_call x1, Pallas kernels: 32.4 us -> 29.7 us  [backward(): pl.pallas_call(functools.partial(backward_kernel, sub, lists), grid=(edge...]
  transfers between devices with their start and end apart: 26 -> 26, of which waited for: 5 -> 5; matrix products, arithmetic and copies ran while one was open for 0% -> 0% of each run, Pallas kernels for 27% -> 28%
where the time goes in v4:
time: 165 us
  Pallas kernels  87.4 us (53%)
  starting transfers between devices  35.3 us (21%)
  waiting for transfers between devices  22.2 us (13%)
  local copies, waits for them, and re-layouts  18 us (11%)
  between operations  1.71 us (1%)
    pallas_call x1, Pallas kernels, backward(): pl.pallas_call(functools.partial(backward_kernel, sub, lists), grid=(edge...  29.7 us
    pallas_call x1, Pallas kernels, forward(): pl.pallas_call(functools.partial(forward_kernel, sub, lists), grid=(edges...  29.5 us
    ppermute x12, starting transfers between devices, shifted(): return lax.ppermute(block, axis, route)  18.4 us
    unnamed x63, local copies, waits for them, and re-layouts  18 us
    ppermute x6, waiting for transfers between devices, over_graph(): arrived.append(lax.ppermute(send, 'graph', route))  14.2 us
    ppermute x6, starting transfers between devices, over_graph(): arrived.append(lax.ppermute(send, 'graph', route))  8.41 us
    ppermute x6, starting transfers between devices, over_dp(): lax.ppermute(share, 'dp', [(i, i ^ step) for i in range(slabs)])  8.17 us
    ppermute x6, waiting for transfers between devices, over_dp(): lax.ppermute(share, 'dp', [(i, i ^ step) for i in range(slabs)])  6.29 us
  transfers between devices with their start and end apart: 26, of which 5 were waited for; matrix products, arithmetic and copies ran while one was open for 0% of the time, Pallas kernels for 28%

profile of v4, /device:TPU:0, one launch (start us, length us, event | category | flops | bytes accessed | tf_op | source)
XLA Modules:
  0.0 164.6 jit_solution(6350744913732811815)
XLA Ops:
  0.7 4.6 %front.1 = (f32[1024,512]{1,0:T(8,128)}, bf16[1024,512]{1,0:T(8,128)(2,1)}, f32[64,1024]{1,0:T(8,128)}, bf16[64,1024]{1,0:T(8,128)(2,1)}, bf16[64,256]{1,0:T(8,1...) custom-call(s32[1,4]{1,0:T(1,128)} %count_ref.6, ...), custom_call_target="tpu_custom_call" | custom-call | flops 3072000000 | bytes 3072000 | tf_op jit(solution)/shard_map/front/pallas_call | solution.py:95
  5.2 0.5 collective-permute-start
  5.7 4.1 %collective-permute-start.1 = (bf16[64,256]{1,0:T(8,128)(2,1)}, bf16[64,256]{1,0:T(8,128)(2,1)}, u32[]{:S(2)}, u32[]{:S(2)}) collective-permute-start(bf16[64,256]{1,0:T(8,128)(2,1)} %get-tuple-element.51), channel_id=1, source_target_pairs={{1,0},{2,1},{3,2},{4,3},{5,4},{6,5},{7,6},{0,7},{9,8},{10,9},{11,1... | collective-permute-start | bytes 98312 | tf_op jit(solution)/shard_map/ppermute | solution.py:37
  9.8 0.2 collective-permute-start.2
  10.0 3.6 %collective-permute-start.3 = (bf16[64,256]{1,0:T(8,128)(2,1)}, bf16[64,256]{1,0:T(8,128)(2,1)}, u32[]{:S(2)}, u32[]{:S(2)}) collective-permute-start(bf16[64,256]{1,0:T(8,128)(2,1)} %get-tuple-element.53), channel_id=1, source_target_pairs={{2,0},{3,1},{4,2},{5,3},{6,4},{7,5},{0,6},{1,7},{10,8},{11,9},{12,... | collective-permute-start | bytes 98312 | tf_op jit(solution)/shard_map/ppermute | solution.py:37
  13.6 0.2 copy.17.trip_ref
  13.9 0.9 copy-done.22
  14.8 2.6 %pick.1 = (f32[128,256]{1,0:T(8,128)S(1)}, s32[128,256]{1,0:T(8,128)S(1)}, bf16[256,512]{1,0:T(8,128)(2,1)S(1)}, bf16[256,512]{1,0:T(8,128)(2,1)S(1)}, bf16[256,...) custom-call(s32[1,4]{1,0:T(1,128)S(1)} %copy-done.9, bf16[1,1024,512]{2,1,0:T(8,128)(2,1)S(1)} %copy-done.1, ...), custom_call_target="tpu_custom_call" | custom-call | flops 3072000000 | bytes 3072000 | tf_op jit(solution)/shard_map/pick/pallas_call | solution.py:137
  17.4 0.6 copy-done.16
  18.1 0.7 copy-done.19
  18.7 3.1 %copy-done = bf16[1,1024,3584]{2,1,0:T(8,128)(2,1)S(1)} copy-done((bf16[1,1024,3584]{2,1,0:T(8,128)(2,1)S(1)}, bf16[1,1024,3584]{2,1,0:T(8,128)(2,1)}, u32[]{:S(2)}) %copy-start) | copy-done | bytes 7340056
  21.8 5.0 %align.1.bas_ref = bf16[32768,128]{1,0:T(8,128)(2,1)S(1)} custom-call(bf16[256,512]{1,0:T(8,128)(2,1)S(1)} %get-tuple-element.47.after_ref, bf16[1,1024,3584]{2,1,0:T(8,128)(2,1)S(1)} %copy-done), custom_call_target="tpu_custom_call" | custom-call | flops 6144000000 | bytes 6144000 | tf_op jit(solution)/shard_map/align/pallas_call | solution.py:206
  26.8 3.3 %copy-done.10 = bf16[32768,128]{1,0:T(8,128)(2,1)} copy-done((bf16[32768,128]{1,0:T(8,128)(2,1)}, bf16[32768,128]{1,0:T(8,128)(2,1)S(1)}, u32[]{:S(2)}) %copy-start.10) | copy-done | bytes 8388632
  30.8 3.6 %collective-permute-start.5 = (bf16[256,512]{1,0:T(8,128)(2,1)S(1)}, bf16[256,512]{1,0:T(8,128)(2,1)S(1)}, u32[]{:S(2)}, u32[]{:S(2)}) collective-permute-start(bf16[256,512]{1,0:T(8,128)(2,1)S(1)} %get-tuple-element.55), channel_id=1, source_target_pairs={{1,0},{2,1},{3,2},{4,3},{5,4},{6,5},{7,6},{0,7},{9,8},{10,9},{11,1... | collective-permute-start | bytes 786440 | tf_op jit(solution)/shard_map/ppermute | solution.py:37
  34.4 3.8 %collective-permute-start.7 = (bf16[256,512]{1,0:T(8,128)(2,1)S(1)}, bf16[256,512]{1,0:T(8,128)(2,1)S(1)}, u32[]{:S(2)}, u32[]{:S(2)}) collective-permute-start(bf16[256,512]{1,0:T(8,128)(2,1)S(1)} %get-tuple-element.57), channel_id=1, source_target_pairs={{2,0},{3,1},{4,2},{5,3},{6,4},{7,5},{0,6},{1,7},{10,8},{11,9},{12,... | collective-permute-start | bytes 786440 | tf_op jit(solution)/shard_map/ppermute | solution.py:37
  38.2 3.4 %copy-done.11 = bf16[32768,128]{1,0:T(8,128)(2,1)S(1)} copy-done((bf16[32768,128]{1,0:T(8,128)(2,1)S(1)}, bf16[32768,128]{1,0:T(8,128)(2,1)}, u32[]{:S(2)}) %copy-start.11) | copy-done | bytes 8388632
  41.6 0.9 copy-done.17
  42.5 0.9 copy-done.20
  43.4 0.9 copy-done.23
  44.3 29.5 %forward.1 = (bf16[1024,8192]{1,0:T(8,128)(2,1)}, bf16[1024,64]{1,0:T(8,128)(2,1)S(1)}, bf16[8192,64]{1,0:T(8,128)(2,1)S(1)}) custom-call(bf16[32768,128]{1,0:T(8,128)(2,1)S(1)} %copy-done.11, f32[128,256]{1,0:T(8,128)S(1)} %copy-done.17, s32[128,256]{1,0:T(8,128)S(1)} %copy-done.20, bf16[64,1024]{1,0:T(8,128)(2,1)S(1)} %copy-done.23, ...), custom_call_target="tpu_custom_call" | custom-call | flops 29696000000 | bytes 29696000 | tf_op jit(solution)/shard_map/forward/pallas_call | solution.py:303
  73.8 1.4 copy-done.24
  75.3 6.2 %state_grads.1 = (bf16[1024,64]{1,0:T(8,128)(2,1)S(1)}, f32[64,1024]{1,0:T(8,128)S(1)}) custom-call(s32[1,1]{1,0:T(1,128)S(6)} %copy.18.count_ref, bf16[1024,64]{1,0:T(8,128)(2,1)S(1)} %get-tuple-element.54.state_ref, bf16[1,1024,512]{2,1,0:T(8,128)(2,1)S(1)} %copy-done.1, s32[1,1024]{1,0:T(1,128)S(1)} %copy-done.7, bf16[1,1024,512]{2,1,0:T(8,128)(2,1)S(1)} %copy-done.1, ...), custom_call_target="tpu_custom_call" | custom-call | flops 7168000000 | bytes 7168000 | tf_op jit(solution)/shard_map/state_grads/pallas_call | solution.py:383
  81.6 1.6 copy-done.25
  83.2 29.7 %backward.1 = (f32[256,256]{1,0:T(8,128)S(1)}, bf16[64,256]{1,0:T(8,128)(2,1)S(1)}, bf16[64,256]{1,0:T(8,128)(2,1)S(1)}, bf16[64,256]{1,0:T(8,128)(2,1)S(1)}, bf16[64,256]{1,0:T(8,128)(2,1)S(1)}) custom-call(bf16[32768,128]{1,0:T(8,128)(2,1)S(1)} %copy-done.12, bf16[1024,64]{1,0:T(8,128)(2,1)S(1)} %get-tuple-element.58.grad_ref, f32[128,256]{1,0:T(8,128)S(1)} %copy-done.18, ...), custom_call_target="tpu_custom_call" | custom-call | flops 32768000000 | bytes 32768000 | tf_op jit(solution)/shard_map/backward/pallas_call | solution.py:583
  113.0 2.0 %collective-permute-start.11 = (bf16[64,256]{1,0:T(8,128)(2,1)S(1)}, bf16[64,256]{1,0:T(8,128)(2,1)S(1)}, u32[]{:S(2)}, u32[]{:S(2)}) collective-permute-start(bf16[64,256]{1,0:T(8,128)(2,1)S(1)} %get-tuple-element.67), channel_id=1, source_target_pairs={{6,0},{7,1},{0,2},{1,3},{2,4},{3,5},{4,6},{5,7},{14,8},{15,9},{8,1... | collective-permute-start | bytes 98312 | tf_op jit(solution)/shard_map/ppermute | solution.py:37
  115.0 0.5 collective-permute-start.9
  115.6 4.1 %bil_shares.1 = (bf16[4,64,1152]{2,1,0:T(8,128)(2,1)S(1)}, bf16[4,64,1152]{2,1,0:T(8,128)(2,1)S(1)}) custom-call(s32[1,1]{1,0:T(1,128)S(6)} %select_n.12.core_ref, bf16[1024,8192]{1,0:T(8,128)(2,1)S(1)} %bitcast.3, bf16[1024,64]{1,0:T(8,128)(2,1)S(1)} %get-tuple-element.58.grad_ref, f32[64,1024]{1,0:T(8,128)S(1)} %get-tuple-element.70.up_ref), custom_call_target="tpu_custom_call" | custom-call | flops 4096000000 | bytes 4096000 | tf_op jit(solution)/shard_map/bil_shares/pallas_call | solution.py:455
  119.7 0.1 collective-permute-start.12
  119.8 0.3 collective-permute-done.9.rest_1_
  120.2 4.2 %tail.1 = (bf16[1,1024,512]{2,1,0:T(8,128)(2,1)}, bf16[4,64,640]{2,1,0:T(8,128)(2,1)S(1)}, bf16[4,64,640]{2,1,0:T(8,128)(2,1)S(1)}) custom-call(s32[1,4]{1,0:T(1,128)S(1)} %copy-done.9, s32[1,1]{1,0:T(1,128)S(6)} %select_n.12.core_ref, f32[256,256]{1,0:T(8,128)S(1)} %get-tuple-element.60.pool_ref, s32[1,4,256]{2,1,0:T(4,128)S(1)} %copy-done.8, ...), custom_call_target="tpu_custom_call" | custom-call | flops 4096000000 | bytes 4096000 | tf_op jit(solution)/shard_map/tail/pallas_call | solution.py:650
  124.3 0.2 collective-permute-start.19
  124.6 1.4 collective-permute-done.19.got_ref
  126.0 0.1 shard_map.157
  126.2 0.1 shard_map.155
  126.3 2.3 %collective-permute-start.13 = (bf16[64,1152]{1,0:T(8,128)(2,1)S(1)}, bf16[64,1152]{1,0:T(8,128)(2,1)S(1)}, u32[]{:S(2)}, u32[]{:S(2)}) collective-permute-start(bf16[64,1152]{1,0:T(8,128)(2,1)S(1)} %get-tuple-element.74), channel_id=1, source_target_pairs={{0,2},{1,3},{2,4},{3,5},{4,6},{5,7},{6,0},{7,1},{8,10},{9,11},{10,... | collective-permute-start | bytes 442376 | tf_op jit(solution)/shard_map/ppermute | solution.py:697
  128.6 2.1 %collective-permute-start.14 = (bf16[64,1152]{1,0:T(8,128)(2,1)S(1)}, bf16[64,1152]{1,0:T(8,128)(2,1)S(1)}, u32[]{:S(2)}, u32[]{:S(2)}) collective-permute-start(bf16[64,1152]{1,0:T(8,128)(2,1)S(1)} %get-tuple-element.75), channel_id=1, source_target_pairs={{0,4},{1,5},{2,6},{3,7},{4,0},{5,1},{6,2},{7,3},{8,12},{9,13},{10,... | collective-permute-start | bytes 442376 | tf_op jit(solution)/shard_map/ppermute | solution.py:697
  130.7 2.2 %collective-permute-start.15 = (bf16[64,1152]{1,0:T(8,128)(2,1)S(1)}, bf16[64,1152]{1,0:T(8,128)(2,1)S(1)}, u32[]{:S(2)}, u32[]{:S(2)}) collective-permute-start(bf16[64,1152]{1,0:T(8,128)(2,1)S(1)} %get-tuple-element.76), channel_id=1, source_target_pairs={{0,6},{1,7},{2,0},{3,1},{4,2},{5,3},{6,4},{7,5},{8,14},{9,15},{10,... | collective-permute-start | bytes 442376 | tf_op jit(solution)/shard_map/ppermute | solution.py:697
  133.0 0.5 collective-permute-done.20.refs_1_
  133.4 1.7 %collective-permute-start.22 = (bf16[64,640]{1,0:T(8,128)(2,1)S(1)}, bf16[64,640]{1,0:T(8,128)(2,1)S(1)}, u32[]{:S(2)}, u32[]{:S(2)}) collective-permute-start(bf16[64,640]{1,0:T(8,128)(2,1)S(1)} %get-tuple-element.82), channel_id=1, source_target_pairs={{0,6},{1,7},{2,0},{3,1},{4,2},{5,3},{6,4},{7,5},{8,14},{9,15},{10,... | collective-permute-start | bytes 245768 | tf_op jit(solution)/shard_map/ppermute | solution.py:697
  135.1 13.7 %collective-permute-done.21.refs_2_ = bf16[64,640]{1,0:T(8,128)(2,1)S(1)} collective-permute-done((bf16[64,640]{1,0:T(8,128)(2,1)S(1)}, bf16[64,640]{1,0:T(8,128)(2,1)S(1)}, u32[]{:S(2)}, u32[]{:S(2)}) %collective-permute-start.21) | collective-permute-done | bytes 81952 | tf_op jit(solution)/shard_map/ppermute | solution.py:697
  148.9 2.0 %collective-permute-start.23 = (bf16[64,640]{1,0:T(8,128)(2,1)S(1)}, bf16[64,640]{1,0:T(8,128)(2,1)S(1)}, u32[]{:S(2)}, u32[]{:S(2)}) collective-permute-start(bf16[64,640]{1,0:T(8,128)(2,1)S(1)} %shard_map.158.refs_4_), channel_id=1, source_target_pairs={{0,8},{8,0},{16,24},{24,16},{1,9},{9,1},{17,25},{25,17},{2,10},{10... | collective-permute-start | bytes 245768 | tf_op jit(solution)/shard_map/ppermute | solution.py:711
  151.0 0.1 collective-permute-start.16
  151.1 2.0 %collective-permute-start.17 = (bf16[64,1152]{1,0:T(8,128)(2,1)S(1)}, bf16[64,1152]{1,0:T(8,128)(2,1)S(1)}, u32[]{:S(2)}, u32[]{:S(2)}) collective-permute-start(bf16[64,1152]{1,0:T(8,128)(2,1)S(1)} %shard_map.156.refs_0_), channel_id=1, source_target_pairs={{0,16},{8,24},{16,0},{24,8},{1,17},{9,25},{17,1},{25,9},{2,18},{10... | collective-permute-start | bytes 442376 | tf_op jit(solution)/shard_map/ppermute | solution.py:711
  153.1 1.4 collective-permute-start.18
  154.5 1.5 collective-permute-start.24
  156.1 1.1 collective-permute-start.25
  157.2 6.3 %collective-permute-done.24.refs_6_ = bf16[64,640]{1,0:T(8,128)(2,1)S(1)} collective-permute-done((bf16[64,640]{1,0:T(8,128)(2,1)S(1)}, bf16[64,640]{1,0:T(8,128)(2,1)S(1)}, u32[]{:S(2)}, u32[]{:S(2)}) %collective-permute-start.24) | collective-permute-done | bytes 81952 | tf_op jit(solution)/shard_map/ppermute | solution.py:711
  163.5 1.1 finish.1
  (81 shorter events, 0.4 us)
Async XLA Ops:
  0.6 13.2 %copy-start.8 = (s32[1,4,256]{2,1,0:T(4,128)S(1)}, s32[1,4,256]{2,1,0:T(4,128)}, u32[]{:S(2)}) copy-start(s32[1,4,256]{2,1,0:T(4,128)} %rows_ref.5) | copy-start | bytes 12292
  0.6 13.2 %copy-start.9 = (s32[1,4]{1,0:T(1,128)S(1)}, s32[1,4]{1,0:T(1,128)}, u32[]{:S(2)}) copy-start(s32[1,4]{1,0:T(1,128)} %count_ref.6) | copy-start | bytes 52
  0.7 13.0 %copy-start.26 = (s32[1,1024,32]{1,2,0:T(8,128)S(1)}, s32[1,1024,32]{1,2,0:T(8,128)}, u32[]{:S(2)}) copy-start(s32[1,1024,32]{1,2,0:T(8,128)} %param.19) | copy-start | bytes 393220
  0.7 13.2 %copy-start.1 = (bf16[1,1024,512]{2,1,0:T(8,128)(2,1)S(1)}, bf16[1,1024,512]{2,1,0:T(8,128)(2,1)}, u32[]{:S(2)}) copy-start(bf16[1,1024,512]{2,1,0:T(8,128)(2,1)} %own_ref.1) | copy-start | bytes 3145732
  5.2 25.6 %collective-permute-start = (bf16[64,256]{1,0:T(8,128)(2,1)}, bf16[64,256]{1,0:T(8,128)(2,1)}, u32[]{:S(2)}, u32[]{:S(2)}) collective-permute-start(bf16[64,256]{1,0:T(8,128)(2,1)} %get-tuple-element.50), channel_id=1, source_target_pairs={{7,0},{0,1},{1,2},{2,3},{3,4},{4,5},{5,6},{6,7},{15,8},{8,9},{9,10... | collective-permute-start | bytes 98312 | tf_op jit(solution)/shard_map/ppermute | solution.py:37
  5.7 28.7 %collective-permute-start.1 = (bf16[64,256]{1,0:T(8,128)(2,1)}, bf16[64,256]{1,0:T(8,128)(2,1)}, u32[]{:S(2)}, u32[]{:S(2)}) collective-permute-start(bf16[64,256]{1,0:T(8,128)(2,1)} %get-tuple-element.51), channel_id=1, source_target_pairs={{1,0},{2,1},{3,2},{4,3},{5,4},{6,5},{7,6},{0,7},{9,8},{10,9},{11,1... | collective-permute-start | bytes 98312 | tf_op jit(solution)/shard_map/ppermute | solution.py:37
  9.8 24.6 %collective-permute-start.2 = (bf16[64,256]{1,0:T(8,128)(2,1)}, bf16[64,256]{1,0:T(8,128)(2,1)}, u32[]{:S(2)}, u32[]{:S(2)}) collective-permute-start(bf16[64,256]{1,0:T(8,128)(2,1)} %get-tuple-element.52), channel_id=1, source_target_pairs={{6,0},{7,1},{0,2},{1,3},{2,4},{3,5},{4,6},{5,7},{14,8},{15,9},{8,1... | collective-permute-start | bytes 98312 | tf_op jit(solution)/shard_map/ppermute | solution.py:37
  10.0 28.2 %collective-permute-start.3 = (bf16[64,256]{1,0:T(8,128)(2,1)}, bf16[64,256]{1,0:T(8,128)(2,1)}, u32[]{:S(2)}, u32[]{:S(2)}) collective-permute-start(bf16[64,256]{1,0:T(8,128)(2,1)} %get-tuple-element.53), channel_id=1, source_target_pairs={{2,0},{3,1},{4,2},{5,3},{6,4},{7,5},{0,6},{1,7},{10,8},{11,9},{12,... | collective-permute-start | bytes 98312 | tf_op jit(solution)/shard_map/ppermute | solution.py:37
  18.7 56.5 %collective-permute-start.4 = (bf16[256,512]{1,0:T(8,128)(2,1)S(1)}, bf16[256,512]{1,0:T(8,128)(2,1)S(1)}, u32[]{:S(2)}, u32[]{:S(2)}) collective-permute-start(bf16[256,512]{1,0:T(8,128)(2,1)S(1)} %get-tuple-element.47.after_ref), channel_id=1, source_target_pairs={{7,0},{0,1},{1,2},{2,3},{3,4},{4,5},{5,6},{6,7},{15,8},{8,9},{9,10... | collective-permute-start | bytes 786440 | tf_op jit(solution)/shard_map/ppermute | solution.py:37
  21.8 16.4 %copy-start.3 = (bf16[112,4096]{1,0:T(8,128)(2,1)S(1)}, bf16[112,4096]{1,0:T(8,128)(2,1)}, u32[]{:S(2)}) copy-start(bf16[112,4096]{1,0:T(8,128)(2,1)} %wb_ref.1) | copy-start | bytes 2752516
  26.8 3.3 %copy-start.10 = (bf16[32768,128]{1,0:T(8,128)(2,1)}, bf16[32768,128]{1,0:T(8,128)(2,1)S(1)}, u32[]{:S(2)}) copy-start(bf16[32768,128]{1,0:T(8,128)(2,1)S(1)} %align.1.bas_ref) | copy-start | bytes 25165828
  30.8 44.5 %collective-permute-start.5 = (bf16[256,512]{1,0:T(8,128)(2,1)S(1)}, bf16[256,512]{1,0:T(8,128)(2,1)S(1)}, u32[]{:S(2)}, u32[]{:S(2)}) collective-permute-start(bf16[256,512]{1,0:T(8,128)(2,1)S(1)} %get-tuple-element.55), channel_id=1, source_target_pairs={{1,0},{2,1},{3,2},{4,3},{5,4},{6,5},{7,6},{0,7},{9,8},{10,9},{11,1... | collective-permute-start | bytes 786440 | tf_op jit(solution)/shard_map/ppermute | solution.py:37
  34.4 40.9 %collective-permute-start.6 = (bf16[256,512]{1,0:T(8,128)(2,1)S(1)}, bf16[256,512]{1,0:T(8,128)(2,1)S(1)}, u32[]{:S(2)}, u32[]{:S(2)}) collective-permute-start(bf16[256,512]{1,0:T(8,128)(2,1)S(1)} %get-tuple-element.56), channel_id=1, source_target_pairs={{6,0},{7,1},{0,2},{1,3},{2,4},{3,5},{4,6},{5,7},{14,8},{15,9},{8,1... | collective-permute-start | bytes 786440 | tf_op jit(solution)/shard_map/ppermute | solution.py:37
  34.4 40.9 %collective-permute-start.7 = (bf16[256,512]{1,0:T(8,128)(2,1)S(1)}, bf16[256,512]{1,0:T(8,128)(2,1)S(1)}, u32[]{:S(2)}, u32[]{:S(2)}) collective-permute-start(bf16[256,512]{1,0:T(8,128)(2,1)S(1)} %get-tuple-element.57), channel_id=1, source_target_pairs={{2,0},{3,1},{4,2},{5,3},{6,4},{7,5},{0,6},{1,7},{10,8},{11,9},{12,... | collective-permute-start | bytes 786440 | tf_op jit(solution)/shard_map/ppermute | solution.py:37
  38.2 3.4 %copy-start.11 = (bf16[32768,128]{1,0:T(8,128)(2,1)S(1)}, bf16[32768,128]{1,0:T(8,128)(2,1)}, u32[]{:S(2)}) copy-start(bf16[32768,128]{1,0:T(8,128)(2,1)} %copy-done.10) | copy-start | bytes 25165828
  44.3 30.9 %copy-start.5 = (bf16[2,64,512]{2,1,0:T(8,128)(2,1)S(1)}, bf16[2,64,512]{2,1,0:T(8,128)(2,1)}, u32[]{:S(2)}) copy-start(bf16[2,64,512]{2,1,0:T(8,128)(2,1)} %wu_ref.1) | copy-start | bytes 393220
  44.3 31.0 %copy-start.7 = (s32[1,1024]{1,0:T(1,128)S(1)}, s32[1,1024]{1,0:T(1,128)}, u32[]{:S(2)}) copy-start(s32[1,1024]{1,0:T(1,128)} %rev_ref.1) | copy-start | bytes 12292
  75.3 6.3 %copy-start.12 = (bf16[32768,128]{1,0:T(8,128)(2,1)S(1)}, bf16[32768,128]{1,0:T(8,128)(2,1)}, u32[]{:S(2)}) copy-start(bf16[32768,128]{1,0:T(8,128)(2,1)} %copy-done.10) | copy-start | bytes 25165828
  75.3 6.3 %copy-start.18 = (f32[128,256]{1,0:T(8,128)S(1)}, f32[128,256]{1,0:T(8,128)}, u32[]{:S(2)}) copy-start(f32[128,256]{1,0:T(8,128)} %copy-done.16) | copy-start | bytes 393220
  75.3 6.3 %copy-start.21 = (s32[128,256]{1,0:T(8,128)S(1)}, s32[128,256]{1,0:T(8,128)}, u32[]{:S(2)}) copy-start(s32[128,256]{1,0:T(8,128)} %copy-done.19) | copy-start | bytes 393220
  75.3 40.1 %slice-start = ((s8[16777216]{0:T(1024)(128)(4,1)}), s8[4194304]{0:T(1024)(128)(4,1)S(1)}, s32[]{:S(2)}) async-start(s8[16777216]{0:T(1024)(128)(4,1)} %bitcast.2), calls=%async_computation | async-start | bytes 8388608
  83.2 32.3 %slice-start.1 = ((s8[16777216]{0:T(1024)(128)(4,1)}), s8[4194304]{0:T(1024)(128)(4,1)S(1)}, s32[]{:S(2)}) async-start(s8[16777216]{0:T(1024)(128)(4,1)} %bitcast.2), calls=%async_computation.1 | async-start | bytes 8388608
  83.2 32.3 %slice-start.2 = ((s8[16777216]{0:T(1024)(128)(4,1)}), s8[4194304]{0:T(1024)(128)(4,1)S(1)}, s32[]{:S(2)}) async-start(s8[16777216]{0:T(1024)(128)(4,1)} %bitcast.2), calls=%async_computation.2 | async-start | bytes 8388608
  83.2 32.3 %slice-start.3 = ((s8[16777216]{0:T(1024)(128)(4,1)}), s8[4194304]{0:T(1024)(128)(4,1)S(1)}, s32[]{:S(2)}) async-start(s8[16777216]{0:T(1024)(128)(4,1)} %bitcast.2), calls=%async_computation.3 | async-start | bytes 8388608
  112.9 6.9 %collective-permute-start.10 = (bf16[64,256]{1,0:T(8,128)(2,1)S(1)}, bf16[64,256]{1,0:T(8,128)(2,1)S(1)}, u32[]{:S(2)}, u32[]{:S(2)}) collective-permute-start(bf16[64,256]{1,0:T(8,128)(2,1)S(1)} %get-tuple-element.66), channel_id=1, source_target_pairs={{2,0},{3,1},{4,2},{5,3},{6,4},{7,5},{0,6},{1,7},{10,8},{11,9},{12,... | collective-permute-start | bytes 98312 | tf_op jit(solution)/shard_map/ppermute | solution.py:37
  113.0 6.8 %collective-permute-start.11 = (bf16[64,256]{1,0:T(8,128)(2,1)S(1)}, bf16[64,256]{1,0:T(8,128)(2,1)S(1)}, u32[]{:S(2)}, u32[]{:S(2)}) collective-permute-start(bf16[64,256]{1,0:T(8,128)(2,1)S(1)} %get-tuple-element.67), channel_id=1, source_target_pairs={{6,0},{7,1},{0,2},{1,3},{2,4},{3,5},{4,6},{5,7},{14,8},{15,9},{8,1... | collective-permute-start | bytes 98312 | tf_op jit(solution)/shard_map/ppermute | solution.py:37
  115.0 4.8 %collective-permute-start.8 = (bf16[64,256]{1,0:T(8,128)(2,1)S(1)}, bf16[64,256]{1,0:T(8,128)(2,1)S(1)}, u32[]{:S(2)}, u32[]{:S(2)}) collective-permute-start(bf16[64,256]{1,0:T(8,128)(2,1)S(1)} %get-tuple-element.64), channel_id=1, source_target_pairs={{1,0},{2,1},{3,2},{4,3},{5,4},{6,5},{7,6},{0,7},{9,8},{10,9},{11,1... | collective-permute-start | bytes 98312 | tf_op jit(solution)/shard_map/ppermute | solution.py:37
  115.0 5.1 %collective-permute-start.9 = (bf16[64,256]{1,0:T(8,128)(2,1)S(1)}, bf16[64,256]{1,0:T(8,128)(2,1)S(1)}, u32[]{:S(2)}, u32[]{:S(2)}) collective-permute-start(bf16[64,256]{1,0:T(8,128)(2,1)S(1)} %get-tuple-element.65), channel_id=1, source_target_pairs={{7,0},{0,1},{1,2},{2,3},{3,4},{4,5},{5,6},{6,7},{15,8},{8,9},{9,10... | collective-permute-start | bytes 98312 | tf_op jit(solution)/shard_map/ppermute | solution.py:37
  115.5 4.6 %copy-start.2 = (bf16[1,1024,512]{2,1,0:T(8,128)(2,1)S(1)}, bf16[1,1024,512]{2,1,0:T(8,128)(2,1)}, u32[]{:S(2)}) copy-start(bf16[1,1024,512]{2,1,0:T(8,128)(2,1)} %x_ref.3) | copy-start | bytes 3145732
  115.5 4.6 %copy-start.4 = (bf16[512,512]{1,0:T(8,128)(2,1)S(1)}, bf16[512,512]{1,0:T(8,128)(2,1)}, u32[]{:S(2)}) copy-start(bf16[512,512]{1,0:T(8,128)(2,1)} %we_ref.3) | copy-start | bytes 1572868
  115.5 4.6 %copy-start.6 = (bf16[512,64]{0,1:T(8,128)(2,1)S(1)}, bf16[512,64]{0,1:T(8,128)(2,1)}, u32[]{:S(2)}) copy-start(bf16[512,64]{0,1:T(8,128)(2,1)} %param.16) | copy-start | bytes 196612
  115.5 4.6 %copy-start.13 = (f32[1024,512]{1,0:T(8,128)S(1)}, f32[1024,512]{1,0:T(8,128)}, u32[]{:S(2)}) copy-start(f32[1024,512]{1,0:T(8,128)} %get-tuple-element.62.pre_ref) | copy-start | bytes 6291460
  115.5 4.6 %copy-start.14 = (bf16[1024,512]{1,0:T(8,128)(2,1)S(1)}, bf16[1024,512]{1,0:T(8,128)(2,1)}, u32[]{:S(2)}) copy-start(bf16[1024,512]{1,0:T(8,128)(2,1)} %get-tuple-element.63.hid_ref) | copy-start | bytes 3145732
  115.6 4.6 %copy-start.15 = (f32[64,1024]{1,0:T(8,128)S(1)}, f32[64,1024]{1,0:T(8,128)}, u32[]{:S(2)}) copy-start(f32[64,1024]{1,0:T(8,128)} %get-tuple-element.61.pdt_ref) | copy-start | bytes 786436
  119.7 6.4 %collective-permute-start.12 = (bf16[4,64,1152]{2,1,0:T(8,128)(2,1)S(1)}, bf16[4,64,1152]{2,1,0:T(8,128)(2,1)S(1)}, u32[]{:S(2)}, u32[]{:S(2)}) collective-permute-start(bf16[4,64,1152]{2,1,0:T(8,128)(2,1)S(1)} %get-tuple-element.72), channel_id=1, source_target_pairs={{0,1},{1,0},{2,3},{3,2},{4,5},{5,4},{6,7},{7,6},{8,9},{9,8},{10,11... | collective-permute-start | bytes 1769480 | tf_op jit(solution)/shard_map/ppermute | solution.py:686
  124.3 1.6 collective-permute-start.19
  126.1 7.3 %collective-permute-start.20 = (bf16[64,640]{1,0:T(8,128)(2,1)S(1)}, bf16[64,640]{1,0:T(8,128)(2,1)S(1)}, u32[]{:S(2)}, u32[]{:S(2)}) collective-permute-start(bf16[64,640]{1,0:T(8,128)(2,1)S(1)} %get-tuple-element.80), channel_id=1, source_target_pairs={{0,2},{1,3},{2,4},{3,5},{4,6},{5,7},{6,0},{7,1},{8,10},{9,11},{10,... | collective-permute-start | bytes 245768 | tf_op jit(solution)/shard_map/ppermute | solution.py:697
  126.3 24.6 %collective-permute-start.13 = (bf16[64,1152]{1,0:T(8,128)(2,1)S(1)}, bf16[64,1152]{1,0:T(8,128)(2,1)S(1)}, u32[]{:S(2)}, u32[]{:S(2)}) collective-permute-start(bf16[64,1152]{1,0:T(8,128)(2,1)S(1)} %get-tuple-element.74), channel_id=1, source_target_pairs={{0,2},{1,3},{2,4},{3,5},{4,6},{5,7},{6,0},{7,1},{8,10},{9,11},{10,... | collective-permute-start | bytes 442376 | tf_op jit(solution)/shard_map/ppermute | solution.py:697
  128.6 22.3 %collective-permute-start.14 = (bf16[64,1152]{1,0:T(8,128)(2,1)S(1)}, bf16[64,1152]{1,0:T(8,128)(2,1)S(1)}, u32[]{:S(2)}, u32[]{:S(2)}) collective-permute-start(bf16[64,1152]{1,0:T(8,128)(2,1)S(1)} %get-tuple-element.75), channel_id=1, source_target_pairs={{0,4},{1,5},{2,6},{3,7},{4,0},{5,1},{6,2},{7,3},{8,12},{9,13},{10,... | collective-permute-start | bytes 442376 | tf_op jit(solution)/shard_map/ppermute | solution.py:697
  130.7 20.2 %collective-permute-start.15 = (bf16[64,1152]{1,0:T(8,128)(2,1)S(1)}, bf16[64,1152]{1,0:T(8,128)(2,1)S(1)}, u32[]{:S(2)}, u32[]{:S(2)}) collective-permute-start(bf16[64,1152]{1,0:T(8,128)(2,1)S(1)} %get-tuple-element.76), channel_id=1, source_target_pairs={{0,6},{1,7},{2,0},{3,1},{4,2},{5,3},{6,4},{7,5},{8,14},{9,15},{10,... | collective-permute-start | bytes 442376 | tf_op jit(solution)/shard_map/ppermute | solution.py:697
  133.0 15.9 %collective-permute-start.21 = (bf16[64,640]{1,0:T(8,128)(2,1)S(1)}, bf16[64,640]{1,0:T(8,128)(2,1)S(1)}, u32[]{:S(2)}, u32[]{:S(2)}) collective-permute-start(bf16[64,640]{1,0:T(8,128)(2,1)S(1)} %get-tuple-element.81), channel_id=1, source_target_pairs={{0,4},{1,5},{2,6},{3,7},{4,0},{5,1},{6,2},{7,3},{8,12},{9,13},{10,... | collective-permute-start | bytes 245768 | tf_op jit(solution)/shard_map/ppermute | solution.py:697
  133.4 15.4 %collective-permute-start.22 = (bf16[64,640]{1,0:T(8,128)(2,1)S(1)}, bf16[64,640]{1,0:T(8,128)(2,1)S(1)}, u32[]{:S(2)}, u32[]{:S(2)}) collective-permute-start(bf16[64,640]{1,0:T(8,128)(2,1)S(1)} %get-tuple-element.82), channel_id=1, source_target_pairs={{0,6},{1,7},{2,0},{3,1},{4,2},{5,3},{6,4},{7,5},{8,14},{9,15},{10,... | collective-permute-start | bytes 245768 | tf_op jit(solution)/shard_map/ppermute | solution.py:697
  148.9 7.2 %collective-permute-start.23 = (bf16[64,640]{1,0:T(8,128)(2,1)S(1)}, bf16[64,640]{1,0:T(8,128)(2,1)S(1)}, u32[]{:S(2)}, u32[]{:S(2)}) collective-permute-start(bf16[64,640]{1,0:T(8,128)(2,1)S(1)} %shard_map.158.refs_4_), channel_id=1, source_target_pairs={{0,8},{8,0},{16,24},{24,16},{1,9},{9,1},{17,25},{25,17},{2,10},{10... | collective-permute-start | bytes 245768 | tf_op jit(solution)/shard_map/ppermute | solution.py:711
  151.0 12.5 %collective-permute-start.16 = (bf16[64,1152]{1,0:T(8,128)(2,1)S(1)}, bf16[64,1152]{1,0:T(8,128)(2,1)S(1)}, u32[]{:S(2)}, u32[]{:S(2)}) collective-permute-start(bf16[64,1152]{1,0:T(8,128)(2,1)S(1)} %shard_map.156.refs_0_), channel_id=1, source_target_pairs={{0,8},{8,0},{16,24},{24,16},{1,9},{9,1},{17,25},{25,17},{2,10},{10... | collective-permute-start | bytes 442376 | tf_op jit(solution)/shard_map/ppermute | solution.py:711
  151.1 12.3 %collective-permute-start.17 = (bf16[64,1152]{1,0:T(8,128)(2,1)S(1)}, bf16[64,1152]{1,0:T(8,128)(2,1)S(1)}, u32[]{:S(2)}, u32[]{:S(2)}) collective-permute-start(bf16[64,1152]{1,0:T(8,128)(2,1)S(1)} %shard_map.156.refs_0_), channel_id=1, source_target_pairs={{0,16},{8,24},{16,0},{24,8},{1,17},{9,25},{17,1},{25,9},{2,18},{10... | collective-permute-start | bytes 442376 | tf_op jit(solution)/shard_map/ppermute | solution.py:711
  153.1 10.3 %collective-permute-start.18 = (bf16[64,1152]{1,0:T(8,128)(2,1)S(1)}, bf16[64,1152]{1,0:T(8,128)(2,1)S(1)}, u32[]{:S(2)}, u32[]{:S(2)}) collective-permute-start(bf16[64,1152]{1,0:T(8,128)(2,1)S(1)} %shard_map.156.refs_0_), channel_id=1, source_target_pairs={{0,24},{8,16},{16,8},{24,0},{1,25},{9,17},{17,9},{25,1},{2,26},{10... | collective-permute-start | bytes 442376 | tf_op jit(solution)/shard_map/ppermute | solution.py:711
  154.5 8.9 %collective-permute-start.24 = (bf16[64,640]{1,0:T(8,128)(2,1)S(1)}, bf16[64,640]{1,0:T(8,128)(2,1)S(1)}, u32[]{:S(2)}, u32[]{:S(2)}) collective-permute-start(bf16[64,640]{1,0:T(8,128)(2,1)S(1)} %shard_map.158.refs_4_), channel_id=1, source_target_pairs={{0,16},{8,24},{16,0},{24,8},{1,17},{9,25},{17,1},{25,9},{2,18},{10... | collective-permute-start | bytes 245768 | tf_op jit(solution)/shard_map/ppermute | solution.py:711
  156.1 7.4 %collective-permute-start.25 = (bf16[64,640]{1,0:T(8,128)(2,1)S(1)}, bf16[64,640]{1,0:T(8,128)(2,1)S(1)}, u32[]{:S(2)}, u32[]{:S(2)}) collective-permute-start(bf16[64,640]{1,0:T(8,128)(2,1)S(1)} %shard_map.158.refs_4_), channel_id=1, source_target_pairs={{0,24},{8,16},{16,8},{24,0},{1,25},{9,17},{17,9},{25,1},{2,26},{10... | collective-permute-start | bytes 245768 | tf_op jit(solution)/shard_map/ppermute | solution.py:711
  (9 other events, 11.0 us)

commit v5 on v4

--- a/solution.py
+++ b/solution.py
@@ -298,7 +298,7 @@
     rho = low.shape[1]
     padded = bas.shape[1]
     block = 256
-    sub = 64
+    sub = 256
     resident = lambda *shape: pl.BlockSpec(shape, lambda i: (0,) * len(shape))
     return pl.pallas_call(
         functools.partial(forward_kernel, sub, lists),
@@ -526,7 +526,7 @@
             turn_s[pl.ds(at, GROUP * half), :] = jnp.concatenate(sides, axis=0).astype(bf16)
         return carry
 
-    lax.fori_loop(0, narrow // GROUP, spread, 0, unroll=2)
+    lax.fori_loop(0, narrow // GROUP, spread, 0, unroll=4)
     groups = sub // GROUP
 
     def body(index, carry):
@@ -576,7 +576,7 @@
     rho = low.shape[1]
     padded = bas.shape[1]
     block = 256
-    sub = 64
+    sub = 256
     home = edges // capacity * narrow
     rows = home + lists * narrow
     resident = lambda *shape: pl.BlockSpec(shape, lambda i: (0,) * len(shape))

time: 165 us -> 156 us (0.945)
  Pallas kernels: 87.4 us -> 78.7 us
    pallas_call x1, Pallas kernels: 29.7 us -> 25 us  [backward(): pl.pallas_call(functools.partial(backward_kernel, sub, lists), grid=(edge...]
    pallas_call x1, Pallas kernels: 29.5 us -> 25.4 us  [forward(): pl.pallas_call(functools.partial(forward_kernel, sub, lists), grid=(edges...]
  transfers between devices with their start and end apart: 26 -> 26, of which waited for: 5 -> 5; matrix products, arithmetic and copies ran while one was open for 0% -> 0% of each run, Pallas kernels for 28% -> 27%
where the time goes in v5:
time: 156 us
  Pallas kernels  78.7 us (50%)
  starting transfers between devices  35.3 us (23%)
  waiting for transfers between devices  22.2 us (14%)
  local copies, waits for them, and re-layouts  18 us (12%)
  between operations  1.72 us (1%)
    pallas_call x1, Pallas kernels, forward(): pl.pallas_call(functools.partial(forward_kernel, sub, lists), grid=(edges...  25.4 us
    pallas_call x1, Pallas kernels, backward(): pl.pallas_call(functools.partial(backward_kernel, sub, lists), grid=(edge...  25 us
    ppermute x12, starting transfers between devices, shifted(): return lax.ppermute(block, axis, route)  18.4 us
    unnamed x63, local copies, waits for them, and re-layouts  18 us
    ppermute x6, waiting for transfers between devices, over_graph(): arrived.append(lax.ppermute(send, 'graph', route))  14.2 us
    ppermute x6, starting transfers between devices, over_graph(): arrived.append(lax.ppermute(send, 'graph', route))  8.39 us
    ppermute x6, starting transfers between devices, over_dp(): lax.ppermute(share, 'dp', [(i, i ^ step) for i in range(slabs)])  8.17 us
    ppermute x6, waiting for transfers between devices, over_dp(): lax.ppermute(share, 'dp', [(i, i ^ step) for i in range(slabs)])  6.28 us
  transfers between devices with their start and end apart: 26, of which 5 were waited for; matrix products, arithmetic and copies ran while one was open for 0% of the time, Pallas kernels for 27%

profile of v5, /device:TPU:0, one launch (start us, length us, event | category | flops | bytes accessed | tf_op | source)
XLA Modules:
  0.0 155.9 jit_solution(7980685431681683671)
XLA Ops:
  0.7 4.6 %front.1 = (f32[1024,512]{1,0:T(8,128)}, bf16[1024,512]{1,0:T(8,128)(2,1)}, f32[64,1024]{1,0:T(8,128)}, bf16[64,1024]{1,0:T(8,128)(2,1)}, bf16[64,256]{1,0:T(8,1...) custom-call(s32[1,4]{1,0:T(1,128)} %count_ref.6, ...), custom_call_target="tpu_custom_call" | custom-call | flops 3072000000 | bytes 3072000 | tf_op jit(solution)/shard_map/front/pallas_call | solution.py:95
  5.2 0.5 collective-permute-start
  5.7 4.1 %collective-permute-start.1 = (bf16[64,256]{1,0:T(8,128)(2,1)}, bf16[64,256]{1,0:T(8,128)(2,1)}, u32[]{:S(2)}, u32[]{:S(2)}) collective-permute-start(bf16[64,256]{1,0:T(8,128)(2,1)} %get-tuple-element.51), channel_id=1, source_target_pairs={{1,0},{2,1},{3,2},{4,3},{5,4},{6,5},{7,6},{0,7},{9,8},{10,9},{11,1... | collective-permute-start | bytes 98312 | tf_op jit(solution)/shard_map/ppermute | solution.py:37
  9.8 0.2 collective-permute-start.2
  10.0 3.6 %collective-permute-start.3 = (bf16[64,256]{1,0:T(8,128)(2,1)}, bf16[64,256]{1,0:T(8,128)(2,1)}, u32[]{:S(2)}, u32[]{:S(2)}) collective-permute-start(bf16[64,256]{1,0:T(8,128)(2,1)} %get-tuple-element.53), channel_id=1, source_target_pairs={{2,0},{3,1},{4,2},{5,3},{6,4},{7,5},{0,6},{1,7},{10,8},{11,9},{12,... | collective-permute-start | bytes 98312 | tf_op jit(solution)/shard_map/ppermute | solution.py:37
  13.6 0.2 copy.17.trip_ref
  13.9 0.9 copy-done.22
  14.8 2.6 %pick.1 = (f32[128,256]{1,0:T(8,128)S(1)}, s32[128,256]{1,0:T(8,128)S(1)}, bf16[256,512]{1,0:T(8,128)(2,1)S(1)}, bf16[256,512]{1,0:T(8,128)(2,1)S(1)}, bf16[256,...) custom-call(s32[1,4]{1,0:T(1,128)S(1)} %copy-done.9, bf16[1,1024,512]{2,1,0:T(8,128)(2,1)S(1)} %copy-done.1, ...), custom_call_target="tpu_custom_call" | custom-call | flops 3072000000 | bytes 3072000 | tf_op jit(solution)/shard_map/pick/pallas_call | solution.py:137
  17.4 0.6 copy-done.16
  18.1 0.7 copy-done.19
  18.7 3.1 %copy-done = bf16[1,1024,3584]{2,1,0:T(8,128)(2,1)S(1)} copy-done((bf16[1,1024,3584]{2,1,0:T(8,128)(2,1)S(1)}, bf16[1,1024,3584]{2,1,0:T(8,128)(2,1)}, u32[]{:S(2)}) %copy-start) | copy-done | bytes 7340056
  21.8 5.0 %align.1.bas_ref = bf16[32768,128]{1,0:T(8,128)(2,1)S(1)} custom-call(bf16[256,512]{1,0:T(8,128)(2,1)S(1)} %get-tuple-element.47.after_ref, bf16[1,1024,3584]{2,1,0:T(8,128)(2,1)S(1)} %copy-done), custom_call_target="tpu_custom_call" | custom-call | flops 6144000000 | bytes 6144000 | tf_op jit(solution)/shard_map/align/pallas_call | solution.py:206
  26.8 3.3 %copy-done.10 = bf16[32768,128]{1,0:T(8,128)(2,1)} copy-done((bf16[32768,128]{1,0:T(8,128)(2,1)}, bf16[32768,128]{1,0:T(8,128)(2,1)S(1)}, u32[]{:S(2)}) %copy-start.10) | copy-done | bytes 8388632
  30.8 3.6 %collective-permute-start.5 = (bf16[256,512]{1,0:T(8,128)(2,1)S(1)}, bf16[256,512]{1,0:T(8,128)(2,1)S(1)}, u32[]{:S(2)}, u32[]{:S(2)}) collective-permute-start(bf16[256,512]{1,0:T(8,128)(2,1)S(1)} %get-tuple-element.55), channel_id=1, source_target_pairs={{1,0},{2,1},{3,2},{4,3},{5,4},{6,5},{7,6},{0,7},{9,8},{10,9},{11,1... | collective-permute-start | bytes 786440 | tf_op jit(solution)/shard_map/ppermute | solution.py:37
  34.4 3.8 %collective-permute-start.7 = (bf16[256,512]{1,0:T(8,128)(2,1)S(1)}, bf16[256,512]{1,0:T(8,128)(2,1)S(1)}, u32[]{:S(2)}, u32[]{:S(2)}) collective-permute-start(bf16[256,512]{1,0:T(8,128)(2,1)S(1)} %get-tuple-element.57), channel_id=1, source_target_pairs={{2,0},{3,1},{4,2},{5,3},{6,4},{7,5},{0,6},{1,7},{10,8},{11,9},{12,... | collective-permute-start | bytes 786440 | tf_op jit(solution)/shard_map/ppermute | solution.py:37
  38.2 3.4 %copy-done.11 = bf16[32768,128]{1,0:T(8,128)(2,1)S(1)} copy-done((bf16[32768,128]{1,0:T(8,128)(2,1)S(1)}, bf16[32768,128]{1,0:T(8,128)(2,1)}, u32[]{:S(2)}) %copy-start.11) | copy-done | bytes 8388632
  41.6 0.9 copy-done.17
  42.5 0.9 copy-done.20
  43.4 0.9 copy-done.23
  44.3 25.4 %forward.1 = (bf16[1024,8192]{1,0:T(8,128)(2,1)}, bf16[1024,64]{1,0:T(8,128)(2,1)S(1)}, bf16[8192,64]{1,0:T(8,128)(2,1)S(1)}) custom-call(bf16[32768,128]{1,0:T(8,128)(2,1)S(1)} %copy-done.11, f32[128,256]{1,0:T(8,128)S(1)} %copy-done.17, s32[128,256]{1,0:T(8,128)S(1)} %copy-done.20, bf16[64,1024]{1,0:T(8,128)(2,1)S(1)} %copy-done.23, ...), custom_call_target="tpu_custom_call" | custom-call | flops 29696000000 | bytes 29696000 | tf_op jit(solution)/shard_map/forward/pallas_call | solution.py:303
  69.8 1.4 copy-done.24
  71.3 6.2 %state_grads.1 = (bf16[1024,64]{1,0:T(8,128)(2,1)S(1)}, f32[64,1024]{1,0:T(8,128)S(1)}) custom-call(s32[1,1]{1,0:T(1,128)S(6)} %copy.18.count_ref, bf16[1024,64]{1,0:T(8,128)(2,1)S(1)} %get-tuple-element.54.state_ref, bf16[1,1024,512]{2,1,0:T(8,128)(2,1)S(1)} %copy-done.1, s32[1,1024]{1,0:T(1,128)S(1)} %copy-done.7, bf16[1,1024,512]{2,1,0:T(8,128)(2,1)S(1)} %copy-done.1, ...), custom_call_target="tpu_custom_call" | custom-call | flops 7168000000 | bytes 7168000 | tf_op jit(solution)/shard_map/state_grads/pallas_call | solution.py:383
  77.6 1.6 %copy-done.25 = bf16[8192,64]{1,0:T(8,128)(2,1)S(1)} copy-done((bf16[8192,64]{1,0:T(8,128)(2,1)S(1)}, bf16[8192,64]{1,0:T(8,128)(2,1)}, u32[]{:S(2)}) %copy-start.25) | copy-done | bytes 1048600
  79.2 25.0 %backward.1 = (f32[256,256]{1,0:T(8,128)S(1)}, bf16[64,256]{1,0:T(8,128)(2,1)S(1)}, bf16[64,256]{1,0:T(8,128)(2,1)S(1)}, bf16[64,256]{1,0:T(8,128)(2,1)S(1)}, bf16[64,256]{1,0:T(8,128)(2,1)S(1)}) custom-call(bf16[32768,128]{1,0:T(8,128)(2,1)S(1)} %copy-done.12, bf16[1024,64]{1,0:T(8,128)(2,1)S(1)} %get-tuple-element.58.grad_ref, f32[128,256]{1,0:T(8,128)S(1)} %copy-done.18, ...), custom_call_target="tpu_custom_call" | custom-call | flops 32768000000 | bytes 32768000 | tf_op jit(solution)/shard_map/backward/pallas_call | solution.py:583
  104.2 2.0 %collective-permute-start.11 = (bf16[64,256]{1,0:T(8,128)(2,1)S(1)}, bf16[64,256]{1,0:T(8,128)(2,1)S(1)}, u32[]{:S(2)}, u32[]{:S(2)}) collective-permute-start(bf16[64,256]{1,0:T(8,128)(2,1)S(1)} %get-tuple-element.67), channel_id=1, source_target_pairs={{6,0},{7,1},{0,2},{1,3},{2,4},{3,5},{4,6},{5,7},{14,8},{15,9},{8,1... | collective-permute-start | bytes 98312 | tf_op jit(solution)/shard_map/ppermute | solution.py:37
  106.3 0.5 collective-permute-start.9
  106.9 4.1 %bil_shares.1 = (bf16[4,64,1152]{2,1,0:T(8,128)(2,1)S(1)}, bf16[4,64,1152]{2,1,0:T(8,128)(2,1)S(1)}) custom-call(s32[1,1]{1,0:T(1,128)S(6)} %select_n.12.core_ref, bf16[1024,8192]{1,0:T(8,128)(2,1)S(1)} %bitcast.3, bf16[1024,64]{1,0:T(8,128)(2,1)S(1)} %get-tuple-element.58.grad_ref, f32[64,1024]{1,0:T(8,128)S(1)} %get-tuple-element.70.up_ref), custom_call_target="tpu_custom_call" | custom-call | flops 4096000000 | bytes 4096000 | tf_op jit(solution)/shard_map/bil_shares/pallas_call | solution.py:455
  111.0 0.1 collective-permute-start.12
  111.1 0.3 collective-permute-done.9.rest_1_
  111.4 4.2 %tail.1 = (bf16[1,1024,512]{2,1,0:T(8,128)(2,1)}, bf16[4,64,640]{2,1,0:T(8,128)(2,1)S(1)}, bf16[4,64,640]{2,1,0:T(8,128)(2,1)S(1)}) custom-call(s32[1,4]{1,0:T(1,128)S(1)} %copy-done.9, s32[1,1]{1,0:T(1,128)S(6)} %select_n.12.core_ref, f32[256,256]{1,0:T(8,128)S(1)} %get-tuple-element.60.pool_ref, s32[1,4,256]{2,1,0:T(4,128)S(1)} %copy-done.8, ...), custom_call_target="tpu_custom_call" | custom-call | flops 4096000000 | bytes 4096000 | tf_op jit(solution)/shard_map/tail/pallas_call | solution.py:650
  115.6 0.2 collective-permute-start.19
  115.8 1.4 collective-permute-done.19.got_ref
  117.3 0.1 shard_map.157
  117.4 0.1 shard_map.155
  117.6 2.3 %collective-permute-start.13 = (bf16[64,1152]{1,0:T(8,128)(2,1)S(1)}, bf16[64,1152]{1,0:T(8,128)(2,1)S(1)}, u32[]{:S(2)}, u32[]{:S(2)}) collective-permute-start(bf16[64,1152]{1,0:T(8,128)(2,1)S(1)} %get-tuple-element.74), channel_id=1, source_target_pairs={{0,2},{1,3},{2,4},{3,5},{4,6},{5,7},{6,0},{7,1},{8,10},{9,11},{10,... | collective-permute-start | bytes 442376 | tf_op jit(solution)/shard_map/ppermute | solution.py:697
  119.9 2.1 %collective-permute-start.14 = (bf16[64,1152]{1,0:T(8,128)(2,1)S(1)}, bf16[64,1152]{1,0:T(8,128)(2,1)S(1)}, u32[]{:S(2)}, u32[]{:S(2)}) collective-permute-start(bf16[64,1152]{1,0:T(8,128)(2,1)S(1)} %get-tuple-element.75), channel_id=1, source_target_pairs={{0,4},{1,5},{2,6},{3,7},{4,0},{5,1},{6,2},{7,3},{8,12},{9,13},{10,... | collective-permute-start | bytes 442376 | tf_op jit(solution)/shard_map/ppermute | solution.py:697
  122.0 2.2 %collective-permute-start.15 = (bf16[64,1152]{1,0:T(8,128)(2,1)S(1)}, bf16[64,1152]{1,0:T(8,128)(2,1)S(1)}, u32[]{:S(2)}, u32[]{:S(2)}) collective-permute-start(bf16[64,1152]{1,0:T(8,128)(2,1)S(1)} %get-tuple-element.76), channel_id=1, source_target_pairs={{0,6},{1,7},{2,0},{3,1},{4,2},{5,3},{6,4},{7,5},{8,14},{9,15},{10,... | collective-permute-start | bytes 442376 | tf_op jit(solution)/shard_map/ppermute | solution.py:697
  124.2 0.5 collective-permute-done.20.refs_1_
  124.7 1.7 %collective-permute-start.22 = (bf16[64,640]{1,0:T(8,128)(2,1)S(1)}, bf16[64,640]{1,0:T(8,128)(2,1)S(1)}, u32[]{:S(2)}, u32[]{:S(2)}) collective-permute-start(bf16[64,640]{1,0:T(8,128)(2,1)S(1)} %get-tuple-element.82), channel_id=1, source_target_pairs={{0,6},{1,7},{2,0},{3,1},{4,2},{5,3},{6,4},{7,5},{8,14},{9,15},{10,... | collective-permute-start | bytes 245768 | tf_op jit(solution)/shard_map/ppermute | solution.py:697
  126.4 13.7 %collective-permute-done.21.refs_2_ = bf16[64,640]{1,0:T(8,128)(2,1)S(1)} collective-permute-done((bf16[64,640]{1,0:T(8,128)(2,1)S(1)}, bf16[64,640]{1,0:T(8,128)(2,1)S(1)}, u32[]{:S(2)}, u32[]{:S(2)}) %collective-permute-start.21) | collective-permute-done | bytes 81952 | tf_op jit(solution)/shard_map/ppermute | solution.py:697
  140.2 2.0 %collective-permute-start.23 = (bf16[64,640]{1,0:T(8,128)(2,1)S(1)}, bf16[64,640]{1,0:T(8,128)(2,1)S(1)}, u32[]{:S(2)}, u32[]{:S(2)}) collective-permute-start(bf16[64,640]{1,0:T(8,128)(2,1)S(1)} %shard_map.158.refs_4_), channel_id=1, source_target_pairs={{0,8},{8,0},{16,24},{24,16},{1,9},{9,1},{17,25},{25,17},{2,10},{10... | collective-permute-start | bytes 245768 | tf_op jit(solution)/shard_map/ppermute | solution.py:711
  142.3 0.1 collective-permute-start.16
  142.4 2.0 %collective-permute-start.17 = (bf16[64,1152]{1,0:T(8,128)(2,1)S(1)}, bf16[64,1152]{1,0:T(8,128)(2,1)S(1)}, u32[]{:S(2)}, u32[]{:S(2)}) collective-permute-start(bf16[64,1152]{1,0:T(8,128)(2,1)S(1)} %shard_map.156.refs_0_), channel_id=1, source_target_pairs={{0,16},{8,24},{16,0},{24,8},{1,17},{9,25},{17,1},{25,9},{2,18},{10... | collective-permute-start | bytes 442376 | tf_op jit(solution)/shard_map/ppermute | solution.py:711
  144.4 1.4 collective-permute-start.18
  145.8 1.5 collective-permute-start.24
  147.3 1.1 collective-permute-start.25
  148.4 6.3 %collective-permute-done.24.refs_6_ = bf16[64,640]{1,0:T(8,128)(2,1)S(1)} collective-permute-done((bf16[64,640]{1,0:T(8,128)(2,1)S(1)}, bf16[64,640]{1,0:T(8,128)(2,1)S(1)}, u32[]{:S(2)}, u32[]{:S(2)}) %collective-permute-start.24) | collective-permute-done | bytes 81952 | tf_op jit(solution)/shard_map/ppermute | solution.py:711
  154.7 1.1 finish.1
  (81 shorter events, 0.4 us)
Async XLA Ops:
  0.6 13.2 %copy-start.8 = (s32[1,4,256]{2,1,0:T(4,128)S(1)}, s32[1,4,256]{2,1,0:T(4,128)}, u32[]{:S(2)}) copy-start(s32[1,4,256]{2,1,0:T(4,128)} %rows_ref.5) | copy-start | bytes 12292
  0.6 13.2 %copy-start.9 = (s32[1,4]{1,0:T(1,128)S(1)}, s32[1,4]{1,0:T(1,128)}, u32[]{:S(2)}) copy-start(s32[1,4]{1,0:T(1,128)} %count_ref.6) | copy-start | bytes 52
  0.7 13.0 %copy-start.26 = (s32[1,1024,32]{1,2,0:T(8,128)S(1)}, s32[1,1024,32]{1,2,0:T(8,128)}, u32[]{:S(2)}) copy-start(s32[1,1024,32]{1,2,0:T(8,128)} %param.19) | copy-start | bytes 393220
  0.7 13.2 %copy-start.1 = (bf16[1,1024,512]{2,1,0:T(8,128)(2,1)S(1)}, bf16[1,1024,512]{2,1,0:T(8,128)(2,1)}, u32[]{:S(2)}) copy-start(bf16[1,1024,512]{2,1,0:T(8,128)(2,1)} %own_ref.1) | copy-start | bytes 3145732
  5.2 25.6 %collective-permute-start = (bf16[64,256]{1,0:T(8,128)(2,1)}, bf16[64,256]{1,0:T(8,128)(2,1)}, u32[]{:S(2)}, u32[]{:S(2)}) collective-permute-start(bf16[64,256]{1,0:T(8,128)(2,1)} %get-tuple-element.50), channel_id=1, source_target_pairs={{7,0},{0,1},{1,2},{2,3},{3,4},{4,5},{5,6},{6,7},{15,8},{8,9},{9,10... | collective-permute-start | bytes 98312 | tf_op jit(solution)/shard_map/ppermute | solution.py:37
  5.7 28.7 %collective-permute-start.1 = (bf16[64,256]{1,0:T(8,128)(2,1)}, bf16[64,256]{1,0:T(8,128)(2,1)}, u32[]{:S(2)}, u32[]{:S(2)}) collective-permute-start(bf16[64,256]{1,0:T(8,128)(2,1)} %get-tuple-element.51), channel_id=1, source_target_pairs={{1,0},{2,1},{3,2},{4,3},{5,4},{6,5},{7,6},{0,7},{9,8},{10,9},{11,1... | collective-permute-start | bytes 98312 | tf_op jit(solution)/shard_map/ppermute | solution.py:37
  9.8 24.6 %collective-permute-start.2 = (bf16[64,256]{1,0:T(8,128)(2,1)}, bf16[64,256]{1,0:T(8,128)(2,1)}, u32[]{:S(2)}, u32[]{:S(2)}) collective-permute-start(bf16[64,256]{1,0:T(8,128)(2,1)} %get-tuple-element.52), channel_id=1, source_target_pairs={{6,0},{7,1},{0,2},{1,3},{2,4},{3,5},{4,6},{5,7},{14,8},{15,9},{8,1... | collective-permute-start | bytes 98312 | tf_op jit(solution)/shard_map/ppermute | solution.py:37
  10.0 28.2 %collective-permute-start.3 = (bf16[64,256]{1,0:T(8,128)(2,1)}, bf16[64,256]{1,0:T(8,128)(2,1)}, u32[]{:S(2)}, u32[]{:S(2)}) collective-permute-start(bf16[64,256]{1,0:T(8,128)(2,1)} %get-tuple-element.53), channel_id=1, source_target_pairs={{2,0},{3,1},{4,2},{5,3},{6,4},{7,5},{0,6},{1,7},{10,8},{11,9},{12,... | collective-permute-start | bytes 98312 | tf_op jit(solution)/shard_map/ppermute | solution.py:37
  18.7 52.5 %collective-permute-start.4 = (bf16[256,512]{1,0:T(8,128)(2,1)S(1)}, bf16[256,512]{1,0:T(8,128)(2,1)S(1)}, u32[]{:S(2)}, u32[]{:S(2)}) collective-permute-start(bf16[256,512]{1,0:T(8,128)(2,1)S(1)} %get-tuple-element.47.after_ref), channel_id=1, source_target_pairs={{7,0},{0,1},{1,2},{2,3},{3,4},{4,5},{5,6},{6,7},{15,8},{8,9},{9,10... | collective-permute-start | bytes 786440 | tf_op jit(solution)/shard_map/ppermute | solution.py:37
  21.8 16.4 %copy-start.3 = (bf16[112,4096]{1,0:T(8,128)(2,1)S(1)}, bf16[112,4096]{1,0:T(8,128)(2,1)}, u32[]{:S(2)}) copy-start(bf16[112,4096]{1,0:T(8,128)(2,1)} %wb_ref.1) | copy-start | bytes 2752516
  26.8 3.3 %copy-start.10 = (bf16[32768,128]{1,0:T(8,128)(2,1)}, bf16[32768,128]{1,0:T(8,128)(2,1)S(1)}, u32[]{:S(2)}) copy-start(bf16[32768,128]{1,0:T(8,128)(2,1)S(1)} %align.1.bas_ref) | copy-start | bytes 25165828
  30.8 40.4 %collective-permute-start.5 = (bf16[256,512]{1,0:T(8,128)(2,1)S(1)}, bf16[256,512]{1,0:T(8,128)(2,1)S(1)}, u32[]{:S(2)}, u32[]{:S(2)}) collective-permute-start(bf16[256,512]{1,0:T(8,128)(2,1)S(1)} %get-tuple-element.55), channel_id=1, source_target_pairs={{1,0},{2,1},{3,2},{4,3},{5,4},{6,5},{7,6},{0,7},{9,8},{10,9},{11,1... | collective-permute-start | bytes 786440 | tf_op jit(solution)/shard_map/ppermute | solution.py:37
  34.4 36.8 %collective-permute-start.6 = (bf16[256,512]{1,0:T(8,128)(2,1)S(1)}, bf16[256,512]{1,0:T(8,128)(2,1)S(1)}, u32[]{:S(2)}, u32[]{:S(2)}) collective-permute-start(bf16[256,512]{1,0:T(8,128)(2,1)S(1)} %get-tuple-element.56), channel_id=1, source_target_pairs={{6,0},{7,1},{0,2},{1,3},{2,4},{3,5},{4,6},{5,7},{14,8},{15,9},{8,1... | collective-permute-start | bytes 786440 | tf_op jit(solution)/shard_map/ppermute | solution.py:37
  34.4 36.8 %collective-permute-start.7 = (bf16[256,512]{1,0:T(8,128)(2,1)S(1)}, bf16[256,512]{1,0:T(8,128)(2,1)S(1)}, u32[]{:S(2)}, u32[]{:S(2)}) collective-permute-start(bf16[256,512]{1,0:T(8,128)(2,1)S(1)} %get-tuple-element.57), channel_id=1, source_target_pairs={{2,0},{3,1},{4,2},{5,3},{6,4},{7,5},{0,6},{1,7},{10,8},{11,9},{12,... | collective-permute-start | bytes 786440 | tf_op jit(solution)/shard_map/ppermute | solution.py:37
  38.2 3.4 %copy-start.11 = (bf16[32768,128]{1,0:T(8,128)(2,1)S(1)}, bf16[32768,128]{1,0:T(8,128)(2,1)}, u32[]{:S(2)}) copy-start(bf16[32768,128]{1,0:T(8,128)(2,1)} %copy-done.10) | copy-start | bytes 25165828
  44.3 26.9 %copy-start.5 = (bf16[2,64,512]{2,1,0:T(8,128)(2,1)S(1)}, bf16[2,64,512]{2,1,0:T(8,128)(2,1)}, u32[]{:S(2)}) copy-start(bf16[2,64,512]{2,1,0:T(8,128)(2,1)} %wu_ref.1) | copy-start | bytes 393220
  44.3 26.9 %copy-start.7 = (s32[1,1024]{1,0:T(1,128)S(1)}, s32[1,1024]{1,0:T(1,128)}, u32[]{:S(2)}) copy-start(s32[1,1024]{1,0:T(1,128)} %rev_ref.1) | copy-start | bytes 12292
  71.2 6.3 %copy-start.12 = (bf16[32768,128]{1,0:T(8,128)(2,1)S(1)}, bf16[32768,128]{1,0:T(8,128)(2,1)}, u32[]{:S(2)}) copy-start(bf16[32768,128]{1,0:T(8,128)(2,1)} %copy-done.10) | copy-start | bytes 25165828
  71.2 6.3 %copy-start.18 = (f32[128,256]{1,0:T(8,128)S(1)}, f32[128,256]{1,0:T(8,128)}, u32[]{:S(2)}) copy-start(f32[128,256]{1,0:T(8,128)} %copy-done.16) | copy-start | bytes 393220
  71.3 6.3 %copy-start.21 = (s32[128,256]{1,0:T(8,128)S(1)}, s32[128,256]{1,0:T(8,128)}, u32[]{:S(2)}) copy-start(s32[128,256]{1,0:T(8,128)} %copy-done.19) | copy-start | bytes 393220
  71.3 35.5 %slice-start = ((s8[16777216]{0:T(1024)(128)(4,1)}), s8[4194304]{0:T(1024)(128)(4,1)S(1)}, s32[]{:S(2)}) async-start(s8[16777216]{0:T(1024)(128)(4,1)} %bitcast.2), calls=%async_computation | async-start | bytes 8388608
  79.1 27.6 %slice-start.1 = ((s8[16777216]{0:T(1024)(128)(4,1)}), s8[4194304]{0:T(1024)(128)(4,1)S(1)}, s32[]{:S(2)}) async-start(s8[16777216]{0:T(1024)(128)(4,1)} %bitcast.2), calls=%async_computation.1 | async-start | bytes 8388608
  79.1 27.6 %slice-start.2 = ((s8[16777216]{0:T(1024)(128)(4,1)}), s8[4194304]{0:T(1024)(128)(4,1)S(1)}, s32[]{:S(2)}) async-start(s8[16777216]{0:T(1024)(128)(4,1)} %bitcast.2), calls=%async_computation.2 | async-start | bytes 8388608
  79.2 27.6 %slice-start.3 = ((s8[16777216]{0:T(1024)(128)(4,1)}), s8[4194304]{0:T(1024)(128)(4,1)S(1)}, s32[]{:S(2)}) async-start(s8[16777216]{0:T(1024)(128)(4,1)} %bitcast.2), calls=%async_computation.3 | async-start | bytes 8388608
  104.2 6.9 %collective-permute-start.10 = (bf16[64,256]{1,0:T(8,128)(2,1)S(1)}, bf16[64,256]{1,0:T(8,128)(2,1)S(1)}, u32[]{:S(2)}, u32[]{:S(2)}) collective-permute-start(bf16[64,256]{1,0:T(8,128)(2,1)S(1)} %get-tuple-element.66), channel_id=1, source_target_pairs={{2,0},{3,1},{4,2},{5,3},{6,4},{7,5},{0,6},{1,7},{10,8},{11,9},{12,... | collective-permute-start | bytes 98312 | tf_op jit(solution)/shard_map/ppermute | solution.py:37
  104.2 6.8 %collective-permute-start.11 = (bf16[64,256]{1,0:T(8,128)(2,1)S(1)}, bf16[64,256]{1,0:T(8,128)(2,1)S(1)}, u32[]{:S(2)}, u32[]{:S(2)}) collective-permute-start(bf16[64,256]{1,0:T(8,128)(2,1)S(1)} %get-tuple-element.67), channel_id=1, source_target_pairs={{6,0},{7,1},{0,2},{1,3},{2,4},{3,5},{4,6},{5,7},{14,8},{15,9},{8,1... | collective-permute-start | bytes 98312 | tf_op jit(solution)/shard_map/ppermute | solution.py:37
  106.3 4.8 %collective-permute-start.8 = (bf16[64,256]{1,0:T(8,128)(2,1)S(1)}, bf16[64,256]{1,0:T(8,128)(2,1)S(1)}, u32[]{:S(2)}, u32[]{:S(2)}) collective-permute-start(bf16[64,256]{1,0:T(8,128)(2,1)S(1)} %get-tuple-element.64), channel_id=1, source_target_pairs={{1,0},{2,1},{3,2},{4,3},{5,4},{6,5},{7,6},{0,7},{9,8},{10,9},{11,1... | collective-permute-start | bytes 98312 | tf_op jit(solution)/shard_map/ppermute | solution.py:37
  106.3 5.1 %collective-permute-start.9 = (bf16[64,256]{1,0:T(8,128)(2,1)S(1)}, bf16[64,256]{1,0:T(8,128)(2,1)S(1)}, u32[]{:S(2)}, u32[]{:S(2)}) collective-permute-start(bf16[64,256]{1,0:T(8,128)(2,1)S(1)} %get-tuple-element.65), channel_id=1, source_target_pairs={{7,0},{0,1},{1,2},{2,3},{3,4},{4,5},{5,6},{6,7},{15,8},{8,9},{9,10... | collective-permute-start | bytes 98312 | tf_op jit(solution)/shard_map/ppermute | solution.py:37
  106.8 4.6 %copy-start.2 = (bf16[1,1024,512]{2,1,0:T(8,128)(2,1)S(1)}, bf16[1,1024,512]{2,1,0:T(8,128)(2,1)}, u32[]{:S(2)}) copy-start(bf16[1,1024,512]{2,1,0:T(8,128)(2,1)} %x_ref.3) | copy-start | bytes 3145732
  106.8 4.6 %copy-start.4 = (bf16[512,512]{1,0:T(8,128)(2,1)S(1)}, bf16[512,512]{1,0:T(8,128)(2,1)}, u32[]{:S(2)}) copy-start(bf16[512,512]{1,0:T(8,128)(2,1)} %we_ref.3) | copy-start | bytes 1572868
  106.8 4.6 %copy-start.6 = (bf16[512,64]{0,1:T(8,128)(2,1)S(1)}, bf16[512,64]{0,1:T(8,128)(2,1)}, u32[]{:S(2)}) copy-start(bf16[512,64]{0,1:T(8,128)(2,1)} %param.16) | copy-start | bytes 196612
  106.8 4.6 %copy-start.13 = (f32[1024,512]{1,0:T(8,128)S(1)}, f32[1024,512]{1,0:T(8,128)}, u32[]{:S(2)}) copy-start(f32[1024,512]{1,0:T(8,128)} %get-tuple-element.62.pre_ref) | copy-start | bytes 6291460
  106.8 4.6 %copy-start.14 = (bf16[1024,512]{1,0:T(8,128)(2,1)S(1)}, bf16[1024,512]{1,0:T(8,128)(2,1)}, u32[]{:S(2)}) copy-start(bf16[1024,512]{1,0:T(8,128)(2,1)} %get-tuple-element.63.hid_ref) | copy-start | bytes 3145732
  106.8 4.6 %copy-start.15 = (f32[64,1024]{1,0:T(8,128)S(1)}, f32[64,1024]{1,0:T(8,128)}, u32[]{:S(2)}) copy-start(f32[64,1024]{1,0:T(8,128)} %get-tuple-element.61.pdt_ref) | copy-start | bytes 786436
  111.0 6.4 %collective-permute-start.12 = (bf16[4,64,1152]{2,1,0:T(8,128)(2,1)S(1)}, bf16[4,64,1152]{2,1,0:T(8,128)(2,1)S(1)}, u32[]{:S(2)}, u32[]{:S(2)}) collective-permute-start(bf16[4,64,1152]{2,1,0:T(8,128)(2,1)S(1)} %get-tuple-element.72), channel_id=1, source_target_pairs={{0,1},{1,0},{2,3},{3,2},{4,5},{5,4},{6,7},{7,6},{8,9},{9,8},{10,11... | collective-permute-start | bytes 1769480 | tf_op jit(solution)/shard_map/ppermute | solution.py:686
  115.6 1.6 %collective-permute-start.19 = (bf16[4,64,640]{2,1,0:T(8,128)(2,1)S(1)}, bf16[4,64,640]{2,1,0:T(8,128)(2,1)S(1)}, u32[]{:S(2)}, u32[]{:S(2)}) collective-permute-start(bf16[4,64,640]{2,1,0:T(8,128)(2,1)S(1)} %get-tuple-element.78), channel_id=1, source_target_pairs={{0,1},{1,0},{2,3},{3,2},{4,5},{5,4},{6,7},{7,6},{8,9},{9,8},{10,11... | collective-permute-start | bytes 983048 | tf_op jit(solution)/shard_map/ppermute | solution.py:686
  117.4 7.3 %collective-permute-start.20 = (bf16[64,640]{1,0:T(8,128)(2,1)S(1)}, bf16[64,640]{1,0:T(8,128)(2,1)S(1)}, u32[]{:S(2)}, u32[]{:S(2)}) collective-permute-start(bf16[64,640]{1,0:T(8,128)(2,1)S(1)} %get-tuple-element.80), channel_id=1, source_target_pairs={{0,2},{1,3},{2,4},{3,5},{4,6},{5,7},{6,0},{7,1},{8,10},{9,11},{10,... | collective-permute-start | bytes 245768 | tf_op jit(solution)/shard_map/ppermute | solution.py:697
  117.6 24.6 %collective-permute-start.13 = (bf16[64,1152]{1,0:T(8,128)(2,1)S(1)}, bf16[64,1152]{1,0:T(8,128)(2,1)S(1)}, u32[]{:S(2)}, u32[]{:S(2)}) collective-permute-start(bf16[64,1152]{1,0:T(8,128)(2,1)S(1)} %get-tuple-element.74), channel_id=1, source_target_pairs={{0,2},{1,3},{2,4},{3,5},{4,6},{5,7},{6,0},{7,1},{8,10},{9,11},{10,... | collective-permute-start | bytes 442376 | tf_op jit(solution)/shard_map/ppermute | solution.py:697
  119.9 22.3 %collective-permute-start.14 = (bf16[64,1152]{1,0:T(8,128)(2,1)S(1)}, bf16[64,1152]{1,0:T(8,128)(2,1)S(1)}, u32[]{:S(2)}, u32[]{:S(2)}) collective-permute-start(bf16[64,1152]{1,0:T(8,128)(2,1)S(1)} %get-tuple-element.75), channel_id=1, source_target_pairs={{0,4},{1,5},{2,6},{3,7},{4,0},{5,1},{6,2},{7,3},{8,12},{9,13},{10,... | collective-permute-start | bytes 442376 | tf_op jit(solution)/shard_map/ppermute | solution.py:697
  122.0 20.2 %collective-permute-start.15 = (bf16[64,1152]{1,0:T(8,128)(2,1)S(1)}, bf16[64,1152]{1,0:T(8,128)(2,1)S(1)}, u32[]{:S(2)}, u32[]{:S(2)}) collective-permute-start(bf16[64,1152]{1,0:T(8,128)(2,1)S(1)} %get-tuple-element.76), channel_id=1, source_target_pairs={{0,6},{1,7},{2,0},{3,1},{4,2},{5,3},{6,4},{7,5},{8,14},{9,15},{10,... | collective-permute-start | bytes 442376 | tf_op jit(solution)/shard_map/ppermute | solution.py:697
  124.2 15.9 %collective-permute-start.21 = (bf16[64,640]{1,0:T(8,128)(2,1)S(1)}, bf16[64,640]{1,0:T(8,128)(2,1)S(1)}, u32[]{:S(2)}, u32[]{:S(2)}) collective-permute-start(bf16[64,640]{1,0:T(8,128)(2,1)S(1)} %get-tuple-element.81), channel_id=1, source_target_pairs={{0,4},{1,5},{2,6},{3,7},{4,0},{5,1},{6,2},{7,3},{8,12},{9,13},{10,... | collective-permute-start | bytes 245768 | tf_op jit(solution)/shard_map/ppermute | solution.py:697
  124.7 15.4 %collective-permute-start.22 = (bf16[64,640]{1,0:T(8,128)(2,1)S(1)}, bf16[64,640]{1,0:T(8,128)(2,1)S(1)}, u32[]{:S(2)}, u32[]{:S(2)}) collective-permute-start(bf16[64,640]{1,0:T(8,128)(2,1)S(1)} %get-tuple-element.82), channel_id=1, source_target_pairs={{0,6},{1,7},{2,0},{3,1},{4,2},{5,3},{6,4},{7,5},{8,14},{9,15},{10,... | collective-permute-start | bytes 245768 | tf_op jit(solution)/shard_map/ppermute | solution.py:697
  140.2 7.2 %collective-permute-start.23 = (bf16[64,640]{1,0:T(8,128)(2,1)S(1)}, bf16[64,640]{1,0:T(8,128)(2,1)S(1)}, u32[]{:S(2)}, u32[]{:S(2)}) collective-permute-start(bf16[64,640]{1,0:T(8,128)(2,1)S(1)} %shard_map.158.refs_4_), channel_id=1, source_target_pairs={{0,8},{8,0},{16,24},{24,16},{1,9},{9,1},{17,25},{25,17},{2,10},{10... | collective-permute-start | bytes 245768 | tf_op jit(solution)/shard_map/ppermute | solution.py:711
  142.3 12.4 %collective-permute-start.16 = (bf16[64,1152]{1,0:T(8,128)(2,1)S(1)}, bf16[64,1152]{1,0:T(8,128)(2,1)S(1)}, u32[]{:S(2)}, u32[]{:S(2)}) collective-permute-start(bf16[64,1152]{1,0:T(8,128)(2,1)S(1)} %shard_map.156.refs_0_), channel_id=1, source_target_pairs={{0,8},{8,0},{16,24},{24,16},{1,9},{9,1},{17,25},{25,17},{2,10},{10... | collective-permute-start | bytes 442376 | tf_op jit(solution)/shard_map/ppermute | solution.py:711
  142.4 12.3 %collective-permute-start.17 = (bf16[64,1152]{1,0:T(8,128)(2,1)S(1)}, bf16[64,1152]{1,0:T(8,128)(2,1)S(1)}, u32[]{:S(2)}, u32[]{:S(2)}) collective-permute-start(bf16[64,1152]{1,0:T(8,128)(2,1)S(1)} %shard_map.156.refs_0_), channel_id=1, source_target_pairs={{0,16},{8,24},{16,0},{24,8},{1,17},{9,25},{17,1},{25,9},{2,18},{10... | collective-permute-start | bytes 442376 | tf_op jit(solution)/shard_map/ppermute | solution.py:711
  144.4 10.3 %collective-permute-start.18 = (bf16[64,1152]{1,0:T(8,128)(2,1)S(1)}, bf16[64,1152]{1,0:T(8,128)(2,1)S(1)}, u32[]{:S(2)}, u32[]{:S(2)}) collective-permute-start(bf16[64,1152]{1,0:T(8,128)(2,1)S(1)} %shard_map.156.refs_0_), channel_id=1, source_target_pairs={{0,24},{8,16},{16,8},{24,0},{1,25},{9,17},{17,9},{25,1},{2,26},{10... | collective-permute-start | bytes 442376 | tf_op jit(solution)/shard_map/ppermute | solution.py:711
  145.8 8.9 %collective-permute-start.24 = (bf16[64,640]{1,0:T(8,128)(2,1)S(1)}, bf16[64,640]{1,0:T(8,128)(2,1)S(1)}, u32[]{:S(2)}, u32[]{:S(2)}) collective-permute-start(bf16[64,640]{1,0:T(8,128)(2,1)S(1)} %shard_map.158.refs_4_), channel_id=1, source_target_pairs={{0,16},{8,24},{16,0},{24,8},{1,17},{9,25},{17,1},{25,9},{2,18},{10... | collective-permute-start | bytes 245768 | tf_op jit(solution)/shard_map/ppermute | solution.py:711
  147.3 7.4 %collective-permute-start.25 = (bf16[64,640]{1,0:T(8,128)(2,1)S(1)}, bf16[64,640]{1,0:T(8,128)(2,1)S(1)}, u32[]{:S(2)}, u32[]{:S(2)}) collective-permute-start(bf16[64,640]{1,0:T(8,128)(2,1)S(1)} %shard_map.158.refs_4_), channel_id=1, source_target_pairs={{0,24},{8,16},{16,8},{24,0},{1,25},{9,17},{17,9},{25,1},{2,26},{10... | collective-permute-start | bytes 245768 | tf_op jit(solution)/shard_map/ppermute | solution.py:711
  (9 other events, 11.0 us)
